TPU v7x, 32 devices: a whole 2x2x4 slice. The times are simulated.
32 devices in a mesh: dp: 8 (over z, y), tensor: 4 (over x, core).
Axes of the slice: x: 2, y: 2, z: 4, core: 2. Of those that a mesh axis runs over, the one named last changes fastest.
Arguments:
- tokens: bfloat16 [16, 2048, 768], P('dp', 'tensor'), may hold values from -6 to 6
- segment_ids: int32 [16, 2048], P('dp'), may hold values from 0 to 11, never falling along the last dimension, each value on 1 to 1024 neighbouring positions
- w_query: bfloat16 [768, 768], P('dp', 'tensor'), may hold values from -0.21875 to 0.21875
- w_key: bfloat16 [768, 768], P('dp', 'tensor'), may hold values from -0.21875 to 0.21875
- w_value: bfloat16 [768, 768], P('dp', 'tensor'), may hold values from -0.21875 to 0.21875
- w_out: bfloat16 [768, 768], P('tensor', 'dp'), may hold values from -1.25 to 1.25
- b_query: bfloat16 [12, 64], P('tensor', 'dp'), may hold values from -3 to 3
- b_value: bfloat16 [12, 64], P('tensor', 'dp'), may hold values from -3 to 3
- w_up: bfloat16 [768, 3072], P('dp', 'tensor'), may hold values from -0.21875 to 0.21875
- w_down: bfloat16 [3072, 768], P('tensor', 'dp'), may hold values from -0.109375 to 0.109375
- b_up: bfloat16 [48, 64], P('tensor', 'dp'), may hold values from -3 to 3
- b_out: bfloat16 [768], P(('dp', 'tensor')), may hold values from -3 to 3
- gain_one: bfloat16 [768], P(('dp', 'tensor')), may hold values from 0.25 to 1.75
- shift_one: bfloat16 [768], P(('dp', 'tensor')), may hold values from -3 to 3
- b_down: bfloat16 [768], P(('dp', 'tensor')), may hold values from -3 to 3
- gain_two: bfloat16 [768], P(('dp', 'tensor')), may hold values from 0.25 to 1.75
- shift_two: bfloat16 [768], P(('dp', 'tensor')), may hold values from -3 to 3
- cotangent: float32 [16, 2048, 768], P('dp', 'tensor'), may hold values from -6 to 6
Outputs:
- layer_out: float32 [16, 2048, 768], P('dp', 'tensor')
- grad_tokens: float32 [16, 2048, 768], P('dp', 'tensor')
- grad_w_query: float32 [768, 768], P('dp', 'tensor')
- grad_w_key: float32 [768, 768], P('dp', 'tensor')
- grad_w_value: float32 [768, 768], P('dp', 'tensor')
- grad_w_out: float32 [768, 768], P('tensor', 'dp')
- grad_b_query: float32 [12, 64], P('tensor', 'dp')
- grad_b_value: float32 [12, 64], P('tensor', 'dp')
- grad_w_up: float32 [768, 3072], P('dp', 'tensor')
- grad_w_down: float32 [3072, 768], P('tensor', 'dp')
- grad_b_up: float32 [48, 64], P('tensor', 'dp')
- grad_b_out: float32 [768], P(('dp', 'tensor'))
- grad_gain_one: float32 [768], P(('dp', 'tensor'))
- grad_shift_one: float32 [768], P(('dp', 'tensor'))
- grad_b_down: float32 [768], P(('dp', 'tensor'))
- grad_gain_two: float32 [768], P(('dp', 'tensor'))
- grad_shift_two: float32 [768], P(('dp', 'tensor'))
Inputs may be any that keep to these rules, and one draw needn't show every extreme that they name: `segment_ids`: in each sequence the segment numbers never fall and each of the 12 segments spans 1 to 1024 positions; some segment spans exactly 1024.
All inputs are finite; a program needn't handle non-finite values.
Results may differ from a plain program's by a relative error of at most 0.015.
Values may be sent and summed in bfloat16 or wider, within the bound.
No kernel may reach another device: no remote copies, remote signals or barrier semaphores. Data moves between devices by JAX's collectives and lax.ppermute only.
A program may use at most 192 MiB of HBM per device.

v0:
```python
import jax
import jax.numpy as jnp
from jax import lax
from jax.experimental import pallas as pl
from jax.experimental.pallas import tpu as pltpu
from jax.sharding import PartitionSpec as P

HD = 64
PAIR = 2 * HD
SEGS = 12
QB = 256
KB = 256
NEG = -1e30
EPS = 1e-12
BF = jnp.bfloat16
F32 = jnp.float32
BOTH = ("dp", "tensor")
NT = (((1,), (1,)), ((), ()))


def head_parts(block, scale=None):
    wide = block.astype(F32)
    if scale is not None:
        wide = wide * scale
    lane = lax.broadcasted_iota(jnp.int32, block.shape, 1)
    first = jnp.where(lane < HD, wide, 0.0).astype(BF)
    second = jnp.where(lane >= HD, wide, 0.0).astype(BF)
    return first, second


def attention_forward_kernel(lo_ref, hi_ref, bound_ref, q_ref, k_ref, v_ref, o_ref, lse_ref, vt_ref, acc_ref):
    row = pl.program_id(1)

    @pl.when(row == 0)
    def _():
        vt_ref[...] = v_ref[...].T

    parts = head_parts(q_ref[...], HD ** (-0.5))
    start = bound_ref[0, 0:1, :]
    end = bound_ref[0, 1:2, :]
    acc_ref[...] = jnp.zeros_like(acc_ref)

    def step(kb, carry):
        base = pl.multiple_of(kb * KB, KB)
        keys = k_ref[pl.ds(base, KB), :]
        place = base + lax.broadcasted_iota(jnp.int32, (KB, QB), 0)
        valid = (place >= start) & (place < end)
        after = []
        for h in range(2):
            top, total = carry[2 * h], carry[2 * h + 1]
            scores = lax.dot_general(keys, parts[h], NT, preferred_element_type=F32)
            scores = jnp.where(valid, scores, NEG)
            new_top = jnp.maximum(top, jnp.max(scores, axis=0, keepdims=True))
            fade = jnp.exp(top - new_top)
            raised = jnp.exp(scores - new_top)
            total = fade * total + jnp.sum(raised, axis=0, keepdims=True)
            rows = slice(h * HD, (h + 1) * HD)
            acc_ref[rows, :] = fade * acc_ref[rows, :] + jnp.dot(
                vt_ref[rows, pl.ds(base, KB)], raised.astype(BF), preferred_element_type=F32
            )
            after += [new_top, total]
        return tuple(after)

    low = jnp.full((1, QB), NEG, F32)
    none = jnp.zeros((1, QB), F32)
    top0, total0, top1, total1 = lax.fori_loop(lo_ref[row], hi_ref[row], step, (low, none, low, none))
    acc_ref[0:HD, :] = acc_ref[0:HD, :] / total0
    acc_ref[HD:PAIR, :] = acc_ref[HD:PAIR, :] / total1
    o_ref[...] = acc_ref[...].T.astype(BF)
    lse_ref[0, 0, 0:1, :] = top0 + jnp.log(total0)
    lse_ref[0, 0, 1:2, :] = top1 + jnp.log(total1)


def attention_backward_kernel(
    lo_ref, hi_ref, bound_ref, lse_ref, q_ref, k_ref, v_ref, do_ref, o_ref, out_ref, kt_ref, dq_ref, dk_ref, dv_ref
):
    row = pl.program_id(1)

    @pl.when(row == 0)
    def _():
        kt_ref[...] = k_ref[...].T
        dk_ref[...] = jnp.zeros_like(dk_ref)
        dv_ref[...] = jnp.zeros_like(dv_ref)

    q_parts = head_parts(q_ref[...], HD ** (-0.5))
    grad = do_ref[...]
    g_parts = head_parts(grad)
    start = bound_ref[0, 0:1, :]
    end = bound_ref[0, 1:2, :]
    product = grad.astype(F32) * o_ref[...].astype(F32)
    picker_row = lax.broadcasted_iota(jnp.int32, (8, PAIR), 0)
    picker_lane = lax.broadcasted_iota(jnp.int32, (8, PAIR), 1)
    picker = jnp.where(picker_lane // HD == picker_row, 1.0, 0.0).astype(F32)
    inner = lax.dot_general(picker, product, NT, precision=lax.Precision.HIGHEST, preferred_element_type=F32)
    dq_ref[...] = jnp.zeros_like(dq_ref)

    def step(kb, carry):
        base = pl.multiple_of(kb * KB, KB)
        keys = k_ref[pl.ds(base, KB), :]
        vals = v_ref[pl.ds(base, KB), :]
        place = base + lax.broadcasted_iota(jnp.int32, (KB, QB), 0)
        valid = (place >= start) & (place < end)
        dk = dk_ref[pl.ds(base, KB), :]
        dv = dv_ref[pl.ds(base, KB), :]
        for h in range(2):
            scores = lax.dot_general(keys, q_parts[h], NT, preferred_element_type=F32)
            scores = jnp.where(valid, scores, NEG)
            weights = jnp.exp(scores - lse_ref[0, 0, h : h + 1, :])
            grad_weights = lax.dot_general(vals, g_parts[h], NT, preferred_element_type=F32)
            grad_scores = (weights * (grad_weights - inner[h : h + 1, :])).astype(BF)
            dv = dv + jnp.dot(weights.astype(BF), g_parts[h], preferred_element_type=F32)
            dk = dk + jnp.dot(grad_scores, q_parts[h], preferred_element_type=F32)
            rows = slice(h * HD, (h + 1) * HD)
            dq_ref[rows, :] += jnp.dot(kt_ref[rows, pl.ds(base, KB)], grad_scores, preferred_element_type=F32)
        dk_ref[pl.ds(base, KB), :] = dk
        dv_ref[pl.ds(base, KB), :] = dv
        return carry

    lax.fori_loop(lo_ref[row], hi_ref[row], step, 0)
    out_ref[pl.ds(pl.multiple_of(row * QB, QB), QB), 0:PAIR] = (dq_ref[...] * HD ** (-0.5)).T.astype(BF)

    @pl.when(row == pl.num_programs(1) - 1)
    def _():
        out_ref[:, PAIR : 2 * PAIR] = dk_ref[...].astype(BF)
        out_ref[:, 2 * PAIR : 3 * PAIR] = dv_ref[...].astype(BF)


def attention_forward(qkv, lo, hi, bounds):
    length = qkv.shape[0]
    pairs = qkv.shape[1] // (3 * PAIR)
    blocks = length // QB
    return pl.pallas_call(
        attention_forward_kernel,
        name="attention_forward",
        out_shape=(
            jax.ShapeDtypeStruct((length, pairs * PAIR), BF),
            jax.ShapeDtypeStruct((pairs, blocks, 2, QB), F32),
        ),
        grid_spec=pltpu.PrefetchScalarGridSpec(
            num_scalar_prefetch=2,
            grid=(pairs, blocks),
            in_specs=[
                pl.BlockSpec((1, 2, QB), lambda j, i, lo, hi: (i, 0, 0)),
                pl.BlockSpec((QB, PAIR), lambda j, i, lo, hi: (i, 3 * j)),
                pl.BlockSpec((length, PAIR), lambda j, i, lo, hi: (0, 3 * j + 1)),
                pl.BlockSpec((length, PAIR), lambda j, i, lo, hi: (0, 3 * j + 2)),
            ],
            out_specs=(
                pl.BlockSpec((QB, PAIR), lambda j, i, lo, hi: (i, j)),
                pl.BlockSpec((1, 1, 2, QB), lambda j, i, lo, hi: (j, i, 0, 0)),
            ),
            scratch_shapes=[pltpu.VMEM((PAIR, length), BF), pltpu.VMEM((PAIR, QB), F32)],
        ),
        cost_estimate=pl.CostEstimate(
            flops=pairs * length * length * PAIR * 4,
            transcendentals=pairs * length * length,
            bytes_accessed=qkv.size * 2 + length * pairs * PAIR * 2,
        ),
        compiler_params=pltpu.CompilerParams(dimension_semantics=("arbitrary", "arbitrary")),
    )(lo, hi, bounds, qkv, qkv, qkv)


def attention_backward(qkv, grad, out, lse, lo, hi, bounds):
    length = qkv.shape[0]
    pairs = qkv.shape[1] // (3 * PAIR)
    blocks = length // QB
    return pl.pallas_call(
        attention_backward_kernel,
        name="attention_backward",
        out_shape=jax.ShapeDtypeStruct(qkv.shape, BF),
        grid_spec=pltpu.PrefetchScalarGridSpec(
            num_scalar_prefetch=2,
            grid=(pairs, blocks),
            in_specs=[
                pl.BlockSpec((1, 2, QB), lambda j, i, lo, hi: (i, 0, 0)),
                pl.BlockSpec((1, 1, 2, QB), lambda j, i, lo, hi: (j, i, 0, 0)),
                pl.BlockSpec((QB, PAIR), lambda j, i, lo, hi: (i, 3 * j)),
                pl.BlockSpec((length, PAIR), lambda j, i, lo, hi: (0, 3 * j + 1)),
                pl.BlockSpec((length, PAIR), lambda j, i, lo, hi: (0, 3 * j + 2)),
                pl.BlockSpec((QB, PAIR), lambda j, i, lo, hi: (i, j)),
                pl.BlockSpec((QB, PAIR), lambda j, i, lo, hi: (i, j)),
            ],
            out_specs=pl.BlockSpec((length, 3 * PAIR), lambda j, i, lo, hi: (0, j)),
            scratch_shapes=[
                pltpu.VMEM((PAIR, length), BF),
                pltpu.VMEM((PAIR, QB), F32),
                pltpu.VMEM((length, PAIR), F32),
                pltpu.VMEM((length, PAIR), F32),
            ],
        ),
        cost_estimate=pl.CostEstimate(
            flops=pairs * length * length * PAIR * 10,
            transcendentals=pairs * length * length,
            bytes_accessed=qkv.size * 4 + length * pairs * PAIR * 4,
        ),
        compiler_params=pltpu.CompilerParams(dimension_semantics=("arbitrary", "arbitrary")),
    )(lo, hi, bounds, lse, qkv, qkv, qkv, grad, out)


def segment_bounds(segments):
    length = segments.shape[0]
    names = jnp.arange(SEGS, dtype=jnp.int32)[:, None]
    counts = jnp.sum((segments[None, :] == names).astype(jnp.int32), axis=1, keepdims=True)
    start = jnp.sum(jnp.where(segments[None, :] > names, counts, 0), axis=0)
    end = jnp.sum(jnp.where(segments[None, :] >= names, counts, 0), axis=0)
    start = start.reshape(length // QB, QB)
    end = end.reshape(length // QB, QB)
    lo = start[:, 0] // KB
    hi = (end[:, -1] + (KB - 1)) // KB
    return lo, hi, jnp.stack([start, end], axis=1)


def statistics(rows):
    centred = rows - jnp.mean(rows, axis=-1, keepdims=True)
    inverse = lax.rsqrt(jnp.mean(centred * centred, axis=-1, keepdims=True) + EPS)
    return centred * inverse, inverse


def norm_backward(grad, hat, inverse, gain):
    scaled = grad * gain
    return inverse * (
        scaled
        - jnp.mean(scaled, axis=-1, keepdims=True)
        - hat * jnp.mean(scaled * hat, axis=-1, keepdims=True)
    )


def mm(a, b):
    return lax.dot_general(a, b, (((1,), (0,)), ((), ())), preferred_element_type=F32)


def mm_nt(a, b):
    return lax.dot_general(a, b, NT, preferred_element_type=F32)


def mm_tn(a, b):
    return lax.dot_general(a, b, (((0,), (0,)), ((), ())), preferred_element_type=F32)


def piece_rows(ref):
    block = ref[:, 0]
    return block.reshape(block.shape[0] * block.shape[1], block.shape[2])


def project_kernel(spot_ref, tokens_ref, weights_ref, bias_ref, qkv_ref, w_ref):
    slots, cut, width = weights_ref.shape
    columns = width // 3
    bits = (slots // 2).bit_length() - 1

    @pl.when(pl.program_id(0) == 0)
    def _():
        for d in range(slots // 2):
            other = d ^ spot_ref[0]
            slot = 0
            for b in range(bits):
                slot = slot * 2 + ((other >> b) & 1)
            first = weights_ref[slot * 2 + spot_ref[1]].astype(F32)
            second = weights_ref[slot * 2 + 1 - spot_ref[1]].astype(F32)
            for s in range(3):
                cols = slice(s * columns, (s + 1) * columns)
                joined = jnp.concatenate([first[:, cols], second[:, cols]], axis=1).astype(BF)
                for p in range(2 * columns // PAIR):
                    at = (3 * p + s) * PAIR
                    w_ref[d * cut : (d + 1) * cut, at : at + PAIR] = joined[:, p * PAIR : (p + 1) * PAIR]

    qkv_ref[...] = (mm(tokens_ref[...], w_ref[...]) + bias_ref[...]).astype(BF)


def project(tokens, weights, bias, spot):
    length, features = tokens.shape
    width = 2 * weights.shape[2]
    return pl.pallas_call(
        project_kernel,
        name="project",
        out_shape=(
            jax.ShapeDtypeStruct((length, width), BF),
            jax.ShapeDtypeStruct((features, width), BF),
        ),
        grid_spec=pltpu.PrefetchScalarGridSpec(
            num_scalar_prefetch=1,
            grid=(length // QB,),
            in_specs=[
                pl.BlockSpec((QB, features), lambda i, spot: (i, 0)),
                pl.BlockSpec(weights.shape, lambda i, spot: (0, 0, 0)),
                pl.BlockSpec((1, width), lambda i, spot: (0, 0)),
            ],
            out_specs=(
                pl.BlockSpec((QB, width), lambda i, spot: (i, 0)),
                pl.BlockSpec((features, width), lambda i, spot: (0, 0)),
            ),
        ),
        cost_estimate=pl.CostEstimate(
            flops=2 * length * features * width, transcendentals=0, bytes_accessed=2 * length * (features + width)
        ),
        compiler_params=pltpu.CompilerParams(dimension_semantics=("arbitrary",)),
    )(spot, tokens, weights, bias)


def feed_forward_kernel(x_ref, up_ref, down_ref, bias_ref, act_ref, slope_ref, sum_ref):
    @pl.when(pl.program_id(0) == 0)
    def _():
        sum_ref[...] = jnp.zeros_like(sum_ref)

    up = piece_rows(up_ref)
    down = piece_rows(down_ref)
    for r in range(x_ref.shape[0] // QB):
        rows = slice(r * QB, (r + 1) * QB)
        hidden = mm(x_ref[rows, :], up) + bias_ref[0]
        area = 0.5 * (1.0 + lax.erf(hidden * (2.0**-0.5)))
        activated = (hidden * area).astype(BF)
        act_ref[rows, :] = activated
        slope_ref[rows, :] = (area + hidden * jnp.exp(-0.5 * hidden * hidden) * ((2.0 * jnp.pi) ** -0.5)).astype(BF)
        sum_ref[rows, :] += mm_nt(activated, down)


def feed_forward(x, weights, bias):
    length, features = x.shape
    dp, parts, cut, _ = weights.shape
    units = bias.shape[-1]
    piece = (dp, 1, cut, units)
    return pl.pallas_call(
        feed_forward_kernel,
        name="feed_forward",
        out_shape=(
            jax.ShapeDtypeStruct((length, parts * units), BF),
            jax.ShapeDtypeStruct((length, parts * units), BF),
            jax.ShapeDtypeStruct((length, features), F32),
        ),
        grid=(parts,),
        in_specs=[
            pl.BlockSpec((length, features), lambda t: (0, 0)),
            pl.BlockSpec(piece, lambda t: (0, t, 0, 0)),
            pl.BlockSpec(piece, lambda t: (0, t, 0, 1)),
            pl.BlockSpec((1, 1, units), lambda t: (t, 0, 0)),
        ],
        out_specs=(
            pl.BlockSpec((length, units), lambda t: (0, t)),
            pl.BlockSpec((length, units), lambda t: (0, t)),
            pl.BlockSpec((length, features), lambda t: (0, 0)),
        ),
        cost_estimate=pl.CostEstimate(
            flops=4 * length * features * parts * units,
            transcendentals=2 * length * parts * units,
            bytes_accessed=length * (parts * units * 4 + features * 6),
        ),
        compiler_params=pltpu.CompilerParams(dimension_semantics=("arbitrary",)),
    )(x, weights, weights, bias)


def feed_forward_backward_kernel(
    grad_ref, x_ref, act_ref, slope_ref, up_ref, down_ref, pack_ref, back_ref, bias_ref, xt_ref, gt_ref, gh_ref
):
    @pl.when(pl.program_id(0) == 0)
    def _():
        back_ref[...] = jnp.zeros_like(back_ref)
        xt_ref[...] = x_ref[...].T
        gt_ref[...] = grad_ref[...].T

    up = piece_rows(up_ref)
    down = piece_rows(down_ref)
    total = jnp.zeros((1, act_ref.shape[1]), F32)
    for r in range(x_ref.shape[0] // QB):
        rows = slice(r * QB, (r + 1) * QB)
        grad_hidden = (mm(grad_ref[rows, :], down) * slope_ref[rows, :].astype(F32)).astype(BF)
        gh_ref[rows, :] = grad_hidden
        total = total + jnp.sum(grad_hidden.astype(F32), axis=0, keepdims=True)
        back_ref[rows, :] += mm_nt(grad_hidden, up)
    bias_ref[0] = total
    units = act_ref.shape[1]
    split = (pack_ref.shape[0], pack_ref.shape[2], units)
    pack_ref[:, 0, :, 0:units] = mm(xt_ref[...], gh_ref[...]).astype(BF).reshape(split)
    pack_ref[:, 0, :, units : 2 * units] = mm(gt_ref[...], act_ref[...]).astype(BF).reshape(split)


def feed_forward_backward(grad, x, act, slope, weights):
    length, features = x.shape
    dp, parts, cut, width = weights.shape
    units = act.shape[1] // parts
    piece = (dp, 1, cut, units)
    whole = pl.BlockSpec((length, features), lambda t: (0, 0))
    part = pl.BlockSpec((length, units), lambda t: (0, t))
    return pl.pallas_call(
        feed_forward_backward_kernel,
        name="feed_forward_backward",
        out_shape=(
            jax.ShapeDtypeStruct((dp, parts, cut, width), BF),
            jax.ShapeDtypeStruct((length, features), F32),
            jax.ShapeDtypeStruct((parts, 1, units), F32),
        ),
        grid=(parts,),
        in_specs=[
            whole,
            whole,
            part,
            part,
            pl.BlockSpec(piece, lambda t: (0, t, 0, 0)),
            pl.BlockSpec(piece, lambda t: (0, t, 0, 1)),
        ],
        out_specs=(
            pl.BlockSpec((dp, 1, cut, 2 * units), lambda t: (0, t, 0, 0)),
            whole,
            pl.BlockSpec((1, 1, units), lambda t: (t, 0, 0)),
        ),
        scratch_shapes=[
            pltpu.VMEM((features, length), BF),
            pltpu.VMEM((features, length), BF),
            pltpu.VMEM((length, units), BF),
        ],
        cost_estimate=pl.CostEstimate(
            flops=8 * length * features * parts * units,
            transcendentals=0,
            bytes_accessed=length * (parts * units * 4 + features * 8) + dp * parts * cut * width * 4,
        ),
        compiler_params=pltpu.CompilerParams(dimension_semantics=("arbitrary",)),
    )(grad, x, act, slope, weights, weights)


def output_gradient_kernel(grad_ref, context_ref, _, pack_ref, full_ref):
    part = pl.program_id(0)
    columns = context_ref.shape[1] // 4

    @pl.when(part == 0)
    def _():
        full_ref[...] = mm(grad_ref[...].T, context_ref[...])

    split = (pack_ref.shape[0], pack_ref.shape[2], pack_ref.shape[3])
    for t in range(4):

        @pl.when(part == t)
        def _():
            at = (t % 2 * 2 + t // 2) * columns
            piece = full_ref[:, at : at + columns]
            rest = jnp.zeros((piece.shape[0], split[2] - columns), F32)
            pack_ref[:, 0] = jnp.concatenate([piece, rest], axis=1).astype(BF).reshape(split)


def output_gradient(grad, context, pack):
    length, features = grad.shape
    dp, parts, cut, width = pack.shape
    whole = pl.BlockSpec((length, features), lambda t: (0, 0))
    return pl.pallas_call(
        output_gradient_kernel,
        name="output_gradient",
        out_shape=jax.ShapeDtypeStruct(pack.shape, BF),
        grid=(parts,),
        in_specs=[whole, whole, pl.BlockSpec(memory_space=pl.ANY)],
        out_specs=pl.BlockSpec((dp, 1, cut, PAIR * 2), lambda t: (0, t, 0, width // (PAIR * 2) - 1)),
        scratch_shapes=[pltpu.VMEM((features, features), F32)],
        input_output_aliases={2: 0},
        cost_estimate=pl.CostEstimate(
            flops=2 * length * features * features, transcendentals=0, bytes_accessed=length * features * 4
        ),
        compiler_params=pltpu.CompilerParams(dimension_semantics=("arbitrary",)),
    )(grad, context, pack)


def make_per_device(dp):
    bits = dp.bit_length() - 1
    assert dp == 1 << bits

    def per_device(
        tokens,
        segment_ids,
        w_query,
        w_key,
        w_value,
        w_out,
        b_query,
        b_value,
        w_up,
        w_down,
        b_up,
        b_out,
        gain_one,
        shift_one,
        b_down,
        gain_two,
        shift_two,
        cotangent,
    ):
        place = lax.axis_index("tensor")
        depth = lax.axis_index("dp")
        across = place // 2
        core = place % 2
        _, quarter, features = tokens.shape
        cut, columns = w_query.shape
        units = w_up.shape[1]
        half = 2 * columns
        pairs = half // PAIR
        first_core = core == 0
        first_chip = across == 0
        tiled = cut % 16 == 0
        groups = (dp, cut) if tiled else (1, dp * cut)

        def swap_chips(value):
            return lax.ppermute(value, "tensor", [(0, 2), (2, 0), (1, 3), (3, 1)])

        def swap_cores(value):
            return lax.ppermute(value, "tensor", [(0, 1), (1, 0), (2, 3), (3, 2)])

        def swap_bit(value, b):
            return lax.ppermute(value, "dp", [(i, i ^ (1 << b)) for i in range(dp)])

        def bit_of(b):
            return (depth >> b) & 1

        def in_order(flag, mine, other, axis):
            return jnp.stack([jnp.where(flag, mine, other), jnp.where(flag, other, mine)], axis=axis)

        def mine_of(value, index, axis):
            return lax.dynamic_index_in_dim(value, index, axis, keepdims=False)

        attention_pack = jnp.concatenate([w_query, w_key, w_value], axis=1)
        if tiled:
            gathered = jnp.stack([attention_pack, swap_chips(attention_pack)])
            for b in reversed(range(bits)):
                gathered = jnp.concatenate([gathered, swap_bit(gathered, b)])
            spot = jnp.stack([depth, across]).astype(jnp.int32)
        else:
            gathered = lax.all_gather(attention_pack, BOTH, axis=0).reshape(dp, 2, 2, cut, 3 * columns)
            gathered = mine_of(gathered, core, 2).transpose(1, 0, 2, 3).reshape(2, dp * cut, 3 * columns)
            spot = jnp.zeros((2,), jnp.int32)

        tokens_own = in_order(first_chip, mine_of(tokens, across, 0), swap_chips(mine_of(tokens, 1 - across, 0)), 0)
        tokens_full = in_order(first_core, tokens_own, swap_cores(tokens_own), 1).reshape(4 * quarter, features)
        tokens_own = tokens_own.reshape(2 * quarter, features)

        small = [b_query, b_value, b_up, b_out, gain_one, shift_one, b_down, gain_two, shift_two]
        sizes = [v.size for v in small]
        lanes = -(-sum(sizes) // PAIR) * PAIR
        packed = jnp.concatenate([v.reshape(-1) for v in small])
        small_all = jnp.pad(packed, (0, lanes - packed.size)).reshape(1, lanes)
        small_all = in_order(first_chip, small_all, swap_chips(small_all), 0)
        for b in range(bits):
            small_all = in_order(bit_of(b) == 0, small_all, swap_bit(small_all, b), 0)
            small_all = small_all.reshape(2 << b, 2, 1, lanes)
        core_bias = small_all[:, :, 0, : sizes[0] + sizes[1]].reshape(dp, 2, 2, *b_query.shape).astype(F32)
        core_bias = core_bias.transpose(2, 1, 3, 0, 4).reshape(2, pairs, PAIR)
        bias_mine = jnp.stack([core_bias[0], jnp.zeros((pairs, PAIR), F32), core_bias[1]], axis=1).reshape(1, 3 * half)
        small_all = in_order(first_core, small_all, swap_cores(small_all), 2).reshape(dp, 4, lanes)
        pieces = []
        offset = 0
        for v, size in zip(small, sizes):
            piece = small_all[:, :, offset : offset + size].astype(F32)
            offset += size
            if v.ndim == 2:
                pieces.append(piece.reshape(dp, 4, *v.shape).transpose(1, 2, 0, 3))
            else:
                pieces.append(piece.reshape(-1))
        _, _, bias_up, out_bias, gain1, shift1, down_bias, gain2, shift2 = pieces
        bias_up = bias_up.reshape(4, 1, units)

        spare = jnp.zeros((cut, 2 * PAIR - columns), BF)
        other_pack = jnp.concatenate([w_up, w_down.T, w_out.T, spare], axis=1)
        width = other_pack.shape[1]
        others = lax.all_gather(other_pack, BOTH, axis=0).reshape(dp, 4, cut, width)
        if not tiled:
            others = others.transpose(1, 0, 2, 3).reshape(1, 4, dp * cut, width)

        cotangent_own = in_order(
            first_chip,
            mine_of(cotangent, across, 0),
            swap_chips(mine_of(cotangent, 1 - across, 0).astype(BF)).astype(F32),
            0,
        ).reshape(2 * quarter, features)
        lo, hi, bounds = segment_bounds(mine_of(segment_ids, across, 0))

        qkv, w_qkv = project(tokens_full, gathered, bias_mine, spot)
        heads_out, lse = attention_forward(qkv, lo, hi, bounds)

        by_core = heads_out.reshape(2, 2, quarter, half)
        kept = mine_of(by_core, core, 1)
        got = swap_cores(mine_of(by_core, 1 - core, 1))
        context = in_order(first_core, kept, got, 2).reshape(2 * quarter, 2 * half)

        w_out_t = (
            others[..., 2 * units : 2 * units + columns]
            .reshape(groups[0], 2, 2, groups[1], columns)
            .transpose(0, 3, 2, 1, 4)
            .reshape(features, features)
        )
        summed = tokens_own.astype(F32) + mm_nt(context, w_out_t) + out_bias
        hat1, inverse1 = statistics(summed)
        normed = hat1 * gain1 + shift1
        normed_low = normed.astype(BF)
        activated, slope, branch = feed_forward(normed_low, others, bias_up)
        hat2, inverse2 = statistics(normed + branch + down_bias)
        out_own = (hat2 * gain2 + shift2).reshape(2, quarter, features)

        def send_back(value):
            kept_part = mine_of(value, across, 0)
            got_part = swap_chips(mine_of(value, 1 - across, 0).astype(BF)).astype(F32)
            return in_order(first_chip, kept_part, got_part, 0)

        layer_out = send_back(out_own)

        grad_z = norm_backward(cotangent_own, hat2, inverse2, gain2)
        grad_branch = grad_z.astype(BF)
        pack, back, grad_bias_up = feed_forward_backward(grad_branch, normed_low, activated, slope, others)
        grad_normed = grad_z + back
        grad_summed = norm_backward(grad_normed, hat1, inverse1, gain1)
        grad_attended = grad_summed.astype(BF)
        pack = output_gradient(grad_attended, context, pack)
        if not tiled:
            pack = pack.reshape(4, dp, cut, width).transpose(1, 0, 2, 3)
        others_mine = lax.psum_scatter(pack.reshape(4 * dp, cut, width), BOTH, scatter_dimension=0, tiled=False)

        grad_context = mm(grad_attended, w_out_t).astype(BF).reshape(2, quarter, 2, half)
        kept = mine_of(grad_context, core, 2)
        got = swap_cores(mine_of(grad_context, 1 - core, 2))
        grad_heads = in_order(first_core, kept, got, 1).reshape(4 * quarter, half)

        grad_qkv = attention_backward(qkv, grad_heads, heads_out, lse, lo, hi, bounds)
        part = mm_nt(grad_qkv, w_qkv).reshape(2, 2, quarter, features)
        part_kept = mine_of(part, core, 1)
        part_got = swap_cores(mine_of(part, 1 - core, 1).astype(BF))
        grad_tokens = send_back(grad_summed.reshape(2, quarter, features) + part_kept + part_got.astype(F32))

        def halve(value, flag, swap, axis, kind):
            kept_half = mine_of(value, flag, axis)
            sent_half = mine_of(value, 1 - flag, axis)
            return (kept_half.astype(F32) + swap(sent_half).astype(F32)).astype(kind)

        grad_w = mm_tn(tokens_full, grad_qkv).astype(BF).reshape(dp, cut, 3 * half)
        for b in range(bits):
            grad_w = halve(grad_w.reshape(-1, 2, cut, 3 * half), bit_of(b), lambda v: swap_bit(v, b), 1, BF)
        grad_w = (
            grad_w.reshape(cut, pairs, 3, PAIR).transpose(0, 2, 1, 3).reshape(cut, 3, 2, columns).transpose(2, 0, 1, 3)
        )
        grad_w = halve(grad_w.reshape(2, cut, 3 * columns), across, swap_chips, 0, F32)

        bias_grads = jnp.sum(grad_qkv.astype(F32), axis=0).reshape(pairs, 3, PAIR)

        def matrix_small(value, like):
            return value.reshape(2, 2, like.shape[0], dp, like.shape[1]).transpose(3, 0, 1, 2, 4).reshape(dp, 2, 2, -1)

        def head_small(value, like):
            value = value.reshape(2, columns)
            zero = jnp.zeros_like(value)
            both = [jnp.where(first_core, value, zero), jnp.where(first_core, zero, value)]
            return matrix_small(jnp.stack(both, axis=1), like)

        def vector_small(value):
            return value.reshape(dp, 2, 2, -1)

        small_grads = jnp.concatenate(
            [
                head_small(bias_grads[:, 0], b_query),
                head_small(bias_grads[:, 2], b_value),
                matrix_small(grad_bias_up, b_up),
                vector_small(jnp.sum(grad_summed, axis=0)),
                vector_small(jnp.sum(grad_normed * hat1, axis=0)),
                vector_small(jnp.sum(grad_normed, axis=0)),
                vector_small(jnp.sum(grad_z, axis=0)),
                vector_small(jnp.sum(cotangent_own * hat2, axis=0)),
                vector_small(jnp.sum(cotangent_own, axis=0)),
            ],
            axis=3,
        )
        small_grads = jnp.pad(small_grads, ((0, 0), (0, 0), (0, 0), (0, lanes - small_grads.shape[3])))
        small_grads = halve(small_grads, core, swap_cores, 2, F32)
        for b in range(bits):
            small_grads = halve(small_grads.reshape(-1, 2, 2, lanes), bit_of(b), lambda v: swap_bit(v, b), 1, F32)
        small_grads = halve(small_grads.reshape(2, lanes), across, swap_chips, 0, F32)

        others_mine = others_mine.astype(F32)
        small_out = []
        offset = 0
        for v, size in zip(small, sizes):
            small_out.append(small_grads[offset : offset + size].reshape(v.shape))
            offset += size
        return (
            layer_out,
            grad_tokens,
            grad_w[:, :columns],
            grad_w[:, columns : 2 * columns],
            grad_w[:, 2 * columns :],
            others_mine[:, 2 * units : 2 * units + columns].T,
            small_out[0],
            small_out[1],
            others_mine[:, :units],
            others_mine[:, units : 2 * units].T,
            small_out[2],
            small_out[3],
            small_out[4],
            small_out[5],
            small_out[6],
            small_out[7],
            small_out[8],
        )

    return per_device


def solution(mesh):
    rows = P("dp", "tensor", None)
    split = P("dp", "tensor")
    turned = P("tensor", "dp")
    vector = P(("dp", "tensor"))
    in_specs = (rows, P("dp", None), split, split, split, turned, turned, turned, split, turned, turned)
    in_specs += (vector,) * 6 + (rows,)
    out_specs = (rows, rows, split, split, split, turned, turned, turned, split, turned, turned)
    out_specs += (vector,) * 6
    return jax.shard_map(
        make_per_device(mesh.shape["dp"]), mesh=mesh, in_specs=in_specs, out_specs=out_specs, check_vma=False
    )
```

profile of v0, /device:TPU:0, one launch (start us, length us, event | category | flops | bytes accessed | tf_op | source)
XLA Modules:
  0.0 529.2 jit_solution(8524637807842670835)
XLA Ops:
  8.2 1.8 concatenate.31
  11.2 3.0 collective-permute-start
  16.7 4.1 concatenate.30
  22.5 2.0 collective-permute-start.2
  24.5 2.4 fusion.16
  27.9 7.2 %collective-permute-done.6 = bf16[1,384]{1,0:T(2,128)(2,1)S(1)} collective-permute-done((bf16[1,384]{1,0:T(2,128)(2,1)S(1)}, bf16[1,384]{1,0:T(2,128)(2,1)S(1)}, u32[]{:S(2)}, u32[]{:S(2)}) %collective-permute-start.6) | collective-permute-done | bytes 800 | tf_op jit(solution)/shard_map/ppermute | solution.py:496
  35.2 2.1 collective-permute-start.7
  38.9 2.1 collective-permute-start.8
  42.6 3.1 collective-permute-start.9
  47.9 2.9 collective-permute-start.3
  50.9 15.8 %collective-permute-done.3 = bf16[2,96,576]{2,1,0:T(8,128)(2,1)S(1)} collective-permute-done((bf16[2,96,576]{2,1,0:T(8,128)(2,1)S(1)}, bf16[2,96,576]{2,1,0:T(8,128)(2,1)S(1)}, u32[]{:S(2)}, u32[]{:S(2)}) %collective-permute-start.3) | collective-permute-done | bytes 221216 | tf_op jit(solution)/shard_map/ppermute | solution.py:502
  70.9 18.8 %collective-permute-done.4 = bf16[4,96,576]{2,1,0:T(8,128)(2,1)S(1)} collective-permute-done((bf16[4,96,576]{2,1,0:T(8,128)(2,1)}, bf16[4,96,576]{2,1,0:T(8,128)(2,1)S(1)}, u32[]{:S(2)}, u32[]{:S(2)}) %collective-permute-start.4) | collective-permute-done | bytes 442400 | tf_op jit(solution)/shard_map/ppermute | solution.py:502
  89.9 1.9 collective-permute-start.5
  94.2 26.6 %collective-permute-done.5 = bf16[8,96,576]{2,1,0:T(8,128)(2,1)S(1)} collective-permute-done((bf16[8,96,576]{2,1,0:T(8,128)(2,1)S(1)}, bf16[8,96,576]{2,1,0:T(8,128)(2,1)S(1)}, u32[]{:S(2)}, u32[]{:S(2)}) %collective-permute-start.5) | collective-permute-done | bytes 884768 | tf_op jit(solution)/shard_map/ppermute | solution.py:502
  123.7 1.9 copy.165
  125.6 11.6 %project.1 = (bf16[2048,1152]{1,0:T(8,128)(2,1)}, bf16[768,1152]{1,0:T(8,128)(2,1)}) custom-call(s32[2]{0:T(128)} %pad_add_fusion.1.spot_ref, bf16[2048,768]{1,0:T(8,128)(2,1)} %bitcast.269, bf16[16,96,576]{2,1,0:T(8,128)(2,1)} %constant_dynamic-update-slice_fusion.weights_ref, f32[1,1152]{1,0:T(1,128)} %reshape.361.bias_ref), custom_call_target="tpu_custom_call" | custom-call | flops 3623878656 | bytes 7864320 | tf_op jit(solution)/shard_map/project/pallas_call | solution.py:272
  137.2 81.2 %attention_forward.1 = (bf16[2048,384]{1,0:T(8,128)(2,1)}, f32[3,8,2,256]{3,2,1,0:T(2,128)}) custom-call(s32[8]{0:T(128)} %and_select_fusion.1.lo_ref, s32[8]{0:T(128)} %and_select_fusion.hi_ref, s32[8,2,256]{2,1,0:T(2,128)} %pad_add_fusion.bound_ref, bf16[2048,1152]{1,0:T(8,128)(2,1)} %get-tuple-element.27.q_ref.k_ref.v_ref, ...), custom_call_target="tpu_custom_call" | custom-call | flops 6442450944 | bytes 6291456 | tf_op jit(solution)/shard_map/attention_forward/pallas_call | solution.py:132
  218.4 2.1 dynamic-slice_bitcast_fusion.1
  225.2 2.0 multiply_reduce_fusion.3
  234.4 2.2 reshape.366
  236.6 3.8 fusion.40
  240.9 1.7 fusion.3.x_ref
  242.6 18.2 %feed_forward.1 = (bf16[1024,3072]{1,0:T(8,128)(2,1)}, bf16[1024,3072]{1,0:T(8,128)(2,1)}, f32[1024,768]{1,0:T(8,128)}) custom-call(bf16[1024,768]{1,0:T(8,128)(2,1)} %fusion.3.x_ref, bf16[8,4,96,1792]{3,2,1,0:T(8,128)(2,1)} %bitcast.292, bf16[8,4,96,1792]{3,2,1,0:T(8,128)(2,1)} %bitcast.293, f32[4,1,768]{2,1,0:T(1,128)} %reshape.413.bias_ref), custom_call_target="tpu_custom_call" | custom-call | flops 9663676416 | bytes 17301504 | tf_op jit(solution)/shard_map/feed_forward/pallas_call | solution.py:321
  260.7 2.9 fusion.39
  266.6 2.7 fusion.37
  272.3 28.4 %feed_forward_backward.1 = (bf16[8,4,96,1792]{3,2,1,0:T(8,128)(2,1)}, f32[1024,768]{1,0:T(8,128)}, f32[4,1,768]{2,1,0:T(1,128)}) custom-call(bf16[1024,768]{1,0:T(8,128)(2,1)} %convert_element_type.139.grad_ref, bf16[1024,768]{1,0:T(8,128)(2,1)} %fusion.3.x_ref, bf16[1024,3072]{1,0:T(8,128)(2,1)} %get-tuple-element.30.act_ref, ...), custom_call_target="tpu_custom_call" | custom-call | flops 19327352832 | bytes 40894464 | tf_op jit(solution)/shard_map/feed_forward_backward/pallas_call | solution.py:382
  300.7 3.8 multiply_reduce_fusion
  305.7 1.7 copy-done.2
  308.7 5.3 output_gradient.1
  315.4 2.7 convolution_convert_fusion.1
  318.7 4.4 constant_dynamic-slice_fusion.10
  329.7 2.0 select_bitcast_fusion.3
  333.2 79.4 %attention_backward.1 = bf16[2048,1152]{1,0:T(8,128)(2,1)} custom-call(s32[8]{0:T(128)} %and_select_fusion.1.lo_ref, s32[8]{0:T(128)} %and_select_fusion.hi_ref, s32[8,2,256]{2,1,0:T(2,128)} %pad_add_fusion.bound_ref, f32[3,8,2,256]{3,2,1,0:T(2,128)} %get-tuple-element.33.lse_ref, bf16[2048,1152]{1,0:T(8,128)(2,1)} %get-tuple-element.27.q_ref.k_ref.v_ref, ...), custom_call_target="tpu_custom_call" | custom-call | flops 16106127360 | bytes 12582912 | tf_op jit(solution)/shard_map/attention_backward/pallas_call | solution.py:167
  412.6 3.0 convert_reduce_fusion
  416.5 7.7 %convolution_convert_fusion = bf16[768,1152]{1,0:T(8,128)(2,1)S(1)} fusion(bf16[2048,768]{1,0:T(8,128)(2,1)} %bitcast.270, bf16[2048,1152]{1,0:T(8,128)(2,1)} %attention_backward.1), kind=kOutput, calls=%fused_computation.1 | convolution fusion | flops 3624763392 | bytes 9633792 | tf_op jit(solution)/shard_map/dot_general | solution.py:237
  427.1 6.4 %fusion.46 = f32[2048,768]{1,0:T(8,128)} fusion(bf16[2048,1152]{1,0:T(8,128)(2,1)S(1)} %bitcast.264, bf16[768,1152]{1,0:T(8,128)(2,1)S(1)} %copy-done.14), kind=kOutput, calls=%fused_computation.188 | convolution fusion | flops 3623878656 | bytes 12779520 | tf_op jit(solution)/shard_map/dot_general | solution.py:233
  435.0 3.4 fusion.9
  438.8 12.3 %collective-permute-done.22 = f32[4,2,384]{2,0,1:T(4,128)S(1)} collective-permute-done((f32[4,2,384]{2,0,1:T(4,128)S(1)}, f32[4,2,384]{2,0,1:T(4,128)S(1)}, u32[]{:S(2)}, u32[]{:S(2)}) %collective-permute-start.22) | collective-permute-done | bytes 12320 | tf_op jit(solution)/shard_map/ppermute | solution.py:502
  456.4 5.9 %collective-permute-start.24 = (f32[1,2,384]{2,0,1:T(1,128)S(1)}, f32[1,2,384]{2,0,1:T(1,128)S(1)}, u32[]{:S(2)}, u32[]{:S(2)}) collective-permute-start(f32[1,2,384]{2,0,1:T(1,128)S(1)} %constant_dynamic-slice_fusion.2), channel_id=1, source_target_pairs={{0,16},{4,20},{8,24},{12,28},{16,0},{20,4},{24,8},{28,12},{1,17},{... | collective-permute-start | bytes 9224 | tf_op jit(solution)/shard_map/ppermute | solution.py:502
  462.4 8.5 %collective-permute-done.18 = bf16[2,96,1152]{2,1,0:T(8,128)(2,1)S(1)} collective-permute-done((bf16[2,96,1152]{2,1,0:T(8,128)(2,1)S(1)}, bf16[2,96,1152]{2,1,0:T(8,128)(2,1)S(1)}, u32[]{:S(2)}, u32[]{:S(2)}) %collective-permute-start.18) | collective-permute-done | bytes 442400 | tf_op jit(solution)/shard_map/ppermute | solution.py:502
  471.0 2.2 collective-permute-start.19
  473.2 2.8 collective-permute-start.25
  476.0 1.9 pad_maximum_fusion.1
  477.9 5.9 %collective-permute-done.19 = bf16[1,96,1152]{2,1,0:T(8,128)(2,1)S(1)} collective-permute-done((bf16[1,96,1152]{2,1,0:T(8,128)(2,1)S(1)}, bf16[1,96,1152]{2,1,0:T(8,128)(2,1)S(1)}, u32[]{:S(2)}, u32[]{:S(2)}) %collective-permute-start.19) | collective-permute-done | bytes 221216 | tf_op jit(solution)/shard_map/ppermute | solution.py:502
  485.9 3.0 fusion.1
  490.6 1.9 collective-permute-start.16
  495.5 17.3 %collective-permute-done.20 = bf16[96,576]{0,1:T(8,128)(2,1)S(1)} collective-permute-done((bf16[96,576]{0,1:T(8,128)(2,1)S(1)}, bf16[96,576]{0,1:T(8,128)(2,1)S(1)}, u32[]{:S(2)}, u32[]{:S(2)}) %collective-permute-start.20) | collective-permute-done | bytes 110624 | tf_op jit(solution)/shard_map/ppermute | solution.py:496
  517.6 1.9 pad_maximum_fusion.3
  (244 shorter events, 78.2 us)
Async XLA Ops:
  7.2 19.7 %copy-start = (s32[2,2048]{1,0:T(2,128)S(1)}, s32[2,2048]{1,0:T(2,128)}, u32[]{:S(2)}) copy-start(s32[2,2048]{1,0:T(2,128)} %param.19) | copy-start | bytes 49156
  7.2 224.6 %all-gather.3.cloned.1.call-start = ((), (), s32[]{:S(2)}) async-start(), calls=%async_computation.2 | async-start | bytes 11354112 | tf_op jit(solution)/shard_map/all_gather | solution.py:556
  10.0 509.5 %reduce-scatter.2.cloned.1.call-start = ((), (), s32[]{:S(2)}) async-start(), calls=%async_computation.1 | async-start | bytes 11354112 | tf_op jit(solution)/shard_map/reduce_scatter | solution.py:606
  11.2 56.3 %collective-permute-start = (bf16[512,768]{1,0:T(8,128)(2,1)S(1)}, bf16[512,768]{1,0:T(8,128)(2,1)S(1)}, u32[]{:S(2)}, u32[]{:S(2)}) collective-permute-start(bf16[512,768]{1,0:T(8,128)(2,1)S(1)} %dynamic-slice_bitcast_fusion.2), channel_id=1, source_target_pairs={{0,2},{2,0},{1,3},{3,1},{4,6},{6,4},{5,7},{7,5},{8,10},{10,8},{9,1... | collective-permute-start | bytes 2359304 | tf_op jit(solution)/shard_map/ppermute | solution.py:496
  20.8 14.4 %collective-permute-start.6 = (bf16[1,384]{1,0:T(2,128)(2,1)S(1)}, bf16[1,384]{1,0:T(2,128)(2,1)S(1)}, u32[]{:S(2)}, u32[]{:S(2)}) collective-permute-start(bf16[1,384]{1,0:T(2,128)(2,1)S(1)} %reshape.358), channel_id=1, source_target_pairs={{0,2},{2,0},{1,3},{3,1},{4,6},{6,4},{5,7},{7,5},{8,10},{10,8},{9,1... | collective-permute-start | bytes 2312 | tf_op jit(solution)/shard_map/ppermute | solution.py:496
  22.5 25.4 %collective-permute-start.2 = (bf16[96,576]{1,0:T(8,128)(2,1)S(1)}, bf16[96,576]{1,0:T(8,128)(2,1)S(1)}, u32[]{:S(2)}, u32[]{:S(2)}) collective-permute-start(bf16[96,576]{1,0:T(8,128)(2,1)S(1)} %get-tuple-element.144), channel_id=1, source_target_pairs={{0,2},{2,0},{1,3},{3,1},{4,6},{6,4},{5,7},{7,5},{8,10},{10,8},{9,1... | collective-permute-start | bytes 331784 | tf_op jit(solution)/shard_map/ppermute | solution.py:496
  26.9 196.9 %collective-permute-start.13 = (bf16[512,768]{1,0:T(8,128)(2,1)}, bf16[512,768]{1,0:T(8,128)(2,1)}, u32[]{:S(2)}, u32[]{:S(2)}) collective-permute-start(bf16[512,768]{1,0:T(8,128)(2,1)} %fusion.16), channel_id=1, source_target_pairs={{0,2},{2,0},{1,3},{3,1},{4,6},{6,4},{5,7},{7,5},{8,10},{10,8},{9,1... | collective-permute-start | bytes 2359304 | tf_op jit(solution)/shard_map/ppermute | solution.py:496
  35.2 3.7 collective-permute-start.7
  38.9 3.7 collective-permute-start.8
  42.6 5.1 collective-permute-start.9
  47.8 44.1 %collective-permute-start.11 = (bf16[8,2,1,384]{3,0,1,2:T(8,128)(2,1)S(1)}, bf16[8,2,1,384]{3,0,1,2:T(8,128)(2,1)S(1)}, u32[]{:S(2)}, u32[]{:S(2)}) collective-permute-start(bf16[8,2,1,384]{3,0,1,2:T(8,128)(2,1)S(1)} %copy.169), channel_id=1, source_target_pairs={{0,1},{1,0},{2,3},{3,2},{4,5},{5,4},{6,7},{7,6},{8,9},{9,8},{10,11... | collective-permute-start | bytes 36872 | tf_op jit(solution)/shard_map/ppermute | solution.py:499
  47.9 18.7 %collective-permute-start.3 = (bf16[2,96,576]{2,1,0:T(8,128)(2,1)S(1)}, bf16[2,96,576]{2,1,0:T(8,128)(2,1)S(1)}, u32[]{:S(2)}, u32[]{:S(2)}) collective-permute-start(bf16[2,96,576]{2,1,0:T(8,128)(2,1)S(1)} %pad_maximum_fusion.9), channel_id=1, source_target_pairs={{0,16},{4,20},{8,24},{12,28},{16,0},{20,4},{24,8},{28,12},{1,17},{... | collective-permute-start | bytes 663560 | tf_op jit(solution)/shard_map/ppermute | solution.py:502
  67.5 22.2 %collective-permute-start.4 = (bf16[4,96,576]{2,1,0:T(8,128)(2,1)}, bf16[4,96,576]{2,1,0:T(8,128)(2,1)S(1)}, u32[]{:S(2)}, u32[]{:S(2)}) collective-permute-start(bf16[4,96,576]{2,1,0:T(8,128)(2,1)} %pad_maximum_fusion.8), channel_id=1, source_target_pairs={{0,8},{4,12},{8,0},{12,4},{16,24},{20,28},{24,16},{28,20},{1,9},{5... | collective-permute-start | bytes 1327112 | tf_op jit(solution)/shard_map/ppermute | solution.py:502
  70.1 51.8 %collective-permute-start.1 = (bf16[2,512,768]{2,1,0:T(8,128)(2,1)}, bf16[2,512,768]{2,1,0:T(8,128)(2,1)}, u32[]{:S(2)}, u32[]{:S(2)}) collective-permute-start(bf16[2,512,768]{2,1,0:T(8,128)(2,1)} %pad_maximum_fusion.4), channel_id=1, source_target_pairs={{0,1},{1,0},{2,3},{3,2},{4,5},{5,4},{6,7},{7,6},{8,9},{9,8},{10,11... | collective-permute-start | bytes 4718600 | tf_op jit(solution)/shard_map/ppermute | solution.py:499
  89.9 30.9 %collective-permute-start.5 = (bf16[8,96,576]{2,1,0:T(8,128)(2,1)S(1)}, bf16[8,96,576]{2,1,0:T(8,128)(2,1)S(1)}, u32[]{:S(2)}, u32[]{:S(2)}) collective-permute-start(bf16[8,96,576]{2,1,0:T(8,128)(2,1)S(1)} %pad_maximum_fusion.7), channel_id=1, source_target_pairs={{0,4},{4,0},{8,12},{12,8},{16,20},{20,16},{24,28},{28,24},{1,5},{5... | collective-permute-start | bytes 2654216 | tf_op jit(solution)/shard_map/ppermute | solution.py:502
  137.2 86.6 %copy-start.10 = (f32[2,512,768]{2,1,0:T(8,128)S(1)}, f32[2,512,768]{2,1,0:T(8,128)}, u32[]{:S(2)}) copy-start(f32[2,512,768]{2,1,0:T(8,128)} %param.35) | copy-start | bytes 9437188
  220.5 6.8 %collective-permute-start.10 = (bf16[2,512,384]{2,1,0:T(8,128)(2,1)}, bf16[2,512,384]{2,1,0:T(8,128)(2,1)}, u32[]{:S(2)}, u32[]{:S(2)}) collective-permute-start(bf16[2,512,384]{2,1,0:T(8,128)(2,1)} %dynamic-slice_bitcast_fusion.1), channel_id=1, source_target_pairs={{0,1},{1,0},{2,3},{3,2},{4,5},{5,4},{6,7},{7,6},{8,9},{9,8},{10,11... | collective-permute-start | bytes 2359304 | tf_op jit(solution)/shard_map/ppermute | solution.py:499
  225.2 2.1 copy-start.11
  263.7 1.9 copy-start.4
  269.3 1.7 copy-start.5
  305.7 1.7 copy-start.2
  314.0 1.4 copy-start.8
  318.7 6.4 %copy-start.13 = (f32[4,1,768]{2,1,0:T(1,128)S(1)}, f32[4,1,768]{2,1,0:T(1,128)}, u32[]{:S(2)}) copy-start(f32[4,1,768]{2,1,0:T(1,128)} %get-tuple-element.36) | copy-start | bytes 36868
  323.1 4.2 copy-start.6
  324.1 5.6 %collective-permute-start.14 = (bf16[2,512,384]{2,1,0:T(8,128)(2,1)}, bf16[2,512,384]{2,1,0:T(8,128)(2,1)}, u32[]{:S(2)}, u32[]{:S(2)}) collective-permute-start(bf16[2,512,384]{2,1,0:T(8,128)(2,1)} %bitcast.251), channel_id=1, source_target_pairs={{0,1},{1,0},{2,3},{3,2},{4,5},{5,4},{6,7},{7,6},{8,9},{9,8},{10,11... | collective-permute-start | bytes 2359304 | tf_op jit(solution)/shard_map/ppermute | solution.py:499
  328.3 126.7 %collective-permute-start.12 = (bf16[512,768]{1,0:T(8,128)(2,1)}, bf16[512,768]{1,0:T(8,128)(2,1)}, u32[]{:S(2)}, u32[]{:S(2)}) collective-permute-start(bf16[512,768]{1,0:T(8,128)(2,1)} %fusion.15), channel_id=1, source_target_pairs={{0,2},{2,0},{1,3},{3,1},{4,6},{6,4},{5,7},{7,5},{8,10},{10,8},{9,1... | collective-permute-start | bytes 2359304 | tf_op jit(solution)/shard_map/ppermute | solution.py:496
  416.4 10.7 %slice-start = ((s8[4718592]{0:T(1024)(128)(4,1)}), s8[4194304]{0:T(1024)(128)(4,1)S(1)}, s32[]{:S(2)}) async-start(s8[4718592]{0:T(1024)(128)(4,1)} %bitcast.263), calls=%async_computation.3 | async-start | bytes 8388608
  416.4 10.7 %slice-start.1 = ((s8[4718592]{0:T(1024)(128)(4,1)}), s8[524288]{0:T(1024)(128)(4,1)S(1)}, s32[]{:S(2)}) async-start(s8[4718592]{0:T(1024)(128)(4,1)} %bitcast.263), calls=%async_computation.4 | async-start | bytes 1048576
  416.4 10.7 %copy-start.14 = (bf16[768,1152]{1,0:T(8,128)(2,1)S(1)}, bf16[768,1152]{1,0:T(8,128)(2,1)}, u32[]{:S(2)}) copy-start(bf16[768,1152]{1,0:T(8,128)(2,1)} %get-tuple-element.34) | copy-start | bytes 5308420
  416.4 17.0 %collective-permute-start.21 = (f32[8,2,384]{2,0,1:T(8,128)S(1)}, f32[8,2,384]{2,0,1:T(8,128)S(1)}, u32[]{:S(2)}, u32[]{:S(2)}) collective-permute-start(f32[8,2,384]{2,0,1:T(8,128)S(1)} %fusion.24), channel_id=1, source_target_pairs={{0,1},{1,0},{2,3},{3,2},{4,5},{5,4},{6,7},{7,6},{8,9},{9,8},{10,11... | collective-permute-start | bytes 73736 | tf_op jit(solution)/shard_map/ppermute | solution.py:499
  424.3 1.2 copy-start.9
  426.4 26.2 %collective-permute-start.17 = (bf16[4,96,1152]{2,1,0:T(8,128)(2,1)}, bf16[4,96,1152]{2,1,0:T(8,128)(2,1)}, u32[]{:S(2)}, u32[]{:S(2)}) collective-permute-start(bf16[4,96,1152]{2,1,0:T(8,128)(2,1)} %dynamic-slice_bitcast_fusion), channel_id=1, source_target_pairs={{0,4},{4,0},{8,12},{12,8},{16,20},{20,16},{24,28},{28,24},{1,5},{5... | collective-permute-start | bytes 2654216 | tf_op jit(solution)/shard_map/ppermute | solution.py:502
  433.6 17.5 %collective-permute-start.22 = (f32[4,2,384]{2,0,1:T(4,128)S(1)}, f32[4,2,384]{2,0,1:T(4,128)S(1)}, u32[]{:S(2)}, u32[]{:S(2)}) collective-permute-start(f32[4,2,384]{2,0,1:T(4,128)S(1)} %bitcast.307), channel_id=1, source_target_pairs={{0,4},{4,0},{8,12},{12,8},{16,20},{20,16},{24,28},{28,24},{1,5},{5... | collective-permute-start | bytes 36872 | tf_op jit(solution)/shard_map/ppermute | solution.py:502
  438.4 47.5 %collective-permute-start.15 = (bf16[2,512,768]{2,1,0:T(8,128)(2,1)}, bf16[2,512,768]{2,1,0:T(8,128)(2,1)}, u32[]{:S(2)}, u32[]{:S(2)}) collective-permute-start(bf16[2,512,768]{2,1,0:T(8,128)(2,1)} %fusion.9), channel_id=1, source_target_pairs={{0,1},{1,0},{2,3},{3,2},{4,5},{5,4},{6,7},{7,6},{8,9},{9,8},{10,11... | collective-permute-start | bytes 4718600 | tf_op jit(solution)/shard_map/ppermute | solution.py:499
  451.1 5.2 collective-permute-start.23
  454.4 16.4 %collective-permute-start.18 = (bf16[2,96,1152]{2,1,0:T(8,128)(2,1)S(1)}, bf16[2,96,1152]{2,1,0:T(8,128)(2,1)S(1)}, u32[]{:S(2)}, u32[]{:S(2)}) collective-permute-start(bf16[2,96,1152]{2,1,0:T(8,128)(2,1)S(1)} %dynamic-slice_bitcast_fusion.3), channel_id=1, source_target_pairs={{0,8},{4,12},{8,0},{12,4},{16,24},{20,28},{24,16},{28,20},{1,9},{5... | collective-permute-start | bytes 1327112 | tf_op jit(solution)/shard_map/ppermute | solution.py:502
  456.4 16.8 %collective-permute-start.24 = (f32[1,2,384]{2,0,1:T(1,128)S(1)}, f32[1,2,384]{2,0,1:T(1,128)S(1)}, u32[]{:S(2)}, u32[]{:S(2)}) collective-permute-start(f32[1,2,384]{2,0,1:T(1,128)S(1)} %constant_dynamic-slice_fusion.2), channel_id=1, source_target_pairs={{0,16},{4,20},{8,24},{12,28},{16,0},{20,4},{24,8},{28,12},{1,17},{... | collective-permute-start | bytes 9224 | tf_op jit(solution)/shard_map/ppermute | solution.py:502
  471.0 12.8 %collective-permute-start.19 = (bf16[1,96,1152]{2,1,0:T(8,128)(2,1)S(1)}, bf16[1,96,1152]{2,1,0:T(8,128)(2,1)S(1)}, u32[]{:S(2)}, u32[]{:S(2)}) collective-permute-start(bf16[1,96,1152]{2,1,0:T(8,128)(2,1)S(1)} %constant_dynamic-slice_fusion.8), channel_id=1, source_target_pairs={{0,16},{4,20},{8,24},{12,28},{16,0},{20,4},{24,8},{28,12},{1,17},{... | collective-permute-start | bytes 663560 | tf_op jit(solution)/shard_map/ppermute | solution.py:502
  473.2 4.7 collective-permute-start.25
  476.0 9.8 %copy-start.3 = (f32[1024,768]{1,0:T(8,128)S(1)}, f32[1024,768]{1,0:T(8,128)}, u32[]{:S(2)}) copy-start(f32[1024,768]{1,0:T(8,128)} %copy-done.2) | copy-start | bytes 9437188
  485.8 6.7 %copy-start.12 = (bf16[2,96,3,192]{1,3,2,0:T(8,128)(2,1)}, bf16[2,96,3,192]{1,3,2,0:T(8,128)(2,1)S(1)}, u32[]{:S(2)}) copy-start(bf16[2,96,3,192]{1,3,2,0:T(8,128)(2,1)S(1)} %copy.194) | copy-start | bytes 663556
  488.8 1.7 copy-start.7
  490.6 25.4 %collective-permute-start.16 = (bf16[512,768]{1,0:T(8,128)(2,1)S(1)}, bf16[512,768]{1,0:T(8,128)(2,1)S(1)}, u32[]{:S(2)}, u32[]{:S(2)}) collective-permute-start(bf16[512,768]{1,0:T(8,128)(2,1)S(1)} %fusion.17), channel_id=1, source_target_pairs={{0,2},{2,0},{1,3},{3,1},{4,6},{6,4},{5,7},{7,5},{8,10},{10,8},{9,1... | collective-permute-start | bytes 2359304 | tf_op jit(solution)/shard_map/ppermute | solution.py:496
  492.5 20.3 %collective-permute-start.20 = (bf16[96,576]{0,1:T(8,128)(2,1)S(1)}, bf16[96,576]{0,1:T(8,128)(2,1)S(1)}, u32[]{:S(2)}, u32[]{:S(2)}) collective-permute-start(bf16[96,576]{0,1:T(8,128)(2,1)S(1)} %dynamic-slice_bitcast_fusion.4), channel_id=1, source_target_pairs={{0,2},{2,0},{1,3},{3,1},{4,6},{6,4},{5,7},{7,5},{8,10},{10,8},{9,1... | collective-permute-start | bytes 331784 | tf_op jit(solution)/shard_map/ppermute | solution.py:496
  517.6 4.5 copy-start.1
Sparse Core Ops, SparseCore 0:
  10.9 112.2 all-gather.2
  314.1 151.1 reduce-scatter.1
where the time goes:
time: 535 us; the launch traced here: 529 us
  Pallas kernels  224 us (42%)
  waiting for transfers between devices  116 us (22%)
  local copies, waits for them, and re-layouts  65.5 us (12%)
  other arithmetic  50.7 us (9%)
  starting transfers between devices  37.3 us (7%)
  matrix products  20.5 us (4%)
  between operations  15.3 us (3%)
    ppermute x12, waiting for transfers between devices, swap_bit(): return lax.ppermute(value, 'dp', [(i, i ^ 1 << b) for i in range(dp)])  91.2 us
    pallas_call x1, Pallas kernels, attention_forward(): pl.pallas_call(attention_forward_kernel, name='attention_forward', out_sh...  81.2 us
    pallas_call x1, Pallas kernels, attention_backward(): pl.pallas_call(attention_backward_kernel, name='attention_backward', out_...  79.4 us
    pallas_call x1, Pallas kernels, feed_forward_backward(): pl.pallas_call(feed_forward_backward_kernel, name='feed_forward_backward'...  28.4 us
    ppermute x12, starting transfers between devices, swap_bit(): return lax.ppermute(value, 'dp', [(i, i ^ 1 << b) for i in range(dp)])  24.5 us
    ppermute x8, waiting for transfers between devices, swap_chips(): return lax.ppermute(value, 'tensor', [(0, 2), (2, 0), (1, 3), (3, 1)])  24.5 us
    unnamed x49, local copies, waits for them, and re-layouts  19 us
    pallas_call x1, Pallas kernels, feed_forward(): pl.pallas_call(feed_forward_kernel, name='feed_forward', out_shape=(jax.S...  18.2 us
  transfers between devices with their start and end apart: 28, of which 11 were waited for; matrix products, arithmetic and copies ran while one was open for 18% of the time, Pallas kernels for 33%

commit v1 on v0

--- a/solution.py
+++ b/solution.py
@@ -8,9 +8,14 @@
 HD = 64
 PAIR = 2 * HD
 SEGS = 12
-QB = 256
+QB = 512
 KB = 256
+RB = 256
 NEG = -1e30
+LIMIT = 50.0
+GAP = 256.0
+FREE = SEGS + 1
+EXTRA = 16
 EPS = 1e-12
 BF = jnp.bfloat16
 F32 = jnp.float32
@@ -18,183 +23,259 @@
 NT = (((1,), (1,)), ((), ()))
 
 
-def head_parts(block, scale=None):
-    wide = block.astype(F32)
-    if scale is not None:
-        wide = wide * scale
-    lane = lax.broadcasted_iota(jnp.int32, block.shape, 1)
-    first = jnp.where(lane < HD, wide, 0.0).astype(BF)
-    second = jnp.where(lane >= HD, wide, 0.0).astype(BF)
-    return first, second
-
-
-def attention_forward_kernel(lo_ref, hi_ref, bound_ref, q_ref, k_ref, v_ref, o_ref, lse_ref, vt_ref, acc_ref):
-    row = pl.program_id(1)
+def own_lanes(shape, h):
+    lane = lax.broadcasted_iota(jnp.int32, shape, 1)
+    return (lane < HD) if h % 2 == 0 else (lane >= HD)
+
+
+def with_column(base, column, h):
+    lane = lax.broadcasted_iota(jnp.int32, base.shape, 1) - (HD if h % 2 == 0 else 0)
+    high = column.astype(BF).astype(F32)
+    middle = (column - high).astype(BF).astype(F32)
+    low = column - high - middle
+    base = jnp.where(lane == FREE, high, base)
+    base = jnp.where(lane == FREE + 1, middle, base)
+    return jnp.where(lane == FREE + 2, low, base)
+
+
+def fits(limit_ref, heads):
+    largest = limit_ref[0, 0] * limit_ref[0, heads]
+    for h in range(1, heads):
+        largest = jnp.maximum(largest, limit_ref[0, h] * limit_ref[0, heads + h])
+    return largest <= LIMIT * LIMIT
+
+
+def attention_forward_kernel(
+    lo_ref, hi_ref, limit_ref, bound_ref, q_ref, key_ref, val_ref, o_ref, lse_ref, acc_ref, top_ref
+):
+    row = pl.program_id(0)
+    heads = key_ref.shape[1] // PAIR
+    acc_ref[...] = jnp.zeros_like(acc_ref)
+    plain = fits(limit_ref, heads)
+
+    @pl.when(plain)
+    def _():
+        def step(kb, carry):
+            there = pl.ds(pl.multiple_of(kb * KB, KB), KB)
+            for h in range(heads):
+                cols = slice(h * PAIR, (h + 1) * PAIR)
+                scores = lax.dot_general(q_ref[:, cols], key_ref[there, cols], NT, preferred_element_type=F32)
+                raised = jnp.exp(scores).astype(BF)
+                acc_ref[:, cols] += jnp.dot(raised, val_ref[there, cols], preferred_element_type=F32)
+            return carry
+
+        lax.fori_loop(lo_ref[row], hi_ref[row], step, 0)
+        top_ref[...] = jnp.zeros_like(top_ref)
+
+    @pl.when(jnp.logical_not(plain))
+    def _():
+        start = bound_ref[0, 0:1, :].T
+        end = bound_ref[0, 1:2, :].T
+        top_ref[...] = jnp.full_like(top_ref, NEG)
+
+        def step(kb, carry):
+            base = pl.multiple_of(kb * KB, KB)
+            there = pl.ds(base, KB)
+            place = base + lax.broadcasted_iota(jnp.int32, (QB, KB), 1)
+            valid = (place >= start) & (place < end)
+            for h in range(heads):
+                cols = slice(h * PAIR, (h + 1) * PAIR)
+                scores = lax.dot_general(q_ref[:, cols], key_ref[there, cols], NT, preferred_element_type=F32)
+                scores = jnp.where(valid, scores, NEG)
+                before = top_ref[:, h : h + 1]
+                top = jnp.maximum(before, jnp.max(scores, axis=1, keepdims=True))
+                raised = jnp.exp(scores - top).astype(BF)
+                acc_ref[:, cols] = jnp.exp(before - top) * acc_ref[:, cols] + jnp.dot(
+                    raised, val_ref[there, cols], preferred_element_type=F32
+                )
+                top_ref[:, h : h + 1] = top
+            return carry
+
+        lax.fori_loop(lo_ref[row], hi_ref[row], step, 0)
+
+    lse = top_ref[...]
+    lane = lax.broadcasted_iota(jnp.int32, (QB, PAIR), 1)
+    for p in range(heads // 2):
+        both = []
+        for h in (2 * p, 2 * p + 1):
+            block = acc_ref[:, h * PAIR : (h + 1) * PAIR]
+            at = SEGS + (HD if h % 2 == 0 else 0)
+            total = block[:, at : at + 1]
+            both.append(block / total)
+            lse = jnp.where(lane == h, lse + jnp.log(total), lse)
+        o_ref[:, p * PAIR : (p + 1) * PAIR] = jnp.where(lane < HD, both[0], both[1]).astype(BF)
+    lse_ref[...] = lse
+
+
+def attention_backward_kernel(
+    lo_ref,
+    hi_ref,
+    limit_ref,
+    bound_ref,
+    lse_ref,
+    q_ref,
+    key_ref,
+    val_ref,
+    kt_ref,
+    do_ref,
+    o_ref,
+    out_ref,
+    dq_ref,
+    dk_ref,
+    dv_ref,
+):
+    row = pl.program_id(0)
+    heads = key_ref.shape[1] // PAIR
+    pairs = heads // 2
 
     @pl.when(row == 0)
     def _():
-        vt_ref[...] = v_ref[...].T
-
-    parts = head_parts(q_ref[...], HD ** (-0.5))
-    start = bound_ref[0, 0:1, :]
-    end = bound_ref[0, 1:2, :]
-    acc_ref[...] = jnp.zeros_like(acc_ref)
-
-    def step(kb, carry):
-        base = pl.multiple_of(kb * KB, KB)
-        keys = k_ref[pl.ds(base, KB), :]
-        place = base + lax.broadcasted_iota(jnp.int32, (KB, QB), 0)
-        valid = (place >= start) & (place < end)
-        after = []
-        for h in range(2):
-            top, total = carry[2 * h], carry[2 * h + 1]
-            scores = lax.dot_general(keys, parts[h], NT, preferred_element_type=F32)
-            scores = jnp.where(valid, scores, NEG)
-            new_top = jnp.maximum(top, jnp.max(scores, axis=0, keepdims=True))
-            fade = jnp.exp(top - new_top)
-            raised = jnp.exp(scores - new_top)
-            total = fade * total + jnp.sum(raised, axis=0, keepdims=True)
-            rows = slice(h * HD, (h + 1) * HD)
-            acc_ref[rows, :] = fade * acc_ref[rows, :] + jnp.dot(
-                vt_ref[rows, pl.ds(base, KB)], raised.astype(BF), preferred_element_type=F32
-            )
-            after += [new_top, total]
-        return tuple(after)
-
-    low = jnp.full((1, QB), NEG, F32)
-    none = jnp.zeros((1, QB), F32)
-    top0, total0, top1, total1 = lax.fori_loop(lo_ref[row], hi_ref[row], step, (low, none, low, none))
-    acc_ref[0:HD, :] = acc_ref[0:HD, :] / total0
-    acc_ref[HD:PAIR, :] = acc_ref[HD:PAIR, :] / total1
-    o_ref[...] = acc_ref[...].T.astype(BF)
-    lse_ref[0, 0, 0:1, :] = top0 + jnp.log(total0)
-    lse_ref[0, 0, 1:2, :] = top1 + jnp.log(total1)
-
-
-def attention_backward_kernel(
-    lo_ref, hi_ref, bound_ref, lse_ref, q_ref, k_ref, v_ref, do_ref, o_ref, out_ref, kt_ref, dq_ref, dk_ref, dv_ref
-):
-    row = pl.program_id(1)
-
-    @pl.when(row == 0)
-    def _():
-        kt_ref[...] = k_ref[...].T
         dk_ref[...] = jnp.zeros_like(dk_ref)
         dv_ref[...] = jnp.zeros_like(dv_ref)
 
-    q_parts = head_parts(q_ref[...], HD ** (-0.5))
-    grad = do_ref[...]
-    g_parts = head_parts(grad)
-    start = bound_ref[0, 0:1, :]
-    end = bound_ref[0, 1:2, :]
-    product = grad.astype(F32) * o_ref[...].astype(F32)
-    picker_row = lax.broadcasted_iota(jnp.int32, (8, PAIR), 0)
-    picker_lane = lax.broadcasted_iota(jnp.int32, (8, PAIR), 1)
-    picker = jnp.where(picker_lane // HD == picker_row, 1.0, 0.0).astype(F32)
-    inner = lax.dot_general(picker, product, NT, precision=lax.Precision.HIGHEST, preferred_element_type=F32)
+    here = pl.ds(pl.multiple_of(row * QB, QB), QB)
+    q_parts, g_parts, q_score, g_score = [], [], [], []
+    for p in range(pairs):
+        cols = slice(p * PAIR, (p + 1) * PAIR)
+        grad = do_ref[:, cols].astype(F32)
+        product = grad * o_ref[:, cols].astype(F32)
+        for h in (2 * p, 2 * p + 1):
+            block = q_ref[:, h * PAIR : (h + 1) * PAIR].astype(F32)
+            own = own_lanes(block.shape, h)
+            inner = jnp.sum(jnp.where(own, product, 0.0), axis=1, keepdims=True)
+            g_own = jnp.where(own, grad, 0.0)
+            q_parts.append(jnp.where(own, block, 0.0).astype(BF))
+            g_parts.append(g_own.astype(BF))
+            q_score.append(with_column(block, -lse_ref[:, h : h + 1], h).astype(BF))
+            g_score.append(with_column(g_own, -inner, h).astype(BF))
     dq_ref[...] = jnp.zeros_like(dq_ref)
 
-    def step(kb, carry):
-        base = pl.multiple_of(kb * KB, KB)
-        keys = k_ref[pl.ds(base, KB), :]
-        vals = v_ref[pl.ds(base, KB), :]
-        place = base + lax.broadcasted_iota(jnp.int32, (KB, QB), 0)
-        valid = (place >= start) & (place < end)
-        dk = dk_ref[pl.ds(base, KB), :]
-        dv = dv_ref[pl.ds(base, KB), :]
-        for h in range(2):
-            scores = lax.dot_general(keys, q_parts[h], NT, preferred_element_type=F32)
-            scores = jnp.where(valid, scores, NEG)
-            weights = jnp.exp(scores - lse_ref[0, 0, h : h + 1, :])
-            grad_weights = lax.dot_general(vals, g_parts[h], NT, preferred_element_type=F32)
-            grad_scores = (weights * (grad_weights - inner[h : h + 1, :])).astype(BF)
-            dv = dv + jnp.dot(weights.astype(BF), g_parts[h], preferred_element_type=F32)
-            dk = dk + jnp.dot(grad_scores, q_parts[h], preferred_element_type=F32)
-            rows = slice(h * HD, (h + 1) * HD)
-            dq_ref[rows, :] += jnp.dot(kt_ref[rows, pl.ds(base, KB)], grad_scores, preferred_element_type=F32)
-        dk_ref[pl.ds(base, KB), :] = dk
-        dv_ref[pl.ds(base, KB), :] = dv
-        return carry
-
-    lax.fori_loop(lo_ref[row], hi_ref[row], step, 0)
-    out_ref[pl.ds(pl.multiple_of(row * QB, QB), QB), 0:PAIR] = (dq_ref[...] * HD ** (-0.5)).T.astype(BF)
-
-    @pl.when(row == pl.num_programs(1) - 1)
+    def sweep(masked):
+        start = bound_ref[0, 0:1, :]
+        end = bound_ref[0, 1:2, :]
+
+        def step(kb, carry):
+            base = pl.multiple_of(kb * KB, KB)
+            there = pl.ds(base, KB)
+            if masked:
+                place = base + lax.broadcasted_iota(jnp.int32, (KB, QB), 0)
+                valid = (place >= start) & (place < end)
+            for p in range(pairs):
+                cols = slice(p * PAIR, (p + 1) * PAIR)
+                dk = dk_ref[there, cols]
+                dv = dv_ref[there, cols]
+                for h in (2 * p, 2 * p + 1):
+                    keys = key_ref[there, h * PAIR : (h + 1) * PAIR]
+                    vals = val_ref[there, h * PAIR : (h + 1) * PAIR]
+                    scores = lax.dot_general(keys, q_score[h], NT, preferred_element_type=F32)
+                    if masked:
+                        scores = jnp.where(valid, scores, NEG)
+                    weights = jnp.exp(scores)
+                    grad_scores = weights * lax.dot_general(vals, g_score[h], NT, preferred_element_type=F32)
+                    grad_scores = grad_scores.astype(BF)
+                    dv = dv + jnp.dot(weights.astype(BF), g_parts[h], preferred_element_type=F32)
+                    dk = dk + jnp.dot(grad_scores, q_parts[h], preferred_element_type=F32)
+                    rows = slice(h * HD, (h + 1) * HD)
+                    dq_ref[rows, :] += jnp.dot(kt_ref[rows, there], grad_scores, preferred_element_type=F32)
+                dk_ref[there, cols] = dk
+                dv_ref[there, cols] = dv
+            return carry
+
+        lax.fori_loop(lo_ref[row], hi_ref[row], step, 0)
+
+    plain = fits(limit_ref, heads)
+    pl.when(plain)(lambda: sweep(False))
+    pl.when(jnp.logical_not(plain))(lambda: sweep(True))
+    for p in range(pairs):
+        cols = slice(p * PAIR, (p + 1) * PAIR)
+        out_ref[here, 3 * p * PAIR : (3 * p + 1) * PAIR] = (dq_ref[cols, :] * HD ** (-0.5)).T.astype(BF)
+
+    @pl.when(row == pl.num_programs(0) - 1)
     def _():
-        out_ref[:, PAIR : 2 * PAIR] = dk_ref[...].astype(BF)
-        out_ref[:, 2 * PAIR : 3 * PAIR] = dv_ref[...].astype(BF)
-
-
-def attention_forward(qkv, lo, hi, bounds):
-    length = qkv.shape[0]
-    pairs = qkv.shape[1] // (3 * PAIR)
-    blocks = length // QB
+        for p in range(pairs):
+            cols = slice(p * PAIR, (p + 1) * PAIR)
+            out_ref[:, (3 * p + 1) * PAIR : (3 * p + 2) * PAIR] = dk_ref[:, cols].astype(BF)
+            out_ref[:, (3 * p + 2) * PAIR : (3 * p + 3) * PAIR] = dv_ref[:, cols].astype(BF)
+
+
+def attention_forward(operands, limits, segments):
+    queries, keys, values, _ = operands
+    lo, hi, bounds = segments[:3]
+    length, wide = keys.shape
+    heads = wide // PAIR
+    whole = pl.BlockSpec((length, wide), lambda i, lo, hi: (0, 0))
     return pl.pallas_call(
         attention_forward_kernel,
         name="attention_forward",
         out_shape=(
-            jax.ShapeDtypeStruct((length, pairs * PAIR), BF),
-            jax.ShapeDtypeStruct((pairs, blocks, 2, QB), F32),
+            jax.ShapeDtypeStruct((length, heads * HD), BF),
+            jax.ShapeDtypeStruct((length, PAIR), F32),
         ),
         grid_spec=pltpu.PrefetchScalarGridSpec(
             num_scalar_prefetch=2,
-            grid=(pairs, blocks),
+            grid=(length // QB,),
             in_specs=[
-                pl.BlockSpec((1, 2, QB), lambda j, i, lo, hi: (i, 0, 0)),
-                pl.BlockSpec((QB, PAIR), lambda j, i, lo, hi: (i, 3 * j)),
-                pl.BlockSpec((length, PAIR), lambda j, i, lo, hi: (0, 3 * j + 1)),
-                pl.BlockSpec((length, PAIR), lambda j, i, lo, hi: (0, 3 * j + 2)),
+                pl.BlockSpec(memory_space=pltpu.SMEM),
+                pl.BlockSpec((1, 2, QB), lambda i, lo, hi: (i, 0, 0)),
+                pl.BlockSpec((QB, wide), lambda i, lo, hi: (i, 0)),
+                whole,
+                whole,
             ],
             out_specs=(
-                pl.BlockSpec((QB, PAIR), lambda j, i, lo, hi: (i, j)),
-                pl.BlockSpec((1, 1, 2, QB), lambda j, i, lo, hi: (j, i, 0, 0)),
+                pl.BlockSpec((QB, heads * HD), lambda i, lo, hi: (i, 0)),
+                pl.BlockSpec((QB, PAIR), lambda i, lo, hi: (i, 0)),
             ),
-            scratch_shapes=[pltpu.VMEM((PAIR, length), BF), pltpu.VMEM((PAIR, QB), F32)],
+            scratch_shapes=[pltpu.VMEM((QB, wide), F32), pltpu.VMEM((QB, PAIR), F32)],
         ),
         cost_estimate=pl.CostEstimate(
-            flops=pairs * length * length * PAIR * 4,
-            transcendentals=pairs * length * length,
-            bytes_accessed=qkv.size * 2 + length * pairs * PAIR * 2,
-        ),
-        compiler_params=pltpu.CompilerParams(dimension_semantics=("arbitrary", "arbitrary")),
-    )(lo, hi, bounds, qkv, qkv, qkv)
-
-
-def attention_backward(qkv, grad, out, lse, lo, hi, bounds):
-    length = qkv.shape[0]
-    pairs = qkv.shape[1] // (3 * PAIR)
-    blocks = length // QB
+            flops=length * length * wide * 2,
+            transcendentals=length * length * heads,
+            bytes_accessed=keys.size * 7,
+        ),
+        compiler_params=pltpu.CompilerParams(dimension_semantics=("arbitrary",)),
+    )(lo, hi, limits, bounds, queries, keys, values)
+
+
+def attention_backward(operands, grad, out, lse, limits, segments):
+    queries, keys, values, turned = operands
+    lo, hi, bounds = segments[:3]
+    length, wide = keys.shape
+    heads = wide // PAIR
+    width = heads * HD
+    whole = pl.BlockSpec((length, wide), lambda i, lo, hi: (0, 0))
+    rows = pl.BlockSpec((QB, width), lambda i, lo, hi: (i, 0))
     return pl.pallas_call(
         attention_backward_kernel,
         name="attention_backward",
-        out_shape=jax.ShapeDtypeStruct(qkv.shape, BF),
+        out_shape=jax.ShapeDtypeStruct((length, 3 * width), BF),
         grid_spec=pltpu.PrefetchScalarGridSpec(
             num_scalar_prefetch=2,
-            grid=(pairs, blocks),
+            grid=(length // QB,),
             in_specs=[
-                pl.BlockSpec((1, 2, QB), lambda j, i, lo, hi: (i, 0, 0)),
-                pl.BlockSpec((1, 1, 2, QB), lambda j, i, lo, hi: (j, i, 0, 0)),
-                pl.BlockSpec((QB, PAIR), lambda j, i, lo, hi: (i, 3 * j)),
-                pl.BlockSpec((length, PAIR), lambda j, i, lo, hi: (0, 3 * j + 1)),
-                pl.BlockSpec((length, PAIR), lambda j, i, lo, hi: (0, 3 * j + 2)),
-                pl.BlockSpec((QB, PAIR), lambda j, i, lo, hi: (i, j)),
-                pl.BlockSpec((QB, PAIR), lambda j, i, lo, hi: (i, j)),
+                pl.BlockSpec(memory_space=pltpu.SMEM),
+                pl.BlockSpec((1, 2, QB), lambda i, lo, hi: (i, 0, 0)),
+                pl.BlockSpec((QB, PAIR), lambda i, lo, hi: (i, 0)),
+                pl.BlockSpec((QB, wide), lambda i, lo, hi: (i, 0)),
+                whole,
+                whole,
+                pl.BlockSpec((width, length), lambda i, lo, hi: (0, 0)),
+                rows,
+                rows,
             ],
-            out_specs=pl.BlockSpec((length, 3 * PAIR), lambda j, i, lo, hi: (0, j)),
+            out_specs=pl.BlockSpec((length, 3 * width), lambda i, lo, hi: (0, 0)),
             scratch_shapes=[
-                pltpu.VMEM((PAIR, length), BF),
-                pltpu.VMEM((PAIR, QB), F32),
-                pltpu.VMEM((length, PAIR), F32),
-                pltpu.VMEM((length, PAIR), F32),
+                pltpu.VMEM((width, QB), F32),
+                pltpu.VMEM((length, width), F32),
+                pltpu.VMEM((length, width), F32),
             ],
         ),
         cost_estimate=pl.CostEstimate(
-            flops=pairs * length * length * PAIR * 10,
-            transcendentals=pairs * length * length,
-            bytes_accessed=qkv.size * 4 + length * pairs * PAIR * 4,
-        ),
-        compiler_params=pltpu.CompilerParams(dimension_semantics=("arbitrary", "arbitrary")),
-    )(lo, hi, bounds, lse, qkv, qkv, qkv, grad, out)
+            flops=length * length * wide * 5,
+            transcendentals=length * length * heads,
+            bytes_accessed=keys.size * 11,
+        ),
+        compiler_params=pltpu.CompilerParams(dimension_semantics=("arbitrary",)),
+    )(lo, hi, limits, bounds, lse, queries, keys, values, turned, grad, out)
 
 
 def segment_bounds(segments):
@@ -207,7 +288,11 @@
     end = end.reshape(length // QB, QB)
     lo = start[:, 0] // KB
     hi = (end[:, -1] + (KB - 1)) // KB
-    return lo, hi, jnp.stack([start, end], axis=1)
+    lane = jnp.arange(PAIR, dtype=jnp.int32)[None, :] % HD
+    same = lane == segments[:, None]
+    pattern = jnp.where((lane < SEGS) & same | (lane >= SEGS) & (lane < FREE + 3), 1.0, 0.0).astype(BF)
+    qpattern = jnp.where(lane == SEGS, -GAP, jnp.where(same, GAP, 0.0)).astype(BF)
+    return lo, hi, jnp.stack([start, end], axis=1), pattern, qpattern
 
 
 def statistics(rows):
@@ -242,10 +327,13 @@
     return block.reshape(block.shape[0] * block.shape[1], block.shape[2])
 
 
-def project_kernel(spot_ref, tokens_ref, weights_ref, bias_ref, qkv_ref, w_ref):
+def project_kernel(
+    spot_ref, tokens_ref, weights_ref, bias_ref, pattern_ref, qpattern_ref, q_ref, k_ref, v_ref, kt_ref, w_ref, limit_ref
+):
     slots, cut, width = weights_ref.shape
     columns = width // 3
     bits = (slots // 2).bit_length() - 1
+    pairs = 2 * columns // PAIR
 
     @pl.when(pl.program_id(0) == 0)
     def _():
@@ -259,41 +347,76 @@
             for s in range(3):
                 cols = slice(s * columns, (s + 1) * columns)
                 joined = jnp.concatenate([first[:, cols], second[:, cols]], axis=1).astype(BF)
-                for p in range(2 * columns // PAIR):
+                for p in range(pairs):
                     at = (3 * p + s) * PAIR
                     w_ref[d * cut : (d + 1) * cut, at : at + PAIR] = joined[:, p * PAIR : (p + 1) * PAIR]
-
-    qkv_ref[...] = (mm(tokens_ref[...], w_ref[...]) + bias_ref[...]).astype(BF)
-
-
-def project(tokens, weights, bias, spot):
+        limit_ref[...] = jnp.zeros_like(limit_ref)
+
+    pattern = pattern_ref[...].astype(F32)
+    qpattern = qpattern_ref[...].astype(F32)
+    lane = lax.broadcasted_iota(jnp.int32, (8, PAIR), 1)[0:1, :]
+    largest = limit_ref[...]
+    for p in range(pairs):
+        cols = slice(3 * p * PAIR, 3 * (p + 1) * PAIR)
+        result = (mm(tokens_ref[...], w_ref[:, cols]) + bias_ref[:, cols]).astype(BF).astype(F32)
+        queries = result[:, :PAIR] * HD ** (-0.5)
+        keys = result[:, PAIR : 2 * PAIR]
+        values = result[:, 2 * PAIR :]
+        kt_ref[p * PAIR : (p + 1) * PAIR, :] = keys.astype(BF).T
+        for h in (2 * p, 2 * p + 1):
+            own = own_lanes(queries.shape, h)
+            at = slice(h * PAIR, (h + 1) * PAIR)
+            q_ref[:, at] = jnp.where(own, queries, qpattern).astype(BF)
+            k_ref[:, at] = jnp.where(own, keys, pattern).astype(BF)
+            v_ref[:, at] = jnp.where(own, values, pattern).astype(BF)
+            for kind, part in enumerate((queries, keys)):
+                square = jnp.sum(jnp.where(own, part * part, 0.0), axis=1, keepdims=True)
+                peak = jnp.max(square, axis=0, keepdims=True)
+                largest = jnp.where(lane == kind * 2 * pairs + h, jnp.maximum(largest, peak), largest)
+    limit_ref[...] = largest
+
+
+def project(tokens, weights, bias, spot, pattern, qpattern):
     length, features = tokens.shape
     width = 2 * weights.shape[2]
+    wide = 2 * width // 3
+    lanes = pl.BlockSpec((RB, PAIR), lambda i, spot: (i, 0))
+    rows = pl.BlockSpec((RB, wide), lambda i, spot: (i, 0))
     return pl.pallas_call(
         project_kernel,
         name="project",
         out_shape=(
-            jax.ShapeDtypeStruct((length, width), BF),
+            jax.ShapeDtypeStruct((length, wide), BF),
+            jax.ShapeDtypeStruct((length, wide), BF),
+            jax.ShapeDtypeStruct((length, wide), BF),
+            jax.ShapeDtypeStruct((width // 3, length), BF),
             jax.ShapeDtypeStruct((features, width), BF),
+            jax.ShapeDtypeStruct((1, PAIR), F32),
         ),
         grid_spec=pltpu.PrefetchScalarGridSpec(
             num_scalar_prefetch=1,
-            grid=(length // QB,),
+            grid=(length // RB,),
             in_specs=[
-                pl.BlockSpec((QB, features), lambda i, spot: (i, 0)),
+                pl.BlockSpec((RB, features), lambda i, spot: (i, 0)),
                 pl.BlockSpec(weights.shape, lambda i, spot: (0, 0, 0)),
                 pl.BlockSpec((1, width), lambda i, spot: (0, 0)),
+                lanes,
+                lanes,
             ],
             out_specs=(
-                pl.BlockSpec((QB, width), lambda i, spot: (i, 0)),
+                rows,
+                rows,
+                rows,
+                pl.BlockSpec((width // 3, RB), lambda i, spot: (0, i)),
                 pl.BlockSpec((features, width), lambda i, spot: (0, 0)),
+                pl.BlockSpec((1, PAIR), lambda i, spot: (0, 0)),
             ),
         ),
         cost_estimate=pl.CostEstimate(
-            flops=2 * length * features * width, transcendentals=0, bytes_accessed=2 * length * (features + width)
+            flops=2 * length * features * width, transcendentals=0, bytes_accessed=2 * length * (features + 3 * wide)
         ),
         compiler_params=pltpu.CompilerParams(dimension_semantics=("arbitrary",)),
-    )(spot, tokens, weights, bias)
+    )(spot, tokens, weights, bias, pattern, qpattern)
 
 
 def feed_forward_kernel(x_ref, up_ref, down_ref, bias_ref, act_ref, slope_ref, sum_ref):
@@ -303,8 +426,8 @@
 
     up = piece_rows(up_ref)
     down = piece_rows(down_ref)
-    for r in range(x_ref.shape[0] // QB):
-        rows = slice(r * QB, (r + 1) * QB)
+    for r in range(x_ref.shape[0] // RB):
+        rows = slice(r * RB, (r + 1) * RB)
         hidden = mm(x_ref[rows, :], up) + bias_ref[0]
         area = 0.5 * (1.0 + lax.erf(hidden * (2.0**-0.5)))
         activated = (hidden * area).astype(BF)
@@ -359,8 +482,8 @@
     up = piece_rows(up_ref)
     down = piece_rows(down_ref)
     total = jnp.zeros((1, act_ref.shape[1]), F32)
-    for r in range(x_ref.shape[0] // QB):
-        rows = slice(r * QB, (r + 1) * QB)
+    for r in range(x_ref.shape[0] // RB):
+        rows = slice(r * RB, (r + 1) * RB)
         grad_hidden = (mm(grad_ref[rows, :], down) * slope_ref[rows, :].astype(F32)).astype(BF)
         gh_ref[rows, :] = grad_hidden
         total = total + jnp.sum(grad_hidden.astype(F32), axis=0, keepdims=True)
@@ -514,6 +637,7 @@
         if tiled:
             gathered = jnp.stack([attention_pack, swap_chips(attention_pack)])
             for b in reversed(range(bits)):
+                before_last = gathered
                 gathered = jnp.concatenate([gathered, swap_bit(gathered, b)])
             spot = jnp.stack([depth, across]).astype(jnp.int32)
         else:
@@ -553,6 +677,8 @@
         spare = jnp.zeros((cut, 2 * PAIR - columns), BF)
         other_pack = jnp.concatenate([w_up, w_down.T, w_out.T, spare], axis=1)
         width = other_pack.shape[1]
+        if tiled:
+            other_pack, _ = lax.optimization_barrier((other_pack, before_last))
         others = lax.all_gather(other_pack, BOTH, axis=0).reshape(dp, 4, cut, width)
         if not tiled:
             others = others.transpose(1, 0, 2, 3).reshape(1, 4, dp * cut, width)
@@ -563,10 +689,10 @@
             swap_chips(mine_of(cotangent, 1 - across, 0).astype(BF)).astype(F32),
             0,
         ).reshape(2 * quarter, features)
-        lo, hi, bounds = segment_bounds(mine_of(segment_ids, across, 0))
-
-        qkv, w_qkv = project(tokens_full, gathered, bias_mine, spot)
-        heads_out, lse = attention_forward(qkv, lo, hi, bounds)
+        segments = segment_bounds(mine_of(segment_ids, across, 0))
+
+        *operands, w_qkv, limits = project(tokens_full, gathered, bias_mine, spot, *segments[3:])
+        heads_out, lse = attention_forward(operands, limits, segments)
 
         by_core = heads_out.reshape(2, 2, quarter, half)
         kept = mine_of(by_core, core, 1)
@@ -610,7 +736,7 @@
         got = swap_cores(mine_of(grad_context, 1 - core, 2))
         grad_heads = in_order(first_core, kept, got, 1).reshape(4 * quarter, half)
 
-        grad_qkv = attention_backward(qkv, grad_heads, heads_out, lse, lo, hi, bounds)
+        grad_qkv = attention_backward(operands, grad_heads, heads_out, lse, limits, segments)
         part = mm_nt(grad_qkv, w_qkv).reshape(2, 2, quarter, features)
         part_kept = mine_of(part, core, 1)
         part_got = swap_cores(mine_of(part, 1 - core, 1).astype(BF))

time: 535 us -> 496 us (0.927)
  Pallas kernels: 224 us -> 187 us
  local copies, waits for them, and re-layouts: 65.5 us -> 58.1 us
  waiting for transfers between devices: 116 us -> 123 us
    pallas_call x1, Pallas kernels: 81.2 us -> 59.2 us  [attention_forward(): pl.pallas_call(attention_forward_kernel, name='attention_forward', out_sh...]
    pallas_call x1, Pallas kernels: 79.4 us -> 62.5 us  [attention_backward(): pl.pallas_call(attention_backward_kernel, name='attention_backward', out_...]
    ppermute x8, waiting for transfers between devices: 24.5 us -> 36 us  [swap_chips(): return lax.ppermute(value, 'tensor', [(0, 2), (2, 0), (1, 3), (3, 1)])]
    ppermute x12, waiting for transfers between devices: 91.2 us -> 85.7 us  [swap_bit(): return lax.ppermute(value, 'dp', [(i, i ^ 1 << b) for i in range(dp)])]
    unnamed x49 -> x65, local copies, waits for them, and re-layouts: 19 us -> 18.4 us
  transfers between devices with their start and end apart: 28 -> 28, of which waited for: 11 -> 14; matrix products, arithmetic and copies ran while one was open for 18% -> 19% of each run, Pallas kernels for 33% -> 28%
where the time goes in v1:
time: 496 us; the launch traced here: 489 us
  Pallas kernels  187 us (38%)
  waiting for transfers between devices  123 us (25%)
  local copies, waits for them, and re-layouts  58.1 us (12%)
  other arithmetic  53.3 us (11%)
  starting transfers between devices  32 us (6%)
  matrix products  20.8 us (4%)
  between operations  15.4 us (3%)
    ppermute x12, waiting for transfers between devices, swap_bit(): return lax.ppermute(value, 'dp', [(i, i ^ 1 << b) for i in range(dp)])  85.7 us
    pallas_call x1, Pallas kernels, attention_backward(): pl.pallas_call(attention_backward_kernel, name='attention_backward', out_...  62.5 us
    pallas_call x1, Pallas kernels, attention_forward(): pl.pallas_call(attention_forward_kernel, name='attention_forward', out_sh...  59.2 us
    ppermute x8, waiting for transfers between devices, swap_chips(): return lax.ppermute(value, 'tensor', [(0, 2), (2, 0), (1, 3), (3, 1)])  36 us
    pallas_call x1, Pallas kernels, feed_forward_backward(): pl.pallas_call(feed_forward_backward_kernel, name='feed_forward_backward'...  28 us
    ppermute x12, starting transfers between devices, swap_bit(): return lax.ppermute(value, 'dp', [(i, i ^ 1 << b) for i in range(dp)])  21.1 us
    unnamed x65, local copies, waits for them, and re-layouts  18.4 us
    pallas_call x1, Pallas kernels, feed_forward(): pl.pallas_call(feed_forward_kernel, name='feed_forward', out_shape=(jax.S...  18.3 us
  transfers between devices with their start and end apart: 28, of which 14 were waited for; matrix products, arithmetic and copies ran while one was open for 19% of the time, Pallas kernels for 28%

profile of v1, /device:TPU:0, one launch (start us, length us, event | category | flops | bytes accessed | tf_op | source)
XLA Modules:
  0.0 489.2 jit_solution(7254062481985428069)
XLA Ops:
  8.9 3.0 collective-permute-start.2
  12.0 3.3 collective-permute-done.2
  15.3 2.9 collective-permute-start.3
  18.2 10.4 %collective-permute-done.3 = bf16[2,96,576]{2,1,0:T(8,128)(2,1)S(1)} collective-permute-done((bf16[2,96,576]{2,1,0:T(8,128)(2,1)S(1)}, bf16[2,96,576]{2,1,0:T(8,128)(2,1)S(1)}, u32[]{:S(2)}, u32[]{:S(2)}) %collective-permute-start.3) | collective-permute-done | bytes 221216 | tf_op jit(solution)/shard_map/ppermute | solution.py:625
  30.4 1.8 concatenate.31
  32.2 8.8 %collective-permute-done.4 = bf16[4,96,576]{2,1,0:T(8,128)(2,1)S(1)} collective-permute-done((bf16[4,96,576]{2,1,0:T(8,128)(2,1)S(1)}, bf16[4,96,576]{2,1,0:T(8,128)(2,1)S(1)}, u32[]{:S(2)}, u32[]{:S(2)}) %collective-permute-start.4) | collective-permute-done | bytes 442400 | tf_op jit(solution)/shard_map/ppermute | solution.py:625
  46.1 2.4 fusion.19
  52.3 14.2 %collective-permute-done.6 = bf16[1,384]{1,0:T(2,128)(2,1)S(1)} collective-permute-done((bf16[1,384]{1,0:T(2,128)(2,1)S(1)}, bf16[1,384]{1,0:T(2,128)(2,1)S(1)}, u32[]{:S(2)}, u32[]{:S(2)}) %collective-permute-start.6) | collective-permute-done | bytes 800 | tf_op jit(solution)/shard_map/ppermute | solution.py:619
  70.1 1.7 collective-permute-start.8
  73.8 3.3 collective-permute-start.9
  88.2 19.6 %collective-permute-done.5 = bf16[8,96,576]{2,1,0:T(8,128)(2,1)S(1)} collective-permute-done((bf16[8,96,576]{2,1,0:T(8,128)(2,1)}, bf16[8,96,576]{2,1,0:T(8,128)(2,1)S(1)}, u32[]{:S(2)}, u32[]{:S(2)}) %collective-permute-start.5) | collective-permute-done | bytes 884768 | tf_op jit(solution)/shard_map/ppermute | solution.py:625
  110.7 1.9 copy.165
  112.6 13.7 %project.1 = (bf16[2048,768]{1,0:T(8,128)(2,1)}, bf16[2048,768]{1,0:T(8,128)(2,1)}, bf16[2048,768]{1,0:T(8,128)(2,1)}, bf16[384,2048]{1,0:T(8,128)(2,1)}, bf16[768,1152]{1,0:T(8,128)(2,1)}, /*index=5*/f32[1,128]{1,0:T(1,128)}) custom-call(s32[2]{0:T(128)} %pad_add_fusion.1.spot_ref, bf16[2048,768]{1,0:T(8,128)(2,1)} %bitcast.269, ...), custom_call_target="tpu_custom_call" | custom-call | flops 3623878656 | bytes 12582912 | tf_op jit(solution)/shard_map/project/pallas_call | solution.py:385
  126.3 59.2 %attention_forward.1 = (bf16[2048,384]{1,0:T(8,128)(2,1)}, f32[2048,128]{1,0:T(8,128)}) custom-call(s32[4]{0:T(128)} %and_select_fusion.2.lo_ref, s32[4]{0:T(128)} %and_select_fusion.1.hi_ref, f32[1,128]{1,0:T(1,128)} %get-tuple-element.32.limit_ref, s32[4,2,512]{2,1,0:T(2,128)} %pad_add_fusion.bound_ref, bf16[2048,768]{1,0:T(8,128)(2,1)} %get-tuple-element.33.q_ref, ...), custom_call_target="tpu_custom_call" | custom-call | flops 6442450944 | bytes 11010048 | tf_op jit(solution)/shard_map/attention_forward/pallas_call | solution.py:207
  185.4 2.1 dynamic-slice_bitcast_fusion.1
  189.3 1.9 fusion.15
  191.2 2.0 multiply_reduce_fusion.3
  200.3 2.2 reshape.396
  202.5 3.8 fusion.43
  206.7 1.7 fusion.3.x_ref
  208.4 18.3 %feed_forward.1 = (bf16[1024,3072]{1,0:T(8,128)(2,1)}, bf16[1024,3072]{1,0:T(8,128)(2,1)}, f32[1024,768]{1,0:T(8,128)}) custom-call(bf16[1024,768]{1,0:T(8,128)(2,1)} %fusion.3.x_ref, bf16[8,4,96,1792]{3,2,1,0:T(8,128)(2,1)} %bitcast.292, bf16[8,4,96,1792]{3,2,1,0:T(8,128)(2,1)} %bitcast.293, f32[4,1,768]{2,1,0:T(1,128)} %reshape.443.bias_ref), custom_call_target="tpu_custom_call" | custom-call | flops 9663676416 | bytes 17301504 | tf_op jit(solution)/shard_map/feed_forward/pallas_call | solution.py:444
  226.7 2.9 fusion.42
  232.6 2.7 fusion.40
  235.3 1.8 copy-done.5
  238.4 28.0 %feed_forward_backward.1 = (bf16[8,4,96,1792]{3,2,1,0:T(8,128)(2,1)}, f32[1024,768]{1,0:T(8,128)}, f32[4,1,768]{2,1,0:T(1,128)}) custom-call(bf16[1024,768]{1,0:T(8,128)(2,1)} %convert_element_type.147.grad_ref, bf16[1024,768]{1,0:T(8,128)(2,1)} %fusion.3.x_ref, bf16[1024,3072]{1,0:T(8,128)(2,1)} %get-tuple-element.39.act_ref, ...), custom_call_target="tpu_custom_call" | custom-call | flops 19327352832 | bytes 40894464 | tf_op jit(solution)/shard_map/feed_forward_backward/pallas_call | solution.py:505
  266.4 3.8 multiply_reduce_fusion
  271.3 1.7 copy-done.2
  274.3 5.4 %output_gradient.1 = bf16[8,4,96,1792]{3,2,1,0:T(8,128)(2,1)} custom-call(bf16[1024,768]{1,0:T(8,128)(2,1)} %convert_element_type.148.grad_ref, bf16[1024,768]{1,0:T(8,128)(2,1)} %bitcast.259, bf16[8,4,96,1792]{3,2,1,0:T(8,128)(2,1)} %get-tuple-element.45._), custom_call_target="tpu_custom_call", output_to_operand_aliasing={{}: (2, {})} | custom-call | flops 1207959552 | bytes 3145728 | tf_op jit(solution)/shard_map/output_gradient/pallas_call | solution.py:564
  281.2 2.7 convolution_convert_fusion.1
  284.3 4.4 constant_dynamic-slice_fusion.10
  293.9 2.0 select_bitcast_fusion.3
  297.3 62.5 %attention_backward.1 = bf16[2048,1152]{1,0:T(8,128)(2,1)} custom-call(s32[4]{0:T(128)} %and_select_fusion.2.lo_ref, s32[4]{0:T(128)} %and_select_fusion.1.hi_ref, f32[1,128]{1,0:T(1,128)} %get-tuple-element.32.limit_ref, s32[4,2,512]{2,1,0:T(2,128)} %pad_add_fusion.bound_ref, f32[2048,128]{1,0:T(8,128)} %get-tuple-element.42.lse_ref, ...), custom_call_target="tpu_custom_call" | custom-call | flops 16106127360 | bytes 17301504 | tf_op jit(solution)/shard_map/attention_backward/pallas_call | solution.py:247
  359.8 3.2 convert_reduce_fusion
  363.9 7.9 %convolution_convert_fusion = bf16[768,1152]{1,0:T(8,128)(2,1)S(1)} fusion(bf16[2048,768]{1,0:T(8,128)(2,1)} %bitcast.270, bf16[2048,1152]{1,0:T(8,128)(2,1)} %attention_backward.1), kind=kOutput, calls=%fused_computation.1 | convolution fusion | flops 3624763392 | bytes 9633792 | tf_op jit(solution)/shard_map/dot_general | solution.py:322
  374.1 6.4 %fusion.49 = f32[2048,768]{1,0:T(8,128)} fusion(bf16[2048,1152]{1,0:T(8,128)(2,1)S(1)} %bitcast.264, bf16[768,1152]{1,0:T(8,128)(2,1)S(1)} %copy-done.22), kind=kOutput, calls=%fused_computation.198 | convolution fusion | flops 3623878656 | bytes 12779520 | tf_op jit(solution)/shard_map/dot_general | solution.py:318
  380.6 2.1 collective-permute-start.22
  382.7 3.7 fusion.9
  386.4 19.9 %collective-permute-done.22 = f32[4,2,384]{2,0,1:T(4,128)S(1)} collective-permute-done((f32[4,2,384]{2,0,1:T(4,128)S(1)}, f32[4,2,384]{2,0,1:T(4,128)S(1)}, u32[]{:S(2)}, u32[]{:S(2)}) %collective-permute-start.22) | collective-permute-done | bytes 12320 | tf_op jit(solution)/shard_map/ppermute | solution.py:625
  406.4 1.7 fusion.4
  408.2 2.0 collective-permute-start.18
  411.6 2.0 collective-permute-start.24
  413.7 9.2 %collective-permute-done.18 = bf16[2,96,1152]{2,1,0:T(8,128)(2,1)S(1)} collective-permute-done((bf16[2,96,1152]{2,1,0:T(8,128)(2,1)S(1)}, bf16[2,96,1152]{2,1,0:T(8,128)(2,1)S(1)}, u32[]{:S(2)}, u32[]{:S(2)}) %collective-permute-start.18) | collective-permute-done | bytes 442400 | tf_op jit(solution)/shard_map/ppermute | solution.py:625
  423.0 3.3 collective-permute-start.19
  427.3 1.9 pad_maximum_fusion.1
  430.0 13.2 %collective-permute-done.19 = bf16[1,96,1152]{2,1,0:T(8,128)(2,1)S(1)} collective-permute-done((bf16[1,96,1152]{2,1,0:T(8,128)(2,1)S(1)}, bf16[1,96,1152]{2,1,0:T(8,128)(2,1)S(1)}, u32[]{:S(2)}, u32[]{:S(2)}) %collective-permute-start.19) | collective-permute-done | bytes 221216 | tf_op jit(solution)/shard_map/ppermute | solution.py:625
  445.3 3.0 fusion.1
  455.0 17.7 %collective-permute-done.20 = bf16[96,576]{0,1:T(8,128)(2,1)S(1)} collective-permute-done((bf16[96,576]{0,1:T(8,128)(2,1)S(1)}, bf16[96,576]{0,1:T(8,128)(2,1)S(1)}, u32[]{:S(2)}, u32[]{:S(2)}) %collective-permute-start.20) | collective-permute-done | bytes 110624 | tf_op jit(solution)/shard_map/ppermute | solution.py:619
  477.5 2.0 pad_maximum_fusion.3
  (264 shorter events, 78.5 us)
Async XLA Ops:
  7.2 42.7 %copy-start = (s32[2,2048]{1,0:T(2,128)S(1)}, s32[2,2048]{1,0:T(2,128)}, u32[]{:S(2)}) copy-start(s32[2,2048]{1,0:T(2,128)} %param.19) | copy-start | bytes 49156
  7.2 190.6 %all-gather.3.cloned.1.call-start = ((), (), s32[]{:S(2)}) async-start(), calls=%async_computation.2 | async-start | bytes 11354112 | tf_op jit(solution)/shard_map/all_gather | solution.py:682
  8.8 36.0 %copy-start.13 = (bf16[12,8]{0,1:T(8,128)(2,1)S(1)}, bf16[12,8]{0,1:T(8,128)(2,1)}, u32[]{:S(2)}) copy-start(bf16[12,8]{0,1:T(8,128)(2,1)} %param.28) | copy-start | bytes 580
  8.8 36.2 %copy-start.20 = (bf16[3,8]{1,0:T(4,128)(2,1)S(1)}, bf16[3,8]{1,0:T(4,128)(2,1)}, u32[]{:S(2)}) copy-start(bf16[3,8]{1,0:T(4,128)(2,1)} %param.24) | copy-start | bytes 148
  8.8 36.3 %copy-start.21 = (bf16[3,8]{1,0:T(4,128)(2,1)S(1)}, bf16[3,8]{1,0:T(4,128)(2,1)}, u32[]{:S(2)}) copy-start(bf16[3,8]{1,0:T(4,128)(2,1)} %param.25) | copy-start | bytes 148
  8.9 36.4 %copy-start.14 = (bf16[24]{0:T(256)(128)(2,1)S(1)}, bf16[24]{0:T(256)(128)(2,1)}, u32[]{:S(2)}) copy-start(bf16[24]{0:T(256)(128)(2,1)} %param.29) | copy-start | bytes 148
  8.9 36.4 %copy-start.15 = (bf16[24]{0:T(256)(128)(2,1)S(1)}, bf16[24]{0:T(256)(128)(2,1)}, u32[]{:S(2)}) copy-start(bf16[24]{0:T(256)(128)(2,1)} %param.30) | copy-start | bytes 148
  8.9 36.4 %copy-start.16 = (bf16[24]{0:T(256)(128)(2,1)S(1)}, bf16[24]{0:T(256)(128)(2,1)}, u32[]{:S(2)}) copy-start(bf16[24]{0:T(256)(128)(2,1)} %param.31) | copy-start | bytes 148
  8.9 36.4 %copy-start.17 = (bf16[24]{0:T(256)(128)(2,1)S(1)}, bf16[24]{0:T(256)(128)(2,1)}, u32[]{:S(2)}) copy-start(bf16[24]{0:T(256)(128)(2,1)} %param.32) | copy-start | bytes 148
  8.9 36.4 %copy-start.18 = (bf16[24]{0:T(256)(128)(2,1)S(1)}, bf16[24]{0:T(256)(128)(2,1)}, u32[]{:S(2)}) copy-start(bf16[24]{0:T(256)(128)(2,1)} %param.33) | copy-start | bytes 148
  8.9 36.4 %copy-start.19 = (bf16[24]{0:T(256)(128)(2,1)S(1)}, bf16[24]{0:T(256)(128)(2,1)}, u32[]{:S(2)}) copy-start(bf16[24]{0:T(256)(128)(2,1)} %param.34) | copy-start | bytes 148
  8.9 6.4 %collective-permute-start.2 = (bf16[96,576]{1,0:T(8,128)(2,1)S(1)}, bf16[96,576]{1,0:T(8,128)(2,1)S(1)}, u32[]{:S(2)}, u32[]{:S(2)}) collective-permute-start(bf16[96,576]{1,0:T(8,128)(2,1)S(1)} %get-tuple-element.154), channel_id=1, source_target_pairs={{0,2},{2,0},{1,3},{3,1},{4,6},{6,4},{5,7},{7,5},{8,10},{10,8},{9,1... | collective-permute-start | bytes 331784 | tf_op jit(solution)/shard_map/ppermute | solution.py:619
  15.3 13.4 %collective-permute-start.3 = (bf16[2,96,576]{2,1,0:T(8,128)(2,1)S(1)}, bf16[2,96,576]{2,1,0:T(8,128)(2,1)S(1)}, u32[]{:S(2)}, u32[]{:S(2)}) collective-permute-start(bf16[2,96,576]{2,1,0:T(8,128)(2,1)S(1)} %pad_maximum_fusion.9), channel_id=1, source_target_pairs={{0,16},{4,20},{8,24},{12,28},{16,0},{20,4},{24,8},{28,12},{1,17},{... | collective-permute-start | bytes 663560 | tf_op jit(solution)/shard_map/ppermute | solution.py:625
  28.8 12.2 %collective-permute-start.4 = (bf16[4,96,576]{2,1,0:T(8,128)(2,1)S(1)}, bf16[4,96,576]{2,1,0:T(8,128)(2,1)S(1)}, u32[]{:S(2)}, u32[]{:S(2)}) collective-permute-start(bf16[4,96,576]{2,1,0:T(8,128)(2,1)S(1)} %pad_maximum_fusion.8), channel_id=1, source_target_pairs={{0,8},{4,12},{8,0},{12,4},{16,24},{20,28},{24,16},{28,20},{1,9},{5... | collective-permute-start | bytes 1327112 | tf_op jit(solution)/shard_map/ppermute | solution.py:625
  42.1 437.4 %reduce-scatter.2.cloned.1.call-start = ((), (), s32[]{:S(2)}) async-start(), calls=%async_computation.1 | async-start | bytes 11354112 | tf_op jit(solution)/shard_map/reduce_scatter | solution.py:732
  43.4 35.9 %collective-permute-start = (bf16[512,768]{1,0:T(8,128)(2,1)S(1)}, bf16[512,768]{1,0:T(8,128)(2,1)}, u32[]{:S(2)}, u32[]{:S(2)}) collective-permute-start(bf16[512,768]{1,0:T(8,128)(2,1)S(1)} %dynamic-slice_bitcast_fusion.2), channel_id=1, source_target_pairs={{0,2},{2,0},{1,3},{3,1},{4,6},{6,4},{5,7},{7,5},{8,10},{10,8},{9,1... | collective-permute-start | bytes 2359304 | tf_op jit(solution)/shard_map/ppermute | solution.py:619
  45.4 21.0 %collective-permute-start.6 = (bf16[1,384]{1,0:T(2,128)(2,1)S(1)}, bf16[1,384]{1,0:T(2,128)(2,1)S(1)}, u32[]{:S(2)}, u32[]{:S(2)}) collective-permute-start(bf16[1,384]{1,0:T(2,128)(2,1)S(1)} %reshape.388), channel_id=1, source_target_pairs={{0,2},{2,0},{1,3},{3,1},{4,6},{6,4},{5,7},{7,5},{8,10},{10,8},{9,1... | collective-permute-start | bytes 2312 | tf_op jit(solution)/shard_map/ppermute | solution.py:619
  48.5 140.8 %collective-permute-start.13 = (bf16[512,768]{1,0:T(8,128)(2,1)}, bf16[512,768]{1,0:T(8,128)(2,1)}, u32[]{:S(2)}, u32[]{:S(2)}) collective-permute-start(bf16[512,768]{1,0:T(8,128)(2,1)} %fusion.19), channel_id=1, source_target_pairs={{0,2},{2,0},{1,3},{3,1},{4,6},{6,4},{5,7},{7,5},{8,10},{10,8},{9,1... | collective-permute-start | bytes 2359304 | tf_op jit(solution)/shard_map/ppermute | solution.py:619
  66.4 3.6 collective-permute-start.7
  70.1 3.7 collective-permute-start.8
  73.8 5.4 %collective-permute-start.9 = (bf16[4,2,1,384]{3,1,0,2:T(2,128)(2,1)S(1)}, bf16[4,2,1,384]{3,1,0,2:T(2,128)(2,1)S(1)}, u32[]{:S(2)}, u32[]{:S(2)}) collective-permute-start(bf16[4,2,1,384]{3,1,0,2:T(2,128)(2,1)S(1)} %bitcast.305), channel_id=1, source_target_pairs={{0,16},{4,20},{8,24},{12,28},{16,0},{20,4},{24,8},{28,12},{1,17},{... | collective-permute-start | bytes 18440 | tf_op jit(solution)/shard_map/ppermute | solution.py:625
  82.1 26.7 %collective-permute-start.1 = (bf16[2,512,768]{2,1,0:T(8,128)(2,1)}, bf16[2,512,768]{2,1,0:T(8,128)(2,1)}, u32[]{:S(2)}, u32[]{:S(2)}) collective-permute-start(bf16[2,512,768]{2,1,0:T(8,128)(2,1)} %pad_maximum_fusion.4), channel_id=1, source_target_pairs={{0,1},{1,0},{2,3},{3,2},{4,5},{5,4},{6,7},{7,6},{8,9},{9,8},{10,11... | collective-permute-start | bytes 4718600 | tf_op jit(solution)/shard_map/ppermute | solution.py:622
  82.1 3.7 collective-permute-start.11
  83.6 24.2 %collective-permute-start.5 = (bf16[8,96,576]{2,1,0:T(8,128)(2,1)}, bf16[8,96,576]{2,1,0:T(8,128)(2,1)S(1)}, u32[]{:S(2)}, u32[]{:S(2)}) collective-permute-start(bf16[8,96,576]{2,1,0:T(8,128)(2,1)} %pad_maximum_fusion.7), channel_id=1, source_target_pairs={{0,4},{4,0},{8,12},{12,8},{16,20},{20,16},{24,28},{28,24},{1,5},{5... | collective-permute-start | bytes 2654216 | tf_op jit(solution)/shard_map/ppermute | solution.py:625
  187.6 5.6 %collective-permute-start.10 = (bf16[2,512,384]{2,1,0:T(8,128)(2,1)}, bf16[2,512,384]{2,1,0:T(8,128)(2,1)}, u32[]{:S(2)}, u32[]{:S(2)}) collective-permute-start(bf16[2,512,384]{2,1,0:T(8,128)(2,1)} %dynamic-slice_bitcast_fusion.1), channel_id=1, source_target_pairs={{0,1},{1,0},{2,3},{3,2},{4,5},{5,4},{6,7},{7,6},{8,9},{9,8},{10,11... | collective-permute-start | bytes 2359304 | tf_op jit(solution)/shard_map/ppermute | solution.py:622
  191.2 2.0 copy-start.10
  229.7 1.9 copy-start.4
  284.3 6.4 %copy-start.12 = (f32[4,1,768]{2,1,0:T(1,128)S(1)}, f32[4,1,768]{2,1,0:T(1,128)}, u32[]{:S(2)}) copy-start(f32[4,1,768]{2,1,0:T(1,128)} %get-tuple-element.46) | copy-start | bytes 36868
  288.7 4.2 copy-start.6
  289.7 4.1 collective-permute-start.14
  293.8 116.4 %collective-permute-start.12 = (bf16[512,768]{1,0:T(8,128)(2,1)}, bf16[512,768]{1,0:T(8,128)(2,1)}, u32[]{:S(2)}, u32[]{:S(2)}) collective-permute-start(bf16[512,768]{1,0:T(8,128)(2,1)} %fusion.18), channel_id=1, source_target_pairs={{0,2},{2,0},{1,3},{3,1},{4,6},{6,4},{5,7},{7,5},{8,10},{10,8},{9,1... | collective-permute-start | bytes 2359304 | tf_op jit(solution)/shard_map/ppermute | solution.py:619
  363.8 10.3 %slice-start = ((s8[4718592]{0:T(1024)(128)(4,1)}), s8[4194304]{0:T(1024)(128)(4,1)S(1)}, s32[]{:S(2)}) async-start(s8[4718592]{0:T(1024)(128)(4,1)} %bitcast.263), calls=%async_computation.3 | async-start | bytes 8388608
  363.8 10.2 %slice-start.1 = ((s8[4718592]{0:T(1024)(128)(4,1)}), s8[524288]{0:T(1024)(128)(4,1)S(1)}, s32[]{:S(2)}) async-start(s8[4718592]{0:T(1024)(128)(4,1)} %bitcast.263), calls=%async_computation.4 | async-start | bytes 1048576
  363.9 10.2 %copy-start.22 = (bf16[768,1152]{1,0:T(8,128)(2,1)S(1)}, bf16[768,1152]{1,0:T(8,128)(2,1)}, u32[]{:S(2)}) copy-start(bf16[768,1152]{1,0:T(8,128)(2,1)} %get-tuple-element.44) | copy-start | bytes 5308420
  363.9 16.6 %collective-permute-start.21 = (f32[8,2,384]{2,0,1:T(8,128)S(1)}, f32[8,2,384]{2,0,1:T(8,128)S(1)}, u32[]{:S(2)}, u32[]{:S(2)}) collective-permute-start(f32[8,2,384]{2,0,1:T(8,128)S(1)} %fusion.27), channel_id=1, source_target_pairs={{0,1},{1,0},{2,3},{3,2},{4,5},{5,4},{6,7},{7,6},{8,9},{9,8},{10,11... | collective-permute-start | bytes 73736 | tf_op jit(solution)/shard_map/ppermute | solution.py:622
  374.1 32.4 %collective-permute-start.17 = (bf16[4,96,1152]{2,1,0:T(8,128)(2,1)}, bf16[4,96,1152]{2,1,0:T(8,128)(2,1)}, u32[]{:S(2)}, u32[]{:S(2)}) collective-permute-start(bf16[4,96,1152]{2,1,0:T(8,128)(2,1)} %dynamic-slice_bitcast_fusion), channel_id=1, source_target_pairs={{0,4},{4,0},{8,12},{12,8},{16,20},{20,16},{24,28},{28,24},{1,5},{5... | collective-permute-start | bytes 2654216 | tf_op jit(solution)/shard_map/ppermute | solution.py:625
  380.6 25.7 %collective-permute-start.22 = (f32[4,2,384]{2,0,1:T(4,128)S(1)}, f32[4,2,384]{2,0,1:T(4,128)S(1)}, u32[]{:S(2)}, u32[]{:S(2)}) collective-permute-start(f32[4,2,384]{2,0,1:T(4,128)S(1)} %bitcast.308), channel_id=1, source_target_pairs={{0,4},{4,0},{8,12},{12,8},{16,20},{20,16},{24,28},{28,24},{1,5},{5... | collective-permute-start | bytes 36872 | tf_op jit(solution)/shard_map/ppermute | solution.py:625
  386.4 58.9 %collective-permute-start.15 = (bf16[2,512,768]{2,1,0:T(8,128)(2,1)}, bf16[2,512,768]{2,1,0:T(8,128)(2,1)}, u32[]{:S(2)}, u32[]{:S(2)}) collective-permute-start(bf16[2,512,768]{2,1,0:T(8,128)(2,1)} %fusion.9), channel_id=1, source_target_pairs={{0,1},{1,0},{2,3},{3,2},{4,5},{5,4},{6,7},{7,6},{8,9},{9,8},{10,11... | collective-permute-start | bytes 4718600 | tf_op jit(solution)/shard_map/ppermute | solution.py:622
  406.4 5.2 %collective-permute-start.23 = (f32[2,2,384]{2,0,1:T(2,128)S(1)}, f32[2,2,384]{2,0,1:T(2,128)S(1)}, u32[]{:S(2)}, u32[]{:S(2)}) collective-permute-start(f32[2,2,384]{2,0,1:T(2,128)S(1)} %bitcast.309), channel_id=1, source_target_pairs={{0,8},{4,12},{8,0},{12,4},{16,24},{20,28},{24,16},{28,20},{1,9},{5... | collective-permute-start | bytes 18440 | tf_op jit(solution)/shard_map/ppermute | solution.py:625
  408.2 14.7 %collective-permute-start.18 = (bf16[2,96,1152]{2,1,0:T(8,128)(2,1)S(1)}, bf16[2,96,1152]{2,1,0:T(8,128)(2,1)S(1)}, u32[]{:S(2)}, u32[]{:S(2)}) collective-permute-start(bf16[2,96,1152]{2,1,0:T(8,128)(2,1)S(1)} %dynamic-slice_bitcast_fusion.3), channel_id=1, source_target_pairs={{0,8},{4,12},{8,0},{12,4},{16,24},{20,28},{24,16},{28,20},{1,9},{5... | collective-permute-start | bytes 1327112 | tf_op jit(solution)/shard_map/ppermute | solution.py:625
  411.6 14.7 %collective-permute-start.24 = (f32[1,2,384]{2,0,1:T(1,128)S(1)}, f32[1,2,384]{2,0,1:T(1,128)S(1)}, u32[]{:S(2)}, u32[]{:S(2)}) collective-permute-start(f32[1,2,384]{2,0,1:T(1,128)S(1)} %constant_dynamic-slice_fusion.2), channel_id=1, source_target_pairs={{0,16},{4,20},{8,24},{12,28},{16,0},{20,4},{24,8},{28,12},{1,17},{... | collective-permute-start | bytes 9224 | tf_op jit(solution)/shard_map/ppermute | solution.py:625
  423.0 20.2 %collective-permute-start.19 = (bf16[1,96,1152]{2,1,0:T(8,128)(2,1)S(1)}, bf16[1,96,1152]{2,1,0:T(8,128)(2,1)S(1)}, u32[]{:S(2)}, u32[]{:S(2)}) collective-permute-start(bf16[1,96,1152]{2,1,0:T(8,128)(2,1)S(1)} %constant_dynamic-slice_fusion.8), channel_id=1, source_target_pairs={{0,16},{4,20},{8,24},{12,28},{16,0},{20,4},{24,8},{28,12},{1,17},{... | collective-permute-start | bytes 663560 | tf_op jit(solution)/shard_map/ppermute | solution.py:625
  426.4 3.7 collective-permute-start.25
  427.3 18.0 %copy-start.3 = (f32[1024,768]{1,0:T(8,128)S(1)}, f32[1024,768]{1,0:T(8,128)}, u32[]{:S(2)}) copy-start(f32[1024,768]{1,0:T(8,128)} %copy-done.2) | copy-start | bytes 9437188
  445.3 5.8 %copy-start.11 = (bf16[2,96,3,192]{1,3,2,0:T(8,128)(2,1)}, bf16[2,96,3,192]{1,3,2,0:T(8,128)(2,1)S(1)}, u32[]{:S(2)}) copy-start(bf16[2,96,3,192]{1,3,2,0:T(8,128)(2,1)S(1)} %copy.194) | copy-start | bytes 663556
  450.0 25.8 %collective-permute-start.16 = (bf16[512,768]{1,0:T(8,128)(2,1)S(1)}, bf16[512,768]{1,0:T(8,128)(2,1)S(1)}, u32[]{:S(2)}, u32[]{:S(2)}) collective-permute-start(bf16[512,768]{1,0:T(8,128)(2,1)S(1)} %fusion.20), channel_id=1, source_target_pairs={{0,2},{2,0},{1,3},{3,1},{4,6},{6,4},{5,7},{7,5},{8,10},{10,8},{9,1... | collective-permute-start | bytes 2359304 | tf_op jit(solution)/shard_map/ppermute | solution.py:619
  451.1 21.6 %collective-permute-start.20 = (bf16[96,576]{0,1:T(8,128)(2,1)S(1)}, bf16[96,576]{0,1:T(8,128)(2,1)S(1)}, u32[]{:S(2)}, u32[]{:S(2)}) collective-permute-start(bf16[96,576]{0,1:T(8,128)(2,1)S(1)} %dynamic-slice_bitcast_fusion.4), channel_id=1, source_target_pairs={{0,2},{2,0},{1,3},{3,1},{4,6},{6,4},{5,7},{7,5},{8,10},{10,8},{9,1... | collective-permute-start | bytes 331784 | tf_op jit(solution)/shard_map/ppermute | solution.py:619
  477.5 4.6 copy-start.1
  (5 other events, 7.8 us)
Sparse Core Ops, SparseCore 0:
  42.2 100.0 all-gather.2
  279.9 163.2 reduce-scatter.1

commit v2 on v1

--- a/solution.py
+++ b/solution.py
@@ -4,6 +4,7 @@
 from jax.experimental import pallas as pl
 from jax.experimental.pallas import tpu as pltpu
 from jax.sharding import PartitionSpec as P
+
 
 HD = 64
 PAIR = 2 * HD
@@ -15,7 +16,6 @@
 LIMIT = 50.0
 GAP = 256.0
 FREE = SEGS + 1
-EXTRA = 16
 EPS = 1e-12
 BF = jnp.bfloat16
 F32 = jnp.float32
@@ -575,6 +575,14 @@
         ),
         compiler_params=pltpu.CompilerParams(dimension_semantics=("arbitrary",)),
     )(grad, context, pack)
+
+
+def small_turns(bits):
+    return [0, bits] + list(reversed(range(1, bits)))
+
+
+def tiny_turns(bits):
+    return list(range(1, bits)) + [0, bits]
 
 
 def make_per_device(dp):
@@ -654,10 +662,15 @@
         lanes = -(-sum(sizes) // PAIR) * PAIR
         packed = jnp.concatenate([v.reshape(-1) for v in small])
         small_all = jnp.pad(packed, (0, lanes - packed.size)).reshape(1, lanes)
-        small_all = in_order(first_chip, small_all, swap_chips(small_all), 0)
-        for b in range(bits):
-            small_all = in_order(bit_of(b) == 0, small_all, swap_bit(small_all, b), 0)
-            small_all = small_all.reshape(2 << b, 2, 1, lanes)
+        turns = small_turns(bits)
+        for b in turns:
+            if b == bits:
+                small_all = in_order(first_chip, small_all, swap_chips(small_all), 0)
+            else:
+                small_all = in_order(bit_of(b) == 0, small_all, swap_bit(small_all, b), 0)
+        axes = turns[::-1]
+        where = [axes.index(b) for b in reversed(range(bits))] + [axes.index(bits)]
+        small_all = small_all.transpose(*where, bits + 1, bits + 2).reshape(dp, 2, 1, lanes)
         core_bias = small_all[:, :, 0, : sizes[0] + sizes[1]].reshape(dp, 2, 2, *b_query.shape).astype(F32)
         core_bias = core_bias.transpose(2, 1, 3, 0, 4).reshape(2, pairs, PAIR)
         bias_mine = jnp.stack([core_bias[0], jnp.zeros((pairs, PAIR), F32), core_bias[1]], axis=1).reshape(1, 3 * half)
@@ -683,10 +696,11 @@
         if not tiled:
             others = others.transpose(1, 0, 2, 3).reshape(1, 4, dp * cut, width)
 
+        cotangent_sent = mine_of(cotangent, 1 - across, 0).astype(BF)
         cotangent_own = in_order(
             first_chip,
             mine_of(cotangent, across, 0),
-            swap_chips(mine_of(cotangent, 1 - across, 0).astype(BF)).astype(F32),
+            swap_chips(cotangent_sent).astype(F32),
             0,
         ).reshape(2 * quarter, features)
         segments = segment_bounds(mine_of(segment_ids, across, 0))
@@ -753,7 +767,7 @@
         grad_w = (
             grad_w.reshape(cut, pairs, 3, PAIR).transpose(0, 2, 1, 3).reshape(cut, 3, 2, columns).transpose(2, 0, 1, 3)
         )
-        grad_w = halve(grad_w.reshape(2, cut, 3 * columns), across, swap_chips, 0, F32)
+        grad_w = halve(grad_w.reshape(2, cut, 3 * columns), across, lambda v: swap_chips(v), 0, F32)
 
         bias_grads = jnp.sum(grad_qkv.astype(F32), axis=0).reshape(pairs, 3, PAIR)
 
@@ -784,10 +798,15 @@
             axis=3,
         )
         small_grads = jnp.pad(small_grads, ((0, 0), (0, 0), (0, 0), (0, lanes - small_grads.shape[3])))
-        small_grads = halve(small_grads, core, swap_cores, 2, F32)
-        for b in range(bits):
-            small_grads = halve(small_grads.reshape(-1, 2, 2, lanes), bit_of(b), lambda v: swap_bit(v, b), 1, F32)
-        small_grads = halve(small_grads.reshape(2, lanes), across, swap_chips, 0, F32)
+        small_grads = halve(small_grads, core, lambda v: swap_cores(v), 2, F32)
+        small_grads = small_grads.reshape((2,) * (bits + 1) + (lanes,))
+        left = list(reversed(range(bits))) + [bits]
+        for b in tiny_turns(bits):
+            if b == bits:
+                small_grads = halve(small_grads, across, lambda v: swap_chips(v), left.index(b), F32)
+            else:
+                small_grads = halve(small_grads, bit_of(b), lambda v: swap_bit(v, b), left.index(b), F32)
+            left.remove(b)
 
         others_mine = others_mine.astype(F32)
         small_out = []
@@ -827,6 +846,7 @@
     in_specs += (vector,) * 6 + (rows,)
     out_specs = (rows, rows, split, split, split, turned, turned, turned, split, turned, turned)
     out_specs += (vector,) * 6
-    return jax.shard_map(
-        make_per_device(mesh.shape["dp"]), mesh=mesh, in_specs=in_specs, out_specs=out_specs, check_vma=False
-    )
+    dp = mesh.shape["dp"]
+    inner = make_per_device(dp)
+
+    return jax.shard_map(inner, mesh=mesh, in_specs=in_specs, out_specs=out_specs, check_vma=False)

time: 496 us -> 531 us (1.071)
  waiting for transfers between devices: 123 us -> 152 us
  starting transfers between devices: 32 us -> 40.1 us
    ppermute x8, waiting for transfers between devices: 36 us -> 54.5 us  [swap_chips(): return lax.ppermute(value, 'tensor', [(0, 2), (2, 0), (1, 3), (3, 1)])]
    ppermute x12, waiting for transfers between devices: 85.7 us -> 97.1 us  [swap_bit(): return lax.ppermute(value, 'dp', [(i, i ^ 1 << b) for i in range(dp)])]
    ppermute x12, starting transfers between devices: 21.1 us -> 29.8 us  [swap_bit(): return lax.ppermute(value, 'dp', [(i, i ^ 1 << b) for i in range(dp)])]
    unnamed x65 -> x68, local copies, waits for them, and re-layouts: 18.4 us -> 18.5 us
    another operation x22 -> x21, other arithmetic: 15.3 us -> 15.3 us  [in_order(): jnp.stack([jnp.where(flag, mine, other), jnp.where(flag, other, mine)], a...]
  transfers between devices with their start and end apart: 28 -> 28, of which waited for: 14 -> 12; matrix products, arithmetic and copies ran while one was open for 19% -> 18% of each run, Pallas kernels for 28% -> 25%
where the time goes in v2:
time: 531 us; the launch traced here: 521 us
  Pallas kernels  182 us (34%)
  waiting for transfers between devices  152 us (29%)
  local copies, waits for them, and re-layouts  59.3 us (11%)
  other arithmetic  51.5 us (10%)
  starting transfers between devices  40.1 us (8%)
  matrix products  20.7 us (4%)
  between operations  15.5 us (3%)
    ppermute x12, waiting for transfers between devices, swap_bit(): return lax.ppermute(value, 'dp', [(i, i ^ 1 << b) for i in range(dp)])  97.1 us
    pallas_call x1, Pallas kernels, attention_backward(): pl.pallas_call(attention_backward_kernel, name='attention_backward', out_...  60.2 us
    pallas_call x1, Pallas kernels, attention_forward(): pl.pallas_call(attention_forward_kernel, name='attention_forward', out_sh...  56.8 us
    ppermute x8, waiting for transfers between devices, swap_chips(): return lax.ppermute(value, 'tensor', [(0, 2), (2, 0), (1, 3), (3, 1)])  54.5 us
    ppermute x12, starting transfers between devices, swap_bit(): return lax.ppermute(value, 'dp', [(i, i ^ 1 << b) for i in range(dp)])  29.8 us
    pallas_call x1, Pallas kernels, feed_forward_backward(): pl.pallas_call(feed_forward_backward_kernel, name='feed_forward_backward'...  28 us
    unnamed x68, local copies, waits for them, and re-layouts  18.5 us
    pallas_call x1, Pallas kernels, feed_forward(): pl.pallas_call(feed_forward_kernel, name='feed_forward', out_shape=(jax.S...  18.2 us
  transfers between devices with their start and end apart: 28, of which 12 were waited for; matrix products, arithmetic and copies ran while one was open for 18% of the time, Pallas kernels for 25%

profile of v2, /device:TPU:0, one launch (start us, length us, event | category | flops | bytes accessed | tf_op | source)
XLA Modules:
  0.0 520.9 jit_solution(9156148808356872697)
XLA Ops:
  8.9 3.0 collective-permute-start.2
  12.0 3.3 collective-permute-done.2
  15.3 2.9 collective-permute-start.3
  18.2 10.4 %collective-permute-done.3 = bf16[2,96,576]{2,1,0:T(8,128)(2,1)S(1)} collective-permute-done((bf16[2,96,576]{2,1,0:T(8,128)(2,1)S(1)}, bf16[2,96,576]{2,1,0:T(8,128)(2,1)S(1)}, u32[]{:S(2)}, u32[]{:S(2)}) %collective-permute-start.3) | collective-permute-done | bytes 221216 | tf_op jit(solution)/shard_map/ppermute | solution.py:633
  30.4 1.8 concatenate.31
  32.2 8.8 %collective-permute-done.4 = bf16[4,96,576]{2,1,0:T(8,128)(2,1)S(1)} collective-permute-done((bf16[4,96,576]{2,1,0:T(8,128)(2,1)S(1)}, bf16[4,96,576]{2,1,0:T(8,128)(2,1)S(1)}, u32[]{:S(2)}, u32[]{:S(2)}) %collective-permute-start.4) | collective-permute-done | bytes 442400 | tf_op jit(solution)/shard_map/ppermute | solution.py:633
  46.0 2.4 fusion.19
  53.4 33.9 %collective-permute-done.7 = bf16[2,1,384]{2,0,1:T(2,128)(2,1)S(1)} collective-permute-done((bf16[2,1,384]{2,0,1:T(2,128)(2,1)S(1)}, bf16[2,1,384]{2,0,1:T(2,128)(2,1)S(1)}, u32[]{:S(2)}, u32[]{:S(2)}) %collective-permute-start.7) | collective-permute-done | bytes 1568 | tf_op jit(solution)/shard_map/ppermute | solution.py:627
  87.4 5.2 collective-permute-start.8
  94.3 1.8 collective-permute-start.9
  106.3 39.4 %collective-permute-done.5 = bf16[8,96,576]{2,1,0:T(8,128)(2,1)S(1)} collective-permute-done((bf16[8,96,576]{2,1,0:T(8,128)(2,1)S(1)}, bf16[8,96,576]{2,1,0:T(8,128)(2,1)S(1)}, u32[]{:S(2)}, u32[]{:S(2)}) %collective-permute-start.5) | collective-permute-done | bytes 884768 | tf_op jit(solution)/shard_map/ppermute | solution.py:633
  146.8 1.7 select_bitcast_fusion.1
  148.8 1.9 copy.215
  150.7 13.8 %project.1 = (bf16[2048,768]{1,0:T(8,128)(2,1)}, bf16[2048,768]{1,0:T(8,128)(2,1)}, bf16[2048,768]{1,0:T(8,128)(2,1)}, bf16[384,2048]{1,0:T(8,128)(2,1)}, bf16[768,1152]{1,0:T(8,128)(2,1)}, /*index=5*/f32[1,128]{1,0:T(1,128)}) custom-call(s32[2]{0:T(128)} %pad_add_fusion.1.spot_ref, bf16[2048,768]{1,0:T(8,128)(2,1)} %bitcast.271, ...), custom_call_target="tpu_custom_call" | custom-call | flops 3623878656 | bytes 12582912 | tf_op jit(solution)/shard_map/project/pallas_call | solution.py:385
  164.5 56.8 %attention_forward.1 = (bf16[2048,384]{1,0:T(8,128)(2,1)}, f32[2048,128]{1,0:T(8,128)}) custom-call(s32[4]{0:T(128)} %and_select_fusion.2.lo_ref, s32[4]{0:T(128)} %and_select_fusion.1.hi_ref, f32[1,128]{1,0:T(1,128)} %get-tuple-element.32.limit_ref, s32[4,2,512]{2,1,0:T(2,128)} %pad_add_fusion.bound_ref, bf16[2048,768]{1,0:T(8,128)(2,1)} %get-tuple-element.33.q_ref, ...), custom_call_target="tpu_custom_call" | custom-call | flops 6442450944 | bytes 11010048 | tf_op jit(solution)/shard_map/attention_forward/pallas_call | solution.py:207
  221.2 2.1 dynamic-slice_bitcast_fusion.1
  228.1 2.0 multiply_reduce_fusion.3
  237.3 2.1 reshape.379
  239.4 3.8 fusion.47
  245.4 18.2 %feed_forward.1 = (bf16[1024,3072]{1,0:T(8,128)(2,1)}, bf16[1024,3072]{1,0:T(8,128)(2,1)}, f32[1024,768]{1,0:T(8,128)}) custom-call(bf16[1024,768]{1,0:T(8,128)(2,1)} %fusion.3.x_ref, bf16[8,4,96,1792]{3,2,1,0:T(8,128)(2,1)} %bitcast.294, bf16[8,4,96,1792]{3,2,1,0:T(8,128)(2,1)} %bitcast.295, f32[4,1,768]{2,1,0:T(1,128)} %reshape.425.bias_ref), custom_call_target="tpu_custom_call" | custom-call | flops 9663676416 | bytes 17301504 | tf_op jit(solution)/shard_map/feed_forward/pallas_call | solution.py:444
  263.6 2.9 fusion.46
  269.4 2.7 fusion.44
  272.2 1.8 copy-done.5
  275.2 28.0 %feed_forward_backward.1 = (bf16[8,4,96,1792]{3,2,1,0:T(8,128)(2,1)}, f32[1024,768]{1,0:T(8,128)}, f32[4,1,768]{2,1,0:T(1,128)}) custom-call(bf16[1024,768]{1,0:T(8,128)(2,1)} %convert_element_type.147.grad_ref, bf16[1024,768]{1,0:T(8,128)(2,1)} %fusion.3.x_ref, bf16[1024,3072]{1,0:T(8,128)(2,1)} %get-tuple-element.39.act_ref, ...), custom_call_target="tpu_custom_call" | custom-call | flops 19327352832 | bytes 40894464 | tf_op jit(solution)/shard_map/feed_forward_backward/pallas_call | solution.py:505
  303.2 3.8 multiply_reduce_fusion
  308.2 1.7 copy-done.2
  311.2 5.4 %output_gradient.1 = bf16[8,4,96,1792]{3,2,1,0:T(8,128)(2,1)} custom-call(bf16[1024,768]{1,0:T(8,128)(2,1)} %convert_element_type.148.grad_ref, bf16[1024,768]{1,0:T(8,128)(2,1)} %bitcast.261, bf16[8,4,96,1792]{3,2,1,0:T(8,128)(2,1)} %get-tuple-element.45._), custom_call_target="tpu_custom_call", output_to_operand_aliasing={{}: (2, {})} | custom-call | flops 1207959552 | bytes 3145728 | tf_op jit(solution)/shard_map/output_gradient/pallas_call | solution.py:564
  318.1 2.7 convolution_convert_fusion.1
  321.2 4.4 constant_dynamic-slice_fusion.8
  330.7 2.0 select_bitcast_fusion.3
  334.2 60.2 %attention_backward.1 = bf16[2048,1152]{1,0:T(8,128)(2,1)} custom-call(s32[4]{0:T(128)} %and_select_fusion.2.lo_ref, s32[4]{0:T(128)} %and_select_fusion.1.hi_ref, f32[1,128]{1,0:T(1,128)} %get-tuple-element.32.limit_ref, s32[4,2,512]{2,1,0:T(2,128)} %pad_add_fusion.bound_ref, f32[2048,128]{1,0:T(8,128)} %get-tuple-element.42.lse_ref, ...), custom_call_target="tpu_custom_call" | custom-call | flops 16106127360 | bytes 17301504 | tf_op jit(solution)/shard_map/attention_backward/pallas_call | solution.py:247
  394.3 3.1 convert_reduce_fusion
  398.4 7.9 %convolution_convert_fusion = bf16[768,1152]{1,0:T(8,128)(2,1)S(1)} fusion(bf16[2048,768]{1,0:T(8,128)(2,1)} %bitcast.272, bf16[2048,1152]{1,0:T(8,128)(2,1)} %attention_backward.1), kind=kOutput, calls=%fused_computation.1 | convolution fusion | flops 3624763392 | bytes 9633792 | tf_op jit(solution)/shard_map/dot_general | solution.py:322
  408.5 4.2 collective-permute-start.17
  412.8 6.4 %fusion.53 = f32[2048,768]{1,0:T(8,128)} fusion(bf16[2048,1152]{1,0:T(8,128)(2,1)S(1)} %bitcast.266, bf16[768,1152]{1,0:T(8,128)(2,1)S(1)} %copy-done.24), kind=kOutput, calls=%fused_computation.200 | convolution fusion | flops 3623878656 | bytes 12779520 | tf_op jit(solution)/shard_map/dot_general | solution.py:318
  419.2 1.9 collective-permute-start.22
  421.1 3.2 fusion.9
  426.2 9.4 %collective-permute-done.17 = bf16[4,96,1152]{2,1,0:T(8,128)(2,1)} collective-permute-done((bf16[4,96,1152]{2,1,0:T(8,128)(2,1)}, bf16[4,96,1152]{2,1,0:T(8,128)(2,1)}, u32[]{:S(2)}, u32[]{:S(2)}) %collective-permute-start.17) | collective-permute-done | bytes 884768 | tf_op jit(solution)/shard_map/ppermute | solution.py:633
  437.1 2.5 collective-permute-start.18
  441.1 2.5 collective-permute-start.24
  443.6 14.8 %collective-permute-done.18 = bf16[2,96,1152]{2,1,0:T(8,128)(2,1)S(1)} collective-permute-done((bf16[2,96,1152]{2,1,0:T(8,128)(2,1)S(1)}, bf16[2,96,1152]{2,1,0:T(8,128)(2,1)S(1)}, u32[]{:S(2)}, u32[]{:S(2)}) %collective-permute-start.18) | collective-permute-done | bytes 442400 | tf_op jit(solution)/shard_map/ppermute | solution.py:633
  458.6 3.3 collective-permute-start.19
  462.0 1.9 pad_maximum_fusion.1
  465.6 11.6 %collective-permute-done.19 = bf16[1,96,1152]{2,1,0:T(8,128)(2,1)S(1)} collective-permute-done((bf16[1,96,1152]{2,1,0:T(8,128)(2,1)S(1)}, bf16[1,96,1152]{2,1,0:T(8,128)(2,1)S(1)}, u32[]{:S(2)}, u32[]{:S(2)}) %collective-permute-start.19) | collective-permute-done | bytes 221216 | tf_op jit(solution)/shard_map/ppermute | solution.py:633
  479.3 3.0 fusion.1
  484.1 2.1 collective-permute-start.20
  489.0 15.6 %collective-permute-done.20 = bf16[96,576]{0,1:T(8,128)(2,1)S(1)} collective-permute-done((bf16[96,576]{0,1:T(8,128)(2,1)S(1)}, bf16[96,576]{0,1:T(8,128)(2,1)S(1)}, u32[]{:S(2)}, u32[]{:S(2)}) %collective-permute-start.20) | collective-permute-done | bytes 110624 | tf_op jit(solution)/shard_map/ppermute | solution.py:627
  509.4 1.9 pad_maximum_fusion.3
  (268 shorter events, 79.2 us)
Async XLA Ops:
  7.2 41.8 %copy-start = (s32[2,2048]{1,0:T(2,128)S(1)}, s32[2,2048]{1,0:T(2,128)}, u32[]{:S(2)}) copy-start(s32[2,2048]{1,0:T(2,128)} %param.19) | copy-start | bytes 49156
  7.2 227.5 %all-gather.3.cloned.1.call-start = ((), (), s32[]{:S(2)}) async-start(), calls=%async_computation.2 | async-start | bytes 11354112 | tf_op jit(solution)/shard_map/all_gather | solution.py:695
  8.8 35.1 %copy-start.15 = (bf16[12,8]{0,1:T(8,128)(2,1)S(1)}, bf16[12,8]{0,1:T(8,128)(2,1)}, u32[]{:S(2)}) copy-start(bf16[12,8]{0,1:T(8,128)(2,1)} %param.28) | copy-start | bytes 580
  8.8 35.3 %copy-start.22 = (bf16[3,8]{1,0:T(4,128)(2,1)S(1)}, bf16[3,8]{1,0:T(4,128)(2,1)}, u32[]{:S(2)}) copy-start(bf16[3,8]{1,0:T(4,128)(2,1)} %param.24) | copy-start | bytes 148
  8.8 35.4 %copy-start.23 = (bf16[3,8]{1,0:T(4,128)(2,1)S(1)}, bf16[3,8]{1,0:T(4,128)(2,1)}, u32[]{:S(2)}) copy-start(bf16[3,8]{1,0:T(4,128)(2,1)} %param.25) | copy-start | bytes 148
  8.9 35.4 %copy-start.16 = (bf16[24]{0:T(256)(128)(2,1)S(1)}, bf16[24]{0:T(256)(128)(2,1)}, u32[]{:S(2)}) copy-start(bf16[24]{0:T(256)(128)(2,1)} %param.29) | copy-start | bytes 148
  8.9 35.4 %copy-start.17 = (bf16[24]{0:T(256)(128)(2,1)S(1)}, bf16[24]{0:T(256)(128)(2,1)}, u32[]{:S(2)}) copy-start(bf16[24]{0:T(256)(128)(2,1)} %param.30) | copy-start | bytes 148
  8.9 35.4 %copy-start.18 = (bf16[24]{0:T(256)(128)(2,1)S(1)}, bf16[24]{0:T(256)(128)(2,1)}, u32[]{:S(2)}) copy-start(bf16[24]{0:T(256)(128)(2,1)} %param.31) | copy-start | bytes 148
  8.9 35.4 %copy-start.19 = (bf16[24]{0:T(256)(128)(2,1)S(1)}, bf16[24]{0:T(256)(128)(2,1)}, u32[]{:S(2)}) copy-start(bf16[24]{0:T(256)(128)(2,1)} %param.32) | copy-start | bytes 148
  8.9 35.4 %copy-start.20 = (bf16[24]{0:T(256)(128)(2,1)S(1)}, bf16[24]{0:T(256)(128)(2,1)}, u32[]{:S(2)}) copy-start(bf16[24]{0:T(256)(128)(2,1)} %param.33) | copy-start | bytes 148
  8.9 35.4 %copy-start.21 = (bf16[24]{0:T(256)(128)(2,1)S(1)}, bf16[24]{0:T(256)(128)(2,1)}, u32[]{:S(2)}) copy-start(bf16[24]{0:T(256)(128)(2,1)} %param.34) | copy-start | bytes 148
  8.9 6.4 %collective-permute-start.2 = (bf16[96,576]{1,0:T(8,128)(2,1)S(1)}, bf16[96,576]{1,0:T(8,128)(2,1)S(1)}, u32[]{:S(2)}, u32[]{:S(2)}) collective-permute-start(bf16[96,576]{1,0:T(8,128)(2,1)S(1)} %get-tuple-element.171), channel_id=1, source_target_pairs={{0,2},{2,0},{1,3},{3,1},{4,6},{6,4},{5,7},{7,5},{8,10},{10,8},{9,1... | collective-permute-start | bytes 331784 | tf_op jit(solution)/shard_map/ppermute | solution.py:627
  15.3 13.4 %collective-permute-start.3 = (bf16[2,96,576]{2,1,0:T(8,128)(2,1)S(1)}, bf16[2,96,576]{2,1,0:T(8,128)(2,1)S(1)}, u32[]{:S(2)}, u32[]{:S(2)}) collective-permute-start(bf16[2,96,576]{2,1,0:T(8,128)(2,1)S(1)} %pad_maximum_fusion.9), channel_id=1, source_target_pairs={{0,16},{4,20},{8,24},{12,28},{16,0},{20,4},{24,8},{28,12},{1,17},{... | collective-permute-start | bytes 663560 | tf_op jit(solution)/shard_map/ppermute | solution.py:633
  28.8 12.2 %collective-permute-start.4 = (bf16[4,96,576]{2,1,0:T(8,128)(2,1)S(1)}, bf16[4,96,576]{2,1,0:T(8,128)(2,1)S(1)}, u32[]{:S(2)}, u32[]{:S(2)}) collective-permute-start(bf16[4,96,576]{2,1,0:T(8,128)(2,1)S(1)} %pad_maximum_fusion.8), channel_id=1, source_target_pairs={{0,8},{4,12},{8,0},{12,4},{16,24},{20,28},{24,16},{28,20},{1,9},{5... | collective-permute-start | bytes 1327112 | tf_op jit(solution)/shard_map/ppermute | solution.py:633
  41.2 470.1 %reduce-scatter.2.cloned.1.call-start = ((), (), s32[]{:S(2)}) async-start(), calls=%async_computation.1 | async-start | bytes 11354112 | tf_op jit(solution)/shard_map/reduce_scatter | solution.py:746
  42.4 55.8 %collective-permute-start = (bf16[512,768]{1,0:T(8,128)(2,1)S(1)}, bf16[512,768]{1,0:T(8,128)(2,1)}, u32[]{:S(2)}, u32[]{:S(2)}) collective-permute-start(bf16[512,768]{1,0:T(8,128)(2,1)S(1)} %dynamic-slice_bitcast_fusion.2), channel_id=1, source_target_pairs={{0,2},{2,0},{1,3},{3,1},{4,6},{6,4},{5,7},{7,5},{8,10},{10,8},{9,1... | collective-permute-start | bytes 2359304 | tf_op jit(solution)/shard_map/ppermute | solution.py:627
  44.5 6.9 %collective-permute-start.6 = (bf16[1,384]{1,0:T(2,128)(2,1)S(1)}, bf16[1,384]{1,0:T(2,128)(2,1)S(1)}, u32[]{:S(2)}, u32[]{:S(2)}) collective-permute-start(bf16[1,384]{1,0:T(2,128)(2,1)S(1)} %reshape.372), channel_id=1, source_target_pairs={{0,4},{4,0},{8,12},{12,8},{16,20},{20,16},{24,28},{28,24},{1,5},{5... | collective-permute-start | bytes 2312 | tf_op jit(solution)/shard_map/ppermute | solution.py:633
  48.4 178.2 %collective-permute-start.13 = (bf16[512,768]{1,0:T(8,128)(2,1)}, bf16[512,768]{1,0:T(8,128)(2,1)}, u32[]{:S(2)}, u32[]{:S(2)}) collective-permute-start(bf16[512,768]{1,0:T(8,128)(2,1)} %fusion.19), channel_id=1, source_target_pairs={{0,2},{2,0},{1,3},{3,1},{4,6},{6,4},{5,7},{7,5},{8,10},{10,8},{9,1... | collective-permute-start | bytes 2359304 | tf_op jit(solution)/shard_map/ppermute | solution.py:627
  51.4 36.0 %collective-permute-start.7 = (bf16[2,1,384]{2,0,1:T(2,128)(2,1)S(1)}, bf16[2,1,384]{2,0,1:T(2,128)(2,1)S(1)}, u32[]{:S(2)}, u32[]{:S(2)}) collective-permute-start(bf16[2,1,384]{2,0,1:T(2,128)(2,1)S(1)} %pad_maximum_fusion.15), channel_id=1, source_target_pairs={{0,2},{2,0},{1,3},{3,1},{4,6},{6,4},{5,7},{7,5},{8,10},{10,8},{9,1... | collective-permute-start | bytes 4616 | tf_op jit(solution)/shard_map/ppermute | solution.py:627
  87.4 6.9 %collective-permute-start.8 = (bf16[2,2,1,384]{3,1,0,2:T(2,128)(2,1)S(1)}, bf16[2,2,1,384]{3,1,0,2:T(2,128)(2,1)S(1)}, u32[]{:S(2)}, u32[]{:S(2)}) collective-permute-start(bf16[2,2,1,384]{3,1,0,2:T(2,128)(2,1)S(1)} %pad_maximum_fusion.14), channel_id=1, source_target_pairs={{0,16},{4,20},{8,24},{12,28},{16,0},{20,4},{24,8},{28,12},{1,17},{... | collective-permute-start | bytes 9224 | tf_op jit(solution)/shard_map/ppermute | solution.py:633
  94.3 3.8 collective-permute-start.9
  98.1 5.8 %collective-permute-start.11 = (bf16[8,2,1,384]{3,1,0,2:T(2,128)(2,1)S(1)}, bf16[8,2,1,384]{3,1,0,2:T(2,128)(2,1)S(1)}, u32[]{:S(2)}, u32[]{:S(2)}) collective-permute-start(bf16[8,2,1,384]{3,1,0,2:T(2,128)(2,1)S(1)} %bitcast.306), channel_id=1, source_target_pairs={{0,1},{1,0},{2,3},{3,2},{4,5},{5,4},{6,7},{7,6},{8,9},{9,8},{10,11... | collective-permute-start | bytes 36872 | tf_op jit(solution)/shard_map/ppermute | solution.py:630
  101.0 45.8 %collective-permute-start.1 = (bf16[2,512,768]{2,1,0:T(8,128)(2,1)}, bf16[2,512,768]{2,1,0:T(8,128)(2,1)}, u32[]{:S(2)}, u32[]{:S(2)}) collective-permute-start(bf16[2,512,768]{2,1,0:T(8,128)(2,1)} %pad_maximum_fusion.4), channel_id=1, source_target_pairs={{0,1},{1,0},{2,3},{3,2},{4,5},{5,4},{6,7},{7,6},{8,9},{9,8},{10,11... | collective-permute-start | bytes 4718600 | tf_op jit(solution)/shard_map/ppermute | solution.py:630
  102.4 43.3 %collective-permute-start.5 = (bf16[8,96,576]{2,1,0:T(8,128)(2,1)S(1)}, bf16[8,96,576]{2,1,0:T(8,128)(2,1)S(1)}, u32[]{:S(2)}, u32[]{:S(2)}) collective-permute-start(bf16[8,96,576]{2,1,0:T(8,128)(2,1)S(1)} %pad_maximum_fusion.7), channel_id=1, source_target_pairs={{0,4},{4,0},{8,12},{12,8},{16,20},{20,16},{24,28},{28,24},{1,5},{5... | collective-permute-start | bytes 2654216 | tf_op jit(solution)/shard_map/ppermute | solution.py:633
  164.5 62.2 %copy-start.11 = (f32[2,512,768]{2,1,0:T(8,128)S(1)}, f32[2,512,768]{2,1,0:T(8,128)}, u32[]{:S(2)}) copy-start(f32[2,512,768]{2,1,0:T(8,128)} %param.35) | copy-start | bytes 9437188
  223.4 6.8 %collective-permute-start.10 = (bf16[2,512,384]{2,1,0:T(8,128)(2,1)}, bf16[2,512,384]{2,1,0:T(8,128)(2,1)}, u32[]{:S(2)}, u32[]{:S(2)}) collective-permute-start(bf16[2,512,384]{2,1,0:T(8,128)(2,1)} %dynamic-slice_bitcast_fusion.1), channel_id=1, source_target_pairs={{0,1},{1,0},{2,3},{3,2},{4,5},{5,4},{6,7},{7,6},{8,9},{9,8},{10,11... | collective-permute-start | bytes 2359304 | tf_op jit(solution)/shard_map/ppermute | solution.py:630
  321.1 6.4 %copy-start.14 = (f32[4,1,768]{2,1,0:T(1,128)S(1)}, f32[4,1,768]{2,1,0:T(1,128)}, u32[]{:S(2)}) copy-start(f32[4,1,768]{2,1,0:T(1,128)} %get-tuple-element.46) | copy-start | bytes 36868
  325.5 4.2 copy-start.6
  326.6 4.1 collective-permute-start.14
  330.7 108.9 %collective-permute-start.12 = (bf16[512,768]{1,0:T(8,128)(2,1)}, bf16[512,768]{1,0:T(8,128)(2,1)}, u32[]{:S(2)}, u32[]{:S(2)}) collective-permute-start(bf16[512,768]{1,0:T(8,128)(2,1)} %fusion.18), channel_id=1, source_target_pairs={{0,2},{2,0},{1,3},{3,1},{4,6},{6,4},{5,7},{7,5},{8,10},{10,8},{9,1... | collective-permute-start | bytes 2359304 | tf_op jit(solution)/shard_map/ppermute | solution.py:627
  398.3 14.5 %slice-start = ((s8[4718592]{0:T(1024)(128)(4,1)}), s8[4194304]{0:T(1024)(128)(4,1)S(1)}, s32[]{:S(2)}) async-start(s8[4718592]{0:T(1024)(128)(4,1)} %bitcast.265), calls=%async_computation.3 | async-start | bytes 8388608
  398.3 14.5 %slice-start.1 = ((s8[4718592]{0:T(1024)(128)(4,1)}), s8[524288]{0:T(1024)(128)(4,1)S(1)}, s32[]{:S(2)}) async-start(s8[4718592]{0:T(1024)(128)(4,1)} %bitcast.265), calls=%async_computation.4 | async-start | bytes 1048576
  398.3 14.5 %copy-start.24 = (bf16[768,1152]{1,0:T(8,128)(2,1)S(1)}, bf16[768,1152]{1,0:T(8,128)(2,1)}, u32[]{:S(2)}) copy-start(bf16[768,1152]{1,0:T(8,128)(2,1)} %get-tuple-element.44) | copy-start | bytes 5308420
  398.3 20.8 %collective-permute-start.21 = (f32[8,2,384]{2,0,1:T(8,128)S(1)}, f32[8,2,384]{2,0,1:T(8,128)S(1)}, u32[]{:S(2)}, u32[]{:S(2)}) collective-permute-start(f32[8,2,384]{2,0,1:T(8,128)S(1)} %fusion.27), channel_id=1, source_target_pairs={{0,1},{1,0},{2,3},{3,2},{4,5},{5,4},{6,7},{7,6},{8,9},{9,8},{10,11... | collective-permute-start | bytes 73736 | tf_op jit(solution)/shard_map/ppermute | solution.py:630
  408.5 27.1 %collective-permute-start.17 = (bf16[4,96,1152]{2,1,0:T(8,128)(2,1)}, bf16[4,96,1152]{2,1,0:T(8,128)(2,1)}, u32[]{:S(2)}, u32[]{:S(2)}) collective-permute-start(bf16[4,96,1152]{2,1,0:T(8,128)(2,1)} %dynamic-slice_bitcast_fusion), channel_id=1, source_target_pairs={{0,4},{4,0},{8,12},{12,8},{16,20},{20,16},{24,28},{28,24},{1,5},{5... | collective-permute-start | bytes 2654216 | tf_op jit(solution)/shard_map/ppermute | solution.py:633
  419.2 16.5 %copy-start.10 = (bf16[768,1152]{1,0:T(8,128)(2,1)S(1)}, bf16[768,1152]{1,0:T(8,128)(2,1)}, u32[]{:S(2)}) copy-start(bf16[768,1152]{1,0:T(8,128)(2,1)} %copy-done.9) | copy-start | bytes 5308420
  419.2 5.4 %collective-permute-start.22 = (f32[2,2,2,384]{3,1,0,2:T(2,128)S(1)}, f32[2,2,2,384]{3,1,0,2:T(2,128)S(1)}, u32[]{:S(2)}, u32[]{:S(2)}) collective-permute-start(f32[2,2,2,384]{3,1,0,2:T(2,128)S(1)} %dynamic-slice_bitcast_fusion.5), channel_id=1, source_target_pairs={{0,8},{4,12},{8,0},{12,4},{16,24},{20,28},{24,16},{28,20},{1,9},{5... | collective-permute-start | bytes 36872 | tf_op jit(solution)/shard_map/ppermute | solution.py:633
  424.3 54.9 %collective-permute-start.15 = (bf16[2,512,768]{2,1,0:T(8,128)(2,1)}, bf16[2,512,768]{2,1,0:T(8,128)(2,1)}, u32[]{:S(2)}, u32[]{:S(2)}) collective-permute-start(bf16[2,512,768]{2,1,0:T(8,128)(2,1)} %fusion.9), channel_id=1, source_target_pairs={{0,1},{1,0},{2,3},{3,2},{4,5},{5,4},{6,7},{7,6},{8,9},{9,8},{10,11... | collective-permute-start | bytes 4718600 | tf_op jit(solution)/shard_map/ppermute | solution.py:630
  424.6 16.4 %collective-permute-start.23 = (f32[2,2,384]{2,0,1:T(2,128)S(1)}, f32[2,2,384]{2,0,1:T(2,128)S(1)}, u32[]{:S(2)}, u32[]{:S(2)}) collective-permute-start(f32[2,2,384]{2,0,1:T(2,128)S(1)} %fusion.32), channel_id=1, source_target_pairs={{0,16},{4,20},{8,24},{12,28},{16,0},{20,4},{24,8},{28,12},{1,17},{... | collective-permute-start | bytes 18440 | tf_op jit(solution)/shard_map/ppermute | solution.py:633
  437.1 21.4 %collective-permute-start.18 = (bf16[2,96,1152]{2,1,0:T(8,128)(2,1)S(1)}, bf16[2,96,1152]{2,1,0:T(8,128)(2,1)S(1)}, u32[]{:S(2)}, u32[]{:S(2)}) collective-permute-start(bf16[2,96,1152]{2,1,0:T(8,128)(2,1)S(1)} %dynamic-slice_bitcast_fusion.3), channel_id=1, source_target_pairs={{0,8},{4,12},{8,0},{12,4},{16,24},{20,28},{24,16},{28,20},{1,9},{5... | collective-permute-start | bytes 1327112 | tf_op jit(solution)/shard_map/ppermute | solution.py:633
  441.1 20.8 %collective-permute-start.24 = (f32[2,384]{1,0:T(2,128)S(1)}, f32[2,384]{1,0:T(2,128)S(1)}, u32[]{:S(2)}, u32[]{:S(2)}) collective-permute-start(f32[2,384]{1,0:T(2,128)S(1)} %bitcast.309), channel_id=1, source_target_pairs={{0,4},{4,0},{8,12},{12,8},{16,20},{20,16},{24,28},{28,24},{1,5},{5... | collective-permute-start | bytes 9224 | tf_op jit(solution)/shard_map/ppermute | solution.py:633
  458.6 18.6 %collective-permute-start.19 = (bf16[1,96,1152]{2,1,0:T(8,128)(2,1)S(1)}, bf16[1,96,1152]{2,1,0:T(8,128)(2,1)S(1)}, u32[]{:S(2)}, u32[]{:S(2)}) collective-permute-start(bf16[1,96,1152]{2,1,0:T(8,128)(2,1)S(1)} %constant_dynamic-slice_fusion.6), channel_id=1, source_target_pairs={{0,16},{4,20},{8,24},{12,28},{16,0},{20,4},{24,8},{28,12},{1,17},{... | collective-permute-start | bytes 663560 | tf_op jit(solution)/shard_map/ppermute | solution.py:633
  461.9 3.6 collective-permute-start.25
  462.0 17.3 %copy-start.3 = (f32[1024,768]{1,0:T(8,128)S(1)}, f32[1024,768]{1,0:T(8,128)}, u32[]{:S(2)}) copy-start(f32[1024,768]{1,0:T(8,128)} %copy-done.2) | copy-start | bytes 9437188
  479.3 4.8 copy-start.13
  484.0 23.7 %collective-permute-start.16 = (bf16[512,768]{1,0:T(8,128)(2,1)S(1)}, bf16[512,768]{1,0:T(8,128)(2,1)S(1)}, u32[]{:S(2)}, u32[]{:S(2)}) collective-permute-start(bf16[512,768]{1,0:T(8,128)(2,1)S(1)} %fusion.20), channel_id=1, source_target_pairs={{0,2},{2,0},{1,3},{3,1},{4,6},{6,4},{5,7},{7,5},{8,10},{10,8},{9,1... | collective-permute-start | bytes 2359304 | tf_op jit(solution)/shard_map/ppermute | solution.py:627
  484.1 20.4 %collective-permute-start.20 = (bf16[96,576]{0,1:T(8,128)(2,1)S(1)}, bf16[96,576]{0,1:T(8,128)(2,1)S(1)}, u32[]{:S(2)}, u32[]{:S(2)}) collective-permute-start(bf16[96,576]{0,1:T(8,128)(2,1)S(1)} %dynamic-slice_bitcast_fusion.4), channel_id=1, source_target_pairs={{0,2},{2,0},{1,3},{3,1},{4,6},{6,4},{5,7},{7,5},{8,10},{10,8},{9,1... | collective-permute-start | bytes 331784 | tf_op jit(solution)/shard_map/ppermute | solution.py:627
  509.4 4.5 copy-start.1
  (7 other events, 11.7 us)
Sparse Core Ops, SparseCore 0:
  41.3 120.0 all-gather.2
  316.8 163.6 reduce-scatter.1

commit v3 on v2

--- a/solution.py
+++ b/solution.py
@@ -46,7 +46,7 @@
 
 
 def attention_forward_kernel(
-    lo_ref, hi_ref, limit_ref, bound_ref, q_ref, key_ref, val_ref, o_ref, lse_ref, acc_ref, top_ref
+    lo_ref, hi_ref, spot_ref, limit_ref, bound_ref, q_ref, key_ref, val_ref, kept_ref, sent_ref, lse_ref, acc_ref, top_ref
 ):
     row = pl.program_id(0)
     heads = key_ref.shape[1] // PAIR
@@ -94,6 +94,7 @@
         lax.fori_loop(lo_ref[row], hi_ref[row], step, 0)
 
     lse = top_ref[...]
+    outs = []
     lane = lax.broadcasted_iota(jnp.int32, (QB, PAIR), 1)
     for p in range(heads // 2):
         both = []
@@ -103,13 +104,22 @@
             total = block[:, at : at + 1]
             both.append(block / total)
             lse = jnp.where(lane == h, lse + jnp.log(total), lse)
-        o_ref[:, p * PAIR : (p + 1) * PAIR] = jnp.where(lane < HD, both[0], both[1]).astype(BF)
+        outs.append(jnp.where(lane < HD, both[0], both[1]).astype(BF))
     lse_ref[...] = lse
+
+    def put(ref):
+        for p in range(heads // 2):
+            ref[0, :, p * PAIR : (p + 1) * PAIR] = outs[p]
+
+    stays = row % 2 == spot_ref[1]
+    pl.when(stays)(lambda: put(kept_ref))
+    pl.when(jnp.logical_not(stays))(lambda: put(sent_ref))
 
 
 def attention_backward_kernel(
     lo_ref,
     hi_ref,
+    spot_ref,
     limit_ref,
     bound_ref,
     lse_ref,
@@ -117,8 +127,10 @@
     key_ref,
     val_ref,
     kt_ref,
-    do_ref,
-    o_ref,
+    grad_kept_ref,
+    grad_got_ref,
+    kept_ref,
+    sent_ref,
     out_ref,
     dq_ref,
     dk_ref,
@@ -134,11 +146,12 @@
         dv_ref[...] = jnp.zeros_like(dv_ref)
 
     here = pl.ds(pl.multiple_of(row * QB, QB), QB)
+    stays = row % 2 == spot_ref[1]
     q_parts, g_parts, q_score, g_score = [], [], [], []
     for p in range(pairs):
         cols = slice(p * PAIR, (p + 1) * PAIR)
-        grad = do_ref[:, cols].astype(F32)
-        product = grad * o_ref[:, cols].astype(F32)
+        grad = jnp.where(stays, grad_kept_ref[0, :, cols].astype(F32), grad_got_ref[0, :, cols].astype(F32))
+        product = grad * jnp.where(stays, kept_ref[0, :, cols].astype(F32), sent_ref[0, :, cols].astype(F32))
         for h in (2 * p, 2 * p + 1):
             block = q_ref[:, h * PAIR : (h + 1) * PAIR].astype(F32)
             own = own_lanes(block.shape, h)
@@ -198,32 +211,35 @@
             out_ref[:, (3 * p + 2) * PAIR : (3 * p + 3) * PAIR] = dv_ref[:, cols].astype(BF)
 
 
-def attention_forward(operands, limits, segments):
+def attention_forward(operands, limits, segments, spot):
     queries, keys, values, _ = operands
     lo, hi, bounds = segments[:3]
     length, wide = keys.shape
     heads = wide // PAIR
-    whole = pl.BlockSpec((length, wide), lambda i, lo, hi: (0, 0))
+    assert length == 4 * QB
+    whole = pl.BlockSpec((length, wide), lambda i, *_: (0, 0))
     return pl.pallas_call(
         attention_forward_kernel,
         name="attention_forward",
         out_shape=(
-            jax.ShapeDtypeStruct((length, heads * HD), BF),
+            jax.ShapeDtypeStruct((2, QB, heads * HD), BF),
+            jax.ShapeDtypeStruct((2, QB, heads * HD), BF),
             jax.ShapeDtypeStruct((length, PAIR), F32),
         ),
         grid_spec=pltpu.PrefetchScalarGridSpec(
-            num_scalar_prefetch=2,
-            grid=(length // QB,),
+            num_scalar_prefetch=3,
+            grid=(4,),
             in_specs=[
                 pl.BlockSpec(memory_space=pltpu.SMEM),
-                pl.BlockSpec((1, 2, QB), lambda i, lo, hi: (i, 0, 0)),
-                pl.BlockSpec((QB, wide), lambda i, lo, hi: (i, 0)),
+                pl.BlockSpec((1, 2, QB), lambda i, *_: (i, 0, 0)),
+                pl.BlockSpec((QB, wide), lambda i, *_: (i, 0)),
                 whole,
                 whole,
             ],
             out_specs=(
-                pl.BlockSpec((QB, heads * HD), lambda i, lo, hi: (i, 0)),
-                pl.BlockSpec((QB, PAIR), lambda i, lo, hi: (i, 0)),
+                pl.BlockSpec((1, QB, heads * HD), lambda i, *_: (i // 2, 0, 0)),
+                pl.BlockSpec((1, QB, heads * HD), lambda i, *_: (i // 2, 0, 0)),
+                pl.BlockSpec((QB, PAIR), lambda i, *_: (i, 0)),
             ),
             scratch_shapes=[pltpu.VMEM((QB, wide), F32), pltpu.VMEM((QB, PAIR), F32)],
         ),
@@ -233,36 +249,39 @@
             bytes_accessed=keys.size * 7,
         ),
         compiler_params=pltpu.CompilerParams(dimension_semantics=("arbitrary",)),
-    )(lo, hi, limits, bounds, queries, keys, values)
-
-
-def attention_backward(operands, grad, out, lse, limits, segments):
+    )(lo, hi, spot, limits, bounds, queries, keys, values)
+
+
+def attention_backward(operands, grads, outs, lse, limits, segments, spot):
     queries, keys, values, turned = operands
     lo, hi, bounds = segments[:3]
     length, wide = keys.shape
     heads = wide // PAIR
     width = heads * HD
-    whole = pl.BlockSpec((length, wide), lambda i, lo, hi: (0, 0))
-    rows = pl.BlockSpec((QB, width), lambda i, lo, hi: (i, 0))
+    assert length == 4 * QB
+    whole = pl.BlockSpec((length, wide), lambda i, *_: (0, 0))
+    rows = pl.BlockSpec((1, QB, width), lambda i, *_: (i // 2, 0, 0))
     return pl.pallas_call(
         attention_backward_kernel,
         name="attention_backward",
         out_shape=jax.ShapeDtypeStruct((length, 3 * width), BF),
         grid_spec=pltpu.PrefetchScalarGridSpec(
-            num_scalar_prefetch=2,
-            grid=(length // QB,),
+            num_scalar_prefetch=3,
+            grid=(4,),
             in_specs=[
                 pl.BlockSpec(memory_space=pltpu.SMEM),
-                pl.BlockSpec((1, 2, QB), lambda i, lo, hi: (i, 0, 0)),
-                pl.BlockSpec((QB, PAIR), lambda i, lo, hi: (i, 0)),
-                pl.BlockSpec((QB, wide), lambda i, lo, hi: (i, 0)),
+                pl.BlockSpec((1, 2, QB), lambda i, *_: (i, 0, 0)),
+                pl.BlockSpec((QB, PAIR), lambda i, *_: (i, 0)),
+                pl.BlockSpec((QB, wide), lambda i, *_: (i, 0)),
                 whole,
                 whole,
-                pl.BlockSpec((width, length), lambda i, lo, hi: (0, 0)),
+                pl.BlockSpec((width, length), lambda i, *_: (0, 0)),
+                rows,
+                rows,
                 rows,
                 rows,
             ],
-            out_specs=pl.BlockSpec((length, 3 * width), lambda i, lo, hi: (0, 0)),
+            out_specs=pl.BlockSpec((length, 3 * width), lambda i, *_: (0, 0)),
             scratch_shapes=[
                 pltpu.VMEM((width, QB), F32),
                 pltpu.VMEM((length, width), F32),
@@ -275,7 +294,7 @@
             bytes_accessed=keys.size * 11,
         ),
         compiler_params=pltpu.CompilerParams(dimension_semantics=("arbitrary",)),
-    )(lo, hi, limits, bounds, lse, queries, keys, values, turned, grad, out)
+    )(lo, hi, spot, limits, bounds, lse, queries, keys, values, turned, *grads, *outs)
 
 
 def segment_bounds(segments):
@@ -419,28 +438,120 @@
     )(spot, tokens, weights, bias, pattern, qpattern)
 
 
-def feed_forward_kernel(x_ref, up_ref, down_ref, bias_ref, act_ref, slope_ref, sum_ref):
-    @pl.when(pl.program_id(0) == 0)
+CHUNK = 128
+
+
+def output_weights(piece_ref, spot_ref, w_ref):
+    columns = w_ref.shape[2] // 2
+    for k in range(2):
+        core = spot_ref[1] if k == 0 else 1 - spot_ref[1]
+        first = piece_ref[:, core].astype(F32)
+        second = piece_ref[:, 2 + core].astype(F32)
+        size = first.shape[0] * first.shape[1]
+        joined = [x.reshape(size, x.shape[2])[:, :columns] for x in (first, second)]
+        w_ref[k] = jnp.concatenate(joined, axis=1).astype(BF)
+
+
+def feed_forward_kernel(
+    spot_ref,
+    kept_ref,
+    got_ref,
+    tokens_ref,
+    cotangent_ref,
+    vector_ref,
+    out_w_ref,
+    up_ref,
+    down_ref,
+    bias_ref,
+    act_ref,
+    slope_ref,
+    hat_ref,
+    inverse_ref,
+    low_ref,
+    keep_ref,
+    send_ref,
+    grad_ref,
+    grad_low_ref,
+    total_ref,
+    sum_ref,
+    w_ref,
+):
+    part = pl.program_id(0)
+    length = low_ref.shape[0]
+    out_bias, gain1, shift1, down_bias, gain2, shift2 = [vector_ref[i : i + 1, :] for i in range(6)]
+
+    @pl.when(part == 0)
     def _():
+        output_weights(out_w_ref, spot_ref, w_ref)
         sum_ref[...] = jnp.zeros_like(sum_ref)
+        total_ref[...] = jnp.zeros_like(total_ref)
+
+        def one(r, carry):
+            rows = pl.ds(pl.multiple_of(r * CHUNK, CHUNK), CHUNK)
+            attended = mm_nt(kept_ref[rows, :], w_ref[0]) + mm_nt(got_ref[rows, :], w_ref[1])
+            hat, inverse = statistics(tokens_ref[rows, :].astype(F32) + attended + out_bias)
+            hat_ref[rows, :] = hat
+            inverse_ref[rows, :] = jnp.broadcast_to(inverse, (CHUNK, PAIR))
+            low_ref[rows, :] = (hat * gain1 + shift1).astype(BF)
+            return carry
+
+        lax.fori_loop(0, length // CHUNK, one, 0)
 
     up = piece_rows(up_ref)
     down = piece_rows(down_ref)
-    for r in range(x_ref.shape[0] // RB):
+    for r in range(length // RB):
         rows = slice(r * RB, (r + 1) * RB)
-        hidden = mm(x_ref[rows, :], up) + bias_ref[0]
+        hidden = mm(low_ref[rows, :], up) + bias_ref[0]
         area = 0.5 * (1.0 + lax.erf(hidden * (2.0**-0.5)))
         activated = (hidden * area).astype(BF)
         act_ref[rows, :] = activated
         slope_ref[rows, :] = (area + hidden * jnp.exp(-0.5 * hidden * hidden) * ((2.0 * jnp.pi) ** -0.5)).astype(BF)
         sum_ref[rows, :] += mm_nt(activated, down)
 
-
-def feed_forward(x, weights, bias):
-    length, features = x.shape
-    dp, parts, cut, _ = weights.shape
+    @pl.when(part == pl.num_programs(0) - 1)
+    def _():
+        per_chip = keep_ref.shape[0] // CHUNK
+
+        def one(r, carry):
+            rows = pl.ds(pl.multiple_of(r * CHUNK, CHUNK), CHUNK)
+            normed = hat_ref[rows, :] * gain1 + shift1
+            hat, inverse = statistics(normed + sum_ref[rows, :] + down_bias)
+            result = hat * gain2 + shift2
+            stays = r // per_chip == spot_ref[0]
+            there = pl.ds(pl.multiple_of(r % per_chip * CHUNK, CHUNK), CHUNK)
+
+            @pl.when(stays)
+            def _():
+                keep_ref[there, :] = result
+
+            @pl.when(jnp.logical_not(stays))
+            def _():
+                send_ref[there, :] = result.astype(BF)
+
+            cotangent = cotangent_ref[rows, :]
+            grad = norm_backward(cotangent, hat, inverse, gain2)
+            grad_ref[rows, :] = grad
+            grad_low_ref[rows, :] = grad.astype(BF)
+            for i, value in enumerate((grad, cotangent * hat, cotangent)):
+                total_ref[i : i + 1, :] += jnp.sum(value, axis=0, keepdims=True)
+            return carry
+
+        lax.fori_loop(0, length // CHUNK, one, 0)
+
+
+def once(shape, zeros):
+    return pl.BlockSpec(shape, lambda t, *_: zeros, pipeline_mode=pl.Buffered(1))
+
+
+def feed_forward(spot, kept, got, tokens, cotangent, vectors, weights, bias):
+    length, features = tokens.shape
+    dp, parts, cut, width = weights.shape
     units = bias.shape[-1]
+    half = kept.shape[1]
     piece = (dp, 1, cut, units)
+    rows = pl.BlockSpec((length, features), lambda t, *_: (0, 0))
+    chip = pl.BlockSpec((length // 2, features), lambda t, *_: (0, 0))
+    part = pl.BlockSpec((length, units), lambda t, *_: (0, t))
     return pl.pallas_call(
         feed_forward_kernel,
         name="feed_forward",
@@ -448,34 +559,76 @@
             jax.ShapeDtypeStruct((length, parts * units), BF),
             jax.ShapeDtypeStruct((length, parts * units), BF),
             jax.ShapeDtypeStruct((length, features), F32),
-        ),
-        grid=(parts,),
-        in_specs=[
-            pl.BlockSpec((length, features), lambda t: (0, 0)),
-            pl.BlockSpec(piece, lambda t: (0, t, 0, 0)),
-            pl.BlockSpec(piece, lambda t: (0, t, 0, 1)),
-            pl.BlockSpec((1, 1, units), lambda t: (t, 0, 0)),
-        ],
-        out_specs=(
-            pl.BlockSpec((length, units), lambda t: (0, t)),
-            pl.BlockSpec((length, units), lambda t: (0, t)),
-            pl.BlockSpec((length, features), lambda t: (0, 0)),
+            jax.ShapeDtypeStruct((length, PAIR), F32),
+            jax.ShapeDtypeStruct((length, features), BF),
+            jax.ShapeDtypeStruct((length // 2, features), F32),
+            jax.ShapeDtypeStruct((length // 2, features), BF),
+            jax.ShapeDtypeStruct((length, features), F32),
+            jax.ShapeDtypeStruct((length, features), BF),
+            jax.ShapeDtypeStruct((8, features), F32),
+        ),
+        grid_spec=pltpu.PrefetchScalarGridSpec(
+            num_scalar_prefetch=1,
+            grid=(parts,),
+            in_specs=[
+                once((length, half), (0, 0)),
+                once((length, half), (0, 0)),
+                once((length, features), (0, 0)),
+                once((length, features), (0, 0)),
+                once((8, features), (0, 0)),
+                once((dp, parts, cut, 2 * PAIR), (0, 0, 0, width // (2 * PAIR) - 1)),
+                pl.BlockSpec(piece, lambda t, *_: (0, t, 0, 0)),
+                pl.BlockSpec(piece, lambda t, *_: (0, t, 0, 1)),
+                pl.BlockSpec((1, 1, units), lambda t, *_: (t, 0, 0)),
+            ],
+            out_specs=(
+                part,
+                part,
+                rows,
+                pl.BlockSpec((length, PAIR), lambda t, *_: (0, 0)),
+                rows,
+                chip,
+                chip,
+                rows,
+                rows,
+                pl.BlockSpec((8, features), lambda t, *_: (0, 0)),
+            ),
+            scratch_shapes=[pltpu.VMEM((length, features), F32), pltpu.VMEM((2, features, half), BF)],
         ),
         cost_estimate=pl.CostEstimate(
             flops=4 * length * features * parts * units,
             transcendentals=2 * length * parts * units,
-            bytes_accessed=length * (parts * units * 4 + features * 6),
+            bytes_accessed=length * (parts * units * 4 + features * 24),
         ),
         compiler_params=pltpu.CompilerParams(dimension_semantics=("arbitrary",)),
-    )(x, weights, weights, bias)
+    )(spot, kept, got, tokens, cotangent, vectors, weights, weights, weights, bias)
 
 
 def feed_forward_backward_kernel(
-    grad_ref, x_ref, act_ref, slope_ref, up_ref, down_ref, pack_ref, back_ref, bias_ref, xt_ref, gt_ref, gh_ref
+    grad_ref,
+    x_ref,
+    act_ref,
+    slope_ref,
+    up_ref,
+    down_ref,
+    direct_ref,
+    hat_ref,
+    inverse_ref,
+    vector_ref,
+    pack_ref,
+    bias_ref,
+    summed_ref,
+    summed_low_ref,
+    total_ref,
+    back_ref,
+    xt_ref,
+    gt_ref,
+    gh_ref,
 ):
     @pl.when(pl.program_id(0) == 0)
     def _():
         back_ref[...] = jnp.zeros_like(back_ref)
+        total_ref[...] = jnp.zeros_like(total_ref)
         xt_ref[...] = x_ref[...].T
         gt_ref[...] = grad_ref[...].T
 
@@ -494,21 +647,39 @@
     pack_ref[:, 0, :, 0:units] = mm(xt_ref[...], gh_ref[...]).astype(BF).reshape(split)
     pack_ref[:, 0, :, units : 2 * units] = mm(gt_ref[...], act_ref[...]).astype(BF).reshape(split)
 
-
-def feed_forward_backward(grad, x, act, slope, weights):
+    @pl.when(pl.program_id(0) == pl.num_programs(0) - 1)
+    def _():
+        def one(r, carry):
+            rows = pl.ds(pl.multiple_of(r * CHUNK, CHUNK), CHUNK)
+            grad = direct_ref[rows, :] + back_ref[rows, :]
+            hat = hat_ref[rows, :]
+            summed = norm_backward(grad, hat, inverse_ref[rows, 0:1], vector_ref[1:2, :])
+            summed_ref[rows, :] = summed
+            summed_low_ref[rows, :] = summed.astype(BF)
+            for i, value in enumerate((summed, grad * hat, grad)):
+                total_ref[i : i + 1, :] += jnp.sum(value, axis=0, keepdims=True)
+            return carry
+
+        lax.fori_loop(0, x_ref.shape[0] // CHUNK, one, 0)
+
+
+def feed_forward_backward(grad, x, act, slope, weights, direct, hat, inverse, vectors):
     length, features = x.shape
     dp, parts, cut, width = weights.shape
     units = act.shape[1] // parts
     piece = (dp, 1, cut, units)
-    whole = pl.BlockSpec((length, features), lambda t: (0, 0))
+    whole = once((length, features), (0, 0))
+    rows = pl.BlockSpec((length, features), lambda t: (0, 0))
     part = pl.BlockSpec((length, units), lambda t: (0, t))
     return pl.pallas_call(
         feed_forward_backward_kernel,
         name="feed_forward_backward",
         out_shape=(
             jax.ShapeDtypeStruct((dp, parts, cut, width), BF),
+            jax.ShapeDtypeStruct((parts, 1, units), F32),
             jax.ShapeDtypeStruct((length, features), F32),
-            jax.ShapeDtypeStruct((parts, 1, units), F32),
+            jax.ShapeDtypeStruct((length, features), BF),
+            jax.ShapeDtypeStruct((8, features), F32),
         ),
         grid=(parts,),
         in_specs=[
@@ -518,13 +689,20 @@
             part,
             pl.BlockSpec(piece, lambda t: (0, t, 0, 0)),
             pl.BlockSpec(piece, lambda t: (0, t, 0, 1)),
+            whole,
+            whole,
+            once((length, PAIR), (0, 0)),
+            once((8, features), (0, 0)),
         ],
         out_specs=(
             pl.BlockSpec((dp, 1, cut, 2 * units), lambda t: (0, t, 0, 0)),
-            whole,
             pl.BlockSpec((1, 1, units), lambda t: (t, 0, 0)),
+            rows,
+            rows,
+            pl.BlockSpec((8, features), lambda t: (0, 0)),
         ),
         scratch_shapes=[
+            pltpu.VMEM((length, features), F32),
             pltpu.VMEM((features, length), BF),
             pltpu.VMEM((features, length), BF),
             pltpu.VMEM((length, units), BF),
@@ -532,49 +710,69 @@
         cost_estimate=pl.CostEstimate(
             flops=8 * length * features * parts * units,
             transcendentals=0,
-            bytes_accessed=length * (parts * units * 4 + features * 8) + dp * parts * cut * width * 4,
+            bytes_accessed=length * (parts * units * 4 + features * 18) + dp * parts * cut * width * 4,
         ),
         compiler_params=pltpu.CompilerParams(dimension_semantics=("arbitrary",)),
-    )(grad, x, act, slope, weights, weights)
-
-
-def output_gradient_kernel(grad_ref, context_ref, _, pack_ref, full_ref):
+    )(grad, x, act, slope, weights, weights, direct, hat, inverse, vectors)
+
+
+def output_gradient_kernel(
+    spot_ref, grad_ref, kept_ref, got_ref, out_w_ref, _, pack_ref, own_ref, other_ref, full_ref, w_ref
+):
     part = pl.program_id(0)
-    columns = context_ref.shape[1] // 4
+    columns = kept_ref.shape[1] // 2
 
     @pl.when(part == 0)
     def _():
-        full_ref[...] = mm(grad_ref[...].T, context_ref[...])
-
-    split = (pack_ref.shape[0], pack_ref.shape[2], pack_ref.shape[3])
-    for t in range(4):
-
-        @pl.when(part == t)
-        def _():
-            at = (t % 2 * 2 + t // 2) * columns
-            piece = full_ref[:, at : at + columns]
-            rest = jnp.zeros((piece.shape[0], split[2] - columns), F32)
-            pack_ref[:, 0] = jnp.concatenate([piece, rest], axis=1).astype(BF).reshape(split)
-
-
-def output_gradient(grad, context, pack):
+        turned = grad_ref[...].T
+        rest = jnp.zeros((turned.shape[0], 2 * PAIR - columns), F32)
+        for k, ref in enumerate((kept_ref, got_ref)):
+            result = mm(turned, ref[...])
+            for x in range(2):
+                piece = result[:, x * columns : (x + 1) * columns]
+                full_ref[2 * k + x] = jnp.concatenate([piece, rest], axis=1).astype(BF)
+        output_weights(out_w_ref, spot_ref, w_ref)
+        own_ref[...] = mm(grad_ref[...], w_ref[0]).astype(BF)
+        other_ref[...] = mm(grad_ref[...], w_ref[1]).astype(BF)
+
+    other = (part % 2 + spot_ref[1]) % 2
+    piece = full_ref[2 * other + part // 2]
+    pack_ref[:, 0] = piece.reshape(pack_ref.shape[0], pack_ref.shape[2], pack_ref.shape[3])
+
+
+def output_gradient(spot, grad, kept, got, weights, pack):
     length, features = grad.shape
     dp, parts, cut, width = pack.shape
-    whole = pl.BlockSpec((length, features), lambda t: (0, 0))
+    half = kept.shape[1]
+    last = width // (2 * PAIR) - 1
+    halves = pl.BlockSpec((length, half), lambda t, *_: (0, 0))
     return pl.pallas_call(
         output_gradient_kernel,
         name="output_gradient",
-        out_shape=jax.ShapeDtypeStruct(pack.shape, BF),
-        grid=(parts,),
-        in_specs=[whole, whole, pl.BlockSpec(memory_space=pl.ANY)],
-        out_specs=pl.BlockSpec((dp, 1, cut, PAIR * 2), lambda t: (0, t, 0, width // (PAIR * 2) - 1)),
-        scratch_shapes=[pltpu.VMEM((features, features), F32)],
-        input_output_aliases={2: 0},
+        out_shape=(
+            jax.ShapeDtypeStruct(pack.shape, BF),
+            jax.ShapeDtypeStruct((length, half), BF),
+            jax.ShapeDtypeStruct((length, half), BF),
+        ),
+        grid_spec=pltpu.PrefetchScalarGridSpec(
+            num_scalar_prefetch=1,
+            grid=(parts,),
+            in_specs=[
+                once((length, features), (0, 0)),
+                once((length, half), (0, 0)),
+                once((length, half), (0, 0)),
+                once((dp, parts, cut, 2 * PAIR), (0, 0, 0, last)),
+                pl.BlockSpec(memory_space=pl.ANY),
+            ],
+            out_specs=(pl.BlockSpec((dp, 1, cut, 2 * PAIR), lambda t, *_: (0, t, 0, last)), halves, halves),
+            scratch_shapes=[pltpu.VMEM((4, features, 2 * PAIR), BF), pltpu.VMEM((2, features, half), BF)],
+        ),
+        input_output_aliases={5: 0},
         cost_estimate=pl.CostEstimate(
-            flops=2 * length * features * features, transcendentals=0, bytes_accessed=length * features * 4
+            flops=4 * length * features * features, transcendentals=0, bytes_accessed=length * features * 8
         ),
         compiler_params=pltpu.CompilerParams(dimension_semantics=("arbitrary",)),
-    )(grad, context, pack)
+    )(spot, grad, kept, got, weights, pack)
 
 
 def small_turns(bits):
@@ -621,7 +819,6 @@
         first_core = core == 0
         first_chip = across == 0
         tiled = cut % 16 == 0
-        groups = (dp, cut) if tiled else (1, dp * cut)
 
         def swap_chips(value):
             return lax.ppermute(value, "tensor", [(0, 2), (2, 0), (1, 3), (3, 1)])
@@ -706,54 +903,39 @@
         segments = segment_bounds(mine_of(segment_ids, across, 0))
 
         *operands, w_qkv, limits = project(tokens_full, gathered, bias_mine, spot, *segments[3:])
-        heads_out, lse = attention_forward(operands, limits, segments)
-
-        by_core = heads_out.reshape(2, 2, quarter, half)
-        kept = mine_of(by_core, core, 1)
-        got = swap_cores(mine_of(by_core, 1 - core, 1))
-        context = in_order(first_core, kept, got, 2).reshape(2 * quarter, 2 * half)
-
-        w_out_t = (
-            others[..., 2 * units : 2 * units + columns]
-            .reshape(groups[0], 2, 2, groups[1], columns)
-            .transpose(0, 3, 2, 1, 4)
-            .reshape(features, features)
+        turn = jnp.stack([across, core]).astype(jnp.int32)
+        kept, sent, lse = attention_forward(operands, limits, segments, turn)
+
+        got = swap_cores(sent)
+        flat = (2 * quarter, half)
+        vectors = jnp.stack([out_bias, gain1, shift1, down_bias, gain2, shift2, out_bias, out_bias])
+        activated, slope, hat1, inverse1, normed_low, out_keep, out_send, grad_z, grad_branch, totals2 = feed_forward(
+            turn, kept.reshape(flat), got.reshape(flat), tokens_own, cotangent_own, vectors, others, bias_up
         )
-        summed = tokens_own.astype(F32) + mm_nt(context, w_out_t) + out_bias
-        hat1, inverse1 = statistics(summed)
-        normed = hat1 * gain1 + shift1
-        normed_low = normed.astype(BF)
-        activated, slope, branch = feed_forward(normed_low, others, bias_up)
-        hat2, inverse2 = statistics(normed + branch + down_bias)
-        out_own = (hat2 * gain2 + shift2).reshape(2, quarter, features)
+        layer_out = in_order(first_chip, out_keep, swap_chips(out_send).astype(F32), 0)
+
+        pack, grad_bias_up, grad_summed, grad_attended, totals1 = feed_forward_backward(
+            grad_branch, normed_low, activated, slope, others, grad_z, hat1, inverse1, vectors
+        )
+        pack, grad_kept, grad_sent = output_gradient(
+            turn, grad_attended, kept.reshape(flat), got.reshape(flat), others, pack
+        )
+        if not tiled:
+            pack = pack.reshape(4, dp, cut, width).transpose(1, 0, 2, 3)
+        others_mine = lax.psum_scatter(pack.reshape(4 * dp, cut, width), BOTH, scatter_dimension=0, tiled=False)
+
+        grad_got = swap_cores(grad_sent.reshape(2, quarter, half))
+        grads = (grad_kept.reshape(2, quarter, half), grad_got)
+        grad_qkv = attention_backward(operands, grads, (kept, sent), lse, limits, segments, turn)
+        part = mm_nt(grad_qkv, w_qkv).reshape(2, 2, quarter, features)
+        part_kept = mine_of(part, core, 1)
+        part_got = swap_cores(mine_of(part, 1 - core, 1).astype(BF))
 
         def send_back(value):
             kept_part = mine_of(value, across, 0)
             got_part = swap_chips(mine_of(value, 1 - across, 0).astype(BF)).astype(F32)
             return in_order(first_chip, kept_part, got_part, 0)
 
-        layer_out = send_back(out_own)
-
-        grad_z = norm_backward(cotangent_own, hat2, inverse2, gain2)
-        grad_branch = grad_z.astype(BF)
-        pack, back, grad_bias_up = feed_forward_backward(grad_branch, normed_low, activated, slope, others)
-        grad_normed = grad_z + back
-        grad_summed = norm_backward(grad_normed, hat1, inverse1, gain1)
-        grad_attended = grad_summed.astype(BF)
-        pack = output_gradient(grad_attended, context, pack)
-        if not tiled:
-            pack = pack.reshape(4, dp, cut, width).transpose(1, 0, 2, 3)
-        others_mine = lax.psum_scatter(pack.reshape(4 * dp, cut, width), BOTH, scatter_dimension=0, tiled=False)
-
-        grad_context = mm(grad_attended, w_out_t).astype(BF).reshape(2, quarter, 2, half)
-        kept = mine_of(grad_context, core, 2)
-        got = swap_cores(mine_of(grad_context, 1 - core, 2))
-        grad_heads = in_order(first_core, kept, got, 1).reshape(4 * quarter, half)
-
-        grad_qkv = attention_backward(operands, grad_heads, heads_out, lse, limits, segments)
-        part = mm_nt(grad_qkv, w_qkv).reshape(2, 2, quarter, features)
-        part_kept = mine_of(part, core, 1)
-        part_got = swap_cores(mine_of(part, 1 - core, 1).astype(BF))
         grad_tokens = send_back(grad_summed.reshape(2, quarter, features) + part_kept + part_got.astype(F32))
 
         def halve(value, flag, swap, axis, kind):
@@ -788,12 +970,12 @@
                 head_small(bias_grads[:, 0], b_query),
                 head_small(bias_grads[:, 2], b_value),
                 matrix_small(grad_bias_up, b_up),
-                vector_small(jnp.sum(grad_summed, axis=0)),
-                vector_small(jnp.sum(grad_normed * hat1, axis=0)),
-                vector_small(jnp.sum(grad_normed, axis=0)),
-                vector_small(jnp.sum(grad_z, axis=0)),
-                vector_small(jnp.sum(cotangent_own * hat2, axis=0)),
-                vector_small(jnp.sum(cotangent_own, axis=0)),
+                vector_small(totals1[0]),
+                vector_small(totals1[1]),
+                vector_small(totals1[2]),
+                vector_small(totals2[0]),
+                vector_small(totals2[1]),
+                vector_small(totals2[2]),
             ],
             axis=3,
         )

time: 531 us -> 510 us (0.960)
  Pallas kernels: 182 us -> 207 us
  local copies, waits for them, and re-layouts: 59.3 us -> 37.3 us
  other arithmetic: 51.5 us -> 34.2 us
  matrix products: 20.7 us -> 13 us
    reduce_sum x10 -> x0, other arithmetic: 16 us -> none  [the longest x1 3.79 us: per_device(): jnp.sum(grad_normed * hat1, axis=0)]
    pallas_call x1, Pallas kernels: 18.2 us -> 33.8 us  [feed_forward(): pl.pallas_call(feed_forward_kernel, name='feed_forward', out_shape=(jax.S...]
    ppermute x12, starting transfers between devices: 29.8 us -> 18.9 us  [swap_bit(): return lax.ppermute(value, 'dp', [(i, i ^ 1 << b) for i in range(dp)])]
    ppermute x8, starting transfers between devices: 8.82 us -> 18.4 us  [swap_chips(): return lax.ppermute(value, 'tensor', [(0, 2), (2, 0), (1, 3), (3, 1)])]
    unnamed x68 -> x67, local copies, waits for them, and re-layouts: 18.5 us -> 12.1 us
  transfers between devices with their start and end apart: 28 -> 28, of which waited for: 12 -> 11; matrix products, arithmetic and copies ran while one was open for 18% -> 15% of each run, Pallas kernels for 25% -> 26%
where the time goes in v3:
time: 510 us; the launch traced here: 500 us
  Pallas kernels  207 us (41%)
  waiting for transfers between devices  155 us (30%)
  starting transfers between devices  39 us (8%)
  local copies, waits for them, and re-layouts  37.3 us (7%)
  other arithmetic  34.2 us (7%)
  between operations  15.3 us (3%)
  matrix products  13 us (3%)
    ppermute x12, waiting for transfers between devices, swap_bit(): return lax.ppermute(value, 'dp', [(i, i ^ 1 << b) for i in range(dp)])  98.6 us
    pallas_call x1, Pallas kernels, attention_backward(): pl.pallas_call(attention_backward_kernel, name='attention_backward', out_...  60.9 us
    pallas_call x1, Pallas kernels, attention_forward(): pl.pallas_call(attention_forward_kernel, name='attention_forward', out_sh...  56.9 us
    ppermute x8, waiting for transfers between devices, swap_chips(): return lax.ppermute(value, 'tensor', [(0, 2), (2, 0), (1, 3), (3, 1)])  55.8 us
    pallas_call x1, Pallas kernels, feed_forward(): pl.pallas_call(feed_forward_kernel, name='feed_forward', out_shape=(jax.S...  33.8 us
    pallas_call x1, Pallas kernels, feed_forward_backward(): pl.pallas_call(feed_forward_backward_kernel, name='feed_forward_backward'...  32.7 us
    ppermute x12, starting transfers between devices, swap_bit(): return lax.ppermute(value, 'dp', [(i, i ^ 1 << b) for i in range(dp)])  18.9 us
    ppermute x8, starting transfers between devices, swap_chips(): return lax.ppermute(value, 'tensor', [(0, 2), (2, 0), (1, 3), (3, 1)])  18.4 us
  transfers between devices with their start and end apart: 28, of which 11 were waited for; matrix products, arithmetic and copies ran while one was open for 15% of the time, Pallas kernels for 26%

profile of v3, /device:TPU:0, one launch (start us, length us, event | category | flops | bytes accessed | tf_op | source)
XLA Modules:
  0.0 500.3 jit_solution(13400422589556235869)
XLA Ops:
  7.3 1.7 constant_dynamic-update-slice_fusion.4
  8.9 3.0 collective-permute-start.2
  11.9 3.3 collective-permute-done.2
  15.4 2.9 collective-permute-start.3
  18.3 10.4 %collective-permute-done.3 = bf16[2,96,576]{2,1,0:T(8,128)(2,1)S(1)} collective-permute-done((bf16[2,96,576]{2,1,0:T(8,128)(2,1)S(1)}, bf16[2,96,576]{2,1,0:T(8,128)(2,1)S(1)}, u32[]{:S(2)}, u32[]{:S(2)}) %collective-permute-start.3) | collective-permute-done | bytes 221216 | tf_op jit(solution)/shard_map/ppermute | solution.py:830
  31.3 9.8 %collective-permute-done.4 = bf16[4,96,576]{2,1,0:T(8,128)(2,1)S(1)} collective-permute-done((bf16[4,96,576]{2,1,0:T(8,128)(2,1)S(1)}, bf16[4,96,576]{2,1,0:T(8,128)(2,1)S(1)}, u32[]{:S(2)}, u32[]{:S(2)}) %collective-permute-start.4) | collective-permute-done | bytes 442400 | tf_op jit(solution)/shard_map/ppermute | solution.py:830
  42.8 1.5 collective-permute-start.6
  44.4 1.6 collective-permute-start
  45.9 2.4 fusion.13
  49.9 1.3 fusion.10
  51.8 1.6 collective-permute-start.7
  54.0 36.1 %collective-permute-done.7 = bf16[2,1,384]{2,0,1:T(2,128)(2,1)S(1)} collective-permute-done((bf16[2,1,384]{2,0,1:T(2,128)(2,1)S(1)}, bf16[2,1,384]{2,0,1:T(2,128)(2,1)S(1)}, u32[]{:S(2)}, u32[]{:S(2)}) %collective-permute-start.7) | collective-permute-done | bytes 1568 | tf_op jit(solution)/shard_map/ppermute | solution.py:824
  90.1 5.2 %collective-permute-start.8 = (bf16[2,2,1,384]{3,1,0,2:T(2,128)(2,1)S(1)}, bf16[2,2,1,384]{3,1,0,2:T(2,128)(2,1)S(1)}, u32[]{:S(2)}, u32[]{:S(2)}) collective-permute-start(bf16[2,2,1,384]{3,1,0,2:T(2,128)(2,1)S(1)} %fusion.36), channel_id=1, source_target_pairs={{0,16},{4,20},{8,24},{12,28},{16,0},{20,4},{24,8},{28,12},{1,17},{... | collective-permute-start | bytes 9224 | tf_op jit(solution)/shard_map/ppermute | solution.py:830
  97.0 1.8 collective-permute-start.9
  99.4 1.5 collective-permute-done.9
  103.8 1.4 fusion.39
  110.8 1.9 constant_dynamic-update-slice_fusion.1
  112.7 36.0 %collective-permute-done.5 = bf16[8,96,576]{2,1,0:T(8,128)(2,1)} collective-permute-done((bf16[8,96,576]{2,1,0:T(8,128)(2,1)}, bf16[8,96,576]{2,1,0:T(8,128)(2,1)}, u32[]{:S(2)}, u32[]{:S(2)}) %collective-permute-start.5) | collective-permute-done | bytes 884768 | tf_op jit(solution)/shard_map/ppermute | solution.py:830
  148.7 2.3 constant_dynamic-update-slice_fusion.weights_ref
  151.0 1.6 select_bitcast_fusion.1
  152.9 1.9 copy.218
  154.8 13.8 %project.1 = (bf16[2048,768]{1,0:T(8,128)(2,1)}, bf16[2048,768]{1,0:T(8,128)(2,1)}, bf16[2048,768]{1,0:T(8,128)(2,1)}, bf16[384,2048]{1,0:T(8,128)(2,1)}, bf16[768,1152]{1,0:T(8,128)(2,1)}, /*index=5*/f32[1,128]{1,0:T(1,128)}) custom-call(s32[2]{0:T(128)} %pad_add_fusion.2.spot_ref, bf16[2048,768]{1,0:T(8,128)(2,1)} %bitcast.226, ...), custom_call_target="tpu_custom_call" | custom-call | flops 3623878656 | bytes 12582912 | tf_op jit(solution)/shard_map/project/pallas_call | solution.py:404
  168.5 56.9 %attention_forward.1 = (bf16[2,512,384]{2,1,0:T(8,128)(2,1)}, bf16[2,512,384]{2,1,0:T(8,128)(2,1)}, f32[2048,128]{1,0:T(8,128)}) custom-call(s32[4]{0:T(128)} %and_select_fusion.2.lo_ref, s32[4]{0:T(128)} %and_select_fusion.1.hi_ref, s32[2]{0:T(128)} %pad_add_fusion.1.spot_ref, f32[1,128]{1,0:T(1,128)} %get-tuple-element.45.limit_ref, ...), custom_call_target="tpu_custom_call" | custom-call | flops 6442450944 | bytes 11010048 | tf_op jit(solution)/shard_map/attention_forward/pallas_call | solution.py:221
  227.8 1.9 fusion.2
  229.7 1.9 pad_maximum_fusion.1
  232.5 33.8 %feed_forward.1 = (bf16[1024,3072]{1,0:T(8,128)(2,1)}, bf16[1024,3072]{1,0:T(8,128)(2,1)}, f32[1024,768]{1,0:T(8,128)}, f32[1024,128]{1,0:T(8,128)}, bf16[1024,7...) custom-call(s32[2]{0:T(128)} %pad_add_fusion.1.spot_ref, ...), custom_call_target="tpu_custom_call" | custom-call | flops 9663676416 | bytes 31457280 | tf_op jit(solution)/shard_map/feed_forward/pallas_call | solution.py:555
  266.3 32.7 %feed_forward_backward.1 = (bf16[8,4,96,1792]{3,2,1,0:T(8,128)(2,1)}, f32[4,1,768]{2,1,0:T(1,128)}, f32[1024,768]{1,0:T(8,128)}, bf16[1024,768]{1,0:T(8,128)(2,1)}, f32[8,768]{1,0:T(8,128)}) custom-call(bf16[1024,768]{1,0:T(8,128)(2,1)} %get-tuple-element.54.grad_ref, bf16[1024,768]{1,0:T(8,128)(2,1)} %get-tuple-element.55.x_ref, ...), custom_call_target="tpu_custom_call" | custom-call | flops 19327352832 | bytes 48758784 | tf_op jit(solution)/shard_map/feed_forward_backward/pallas_call | solution.py:674
  299.0 9.0 %output_gradient.1 = (bf16[8,4,96,1792]{3,2,1,0:T(8,128)(2,1)}, bf16[1024,384]{1,0:T(8,128)(2,1)}, bf16[1024,384]{1,0:T(8,128)(2,1)}) custom-call(s32[2]{0:T(128)} %pad_add_fusion.1.spot_ref, bf16[1024,768]{1,0:T(8,128)(2,1)} %get-tuple-element.64.grad_ref, bf16[1024,384]{1,0:T(8,128)(2,1)} %bitcast.223, ...), custom_call_target="tpu_custom_call", output_to_operand_aliasing={{0}: (5, {})} | custom-call | flops 2415919104 | bytes 6291456 | tf_op jit(solution)/shard_map/output_gradient/pallas_call | solution.py:749
  313.4 60.9 %attention_backward.1 = bf16[2048,1152]{1,0:T(8,128)(2,1)} custom-call(s32[4]{0:T(128)} %and_select_fusion.2.lo_ref, s32[4]{0:T(128)} %and_select_fusion.1.hi_ref, s32[2]{0:T(128)} %pad_add_fusion.1.spot_ref, f32[1,128]{1,0:T(1,128)} %get-tuple-element.45.limit_ref, s32[4,2,512]{2,1,0:T(2,128)} %pad_add_fusion.bound_ref, ...), custom_call_target="tpu_custom_call" | custom-call | flops 16106127360 | bytes 17301504 | tf_op jit(solution)/shard_map/attention_backward/pallas_call | solution.py:264
  374.3 3.2 convert_reduce_fusion
  378.4 6.9 %convolution_convert_fusion = bf16[768,1152]{1,0:T(8,128)(2,1)S(1)} fusion(bf16[2048,768]{1,0:T(8,128)(2,1)S(1)} %bitcast.227, bf16[2048,1152]{1,0:T(8,128)(2,1)} %attention_backward.1), kind=kOutput, calls=%fused_computation.1 | convolution fusion | flops 3624763392 | bytes 9633792 | tf_op jit(solution)/shard_map/dot_general | solution.py:341
  387.5 2.1 collective-permute-start.17
  389.6 6.2 %fusion.43 = f32[2048,768]{1,0:T(8,128)} fusion(bf16[2048,1152]{1,0:T(8,128)(2,1)S(1)} %bitcast.217, bf16[768,1152]{1,0:T(8,128)(2,1)S(1)} %copy-done.25), kind=kOutput, calls=%fused_computation.154 | convolution fusion | flops 3623878656 | bytes 12779520 | tf_op jit(solution)/shard_map/dot_general | solution.py:337
  395.9 1.9 collective-permute-start.22
  397.8 2.0 fusion.8
  400.3 1.7 collective-permute-start.23
  402.0 16.1 %collective-permute-done.17 = bf16[4,96,1152]{2,1,0:T(8,128)(2,1)} collective-permute-done((bf16[4,96,1152]{2,1,0:T(8,128)(2,1)}, bf16[4,96,1152]{2,1,0:T(8,128)(2,1)}, u32[]{:S(2)}, u32[]{:S(2)}) %collective-permute-start.17) | collective-permute-done | bytes 884768 | tf_op jit(solution)/shard_map/ppermute | solution.py:830
  418.1 1.4 fusion.1
  419.8 1.4 fusion.4
  422.0 20.6 %collective-permute-done.18 = bf16[2,96,1152]{2,1,0:T(8,128)(2,1)S(1)} collective-permute-done((bf16[2,96,1152]{2,1,0:T(8,128)(2,1)S(1)}, bf16[2,96,1152]{2,1,0:T(8,128)(2,1)S(1)}, u32[]{:S(2)}, u32[]{:S(2)}) %collective-permute-start.18) | collective-permute-done | bytes 442400 | tf_op jit(solution)/shard_map/ppermute | solution.py:830
  442.9 8.2 %collective-permute-start.25 = (f32[384]{0:T(512)S(1)}, f32[384]{0:T(512)S(1)}, u32[]{:S(2)}, u32[]{:S(2)}) collective-permute-start(f32[384]{0:T(512)S(1)} %get-tuple-element.183), channel_id=1, source_target_pairs={{0,2},{2,0},{1,3},{3,1},{4,6},{6,4},{5,7},{7,5},{8,10},{10,8},{9,1... | collective-permute-start | bytes 4616 | tf_op jit(solution)/shard_map/ppermute | solution.py:824
  451.2 1.9 pad_maximum_fusion.2
  453.0 3.1 collective-permute-done.19
  456.6 4.0 fusion
  461.5 3.4 collective-permute-start.16
  467.8 16.4 %collective-permute-done.20 = bf16[96,576]{0,1:T(8,128)(2,1)S(1)} collective-permute-done((bf16[96,576]{0,1:T(8,128)(2,1)S(1)}, bf16[96,576]{0,1:T(8,128)(2,1)S(1)}, u32[]{:S(2)}, u32[]{:S(2)}) %collective-permute-start.20) | collective-permute-done | bytes 110624 | tf_op jit(solution)/shard_map/ppermute | solution.py:824
  487.3 1.4 fusion.6
  488.7 1.9 pad_maximum_fusion.3
  (240 shorter events, 41.4 us)
Async XLA Ops:
  7.2 41.7 %copy-start = (s32[2,2048]{1,0:T(2,128)S(1)}, s32[2,2048]{1,0:T(2,128)}, u32[]{:S(2)}) copy-start(s32[2,2048]{1,0:T(2,128)} %param.19) | copy-start | bytes 49156
  7.2 23.2 %copy-start.12 = (bf16[768,96]{0,1:T(8,128)(2,1)S(1)}, bf16[768,96]{0,1:T(8,128)(2,1)}, u32[]{:S(2)}) copy-start(bf16[768,96]{0,1:T(8,128)(2,1)} %param.27) | copy-start | bytes 442372
  7.2 23.2 %copy-start.11 = (bf16[96,768]{1,0:T(8,128)(2,1)S(1)}, bf16[96,768]{1,0:T(8,128)(2,1)}, u32[]{:S(2)}) copy-start(bf16[96,768]{1,0:T(8,128)(2,1)} %param.26) | copy-start | bytes 442372
  7.2 224.4 %all-gather.3.cloned.1.call-start = ((), (), s32[]{:S(2)}) async-start(), calls=%async_computation.2 | async-start | bytes 11354112 | tf_op jit(solution)/shard_map/all_gather | solution.py:892
  8.9 6.3 %collective-permute-start.2 = (bf16[96,576]{1,0:T(8,128)(2,1)S(1)}, bf16[96,576]{1,0:T(8,128)(2,1)S(1)}, u32[]{:S(2)}, u32[]{:S(2)}) collective-permute-start(bf16[96,576]{1,0:T(8,128)(2,1)S(1)} %get-tuple-element.186), channel_id=1, source_target_pairs={{0,2},{2,0},{1,3},{3,1},{4,6},{6,4},{5,7},{7,5},{8,10},{10,8},{9,1... | collective-permute-start | bytes 331784 | tf_op jit(solution)/shard_map/ppermute | solution.py:824
  15.3 27.0 %copy-start.14 = (bf16[12,8]{0,1:T(8,128)(2,1)S(1)}, bf16[12,8]{0,1:T(8,128)(2,1)}, u32[]{:S(2)}) copy-start(bf16[12,8]{0,1:T(8,128)(2,1)} %param.28) | copy-start | bytes 580
  15.3 27.2 %copy-start.23 = (bf16[3,8]{1,0:T(4,128)(2,1)S(1)}, bf16[3,8]{1,0:T(4,128)(2,1)}, u32[]{:S(2)}) copy-start(bf16[3,8]{1,0:T(4,128)(2,1)} %param.24) | copy-start | bytes 148
  15.3 27.3 %copy-start.24 = (bf16[3,8]{1,0:T(4,128)(2,1)S(1)}, bf16[3,8]{1,0:T(4,128)(2,1)}, u32[]{:S(2)}) copy-start(bf16[3,8]{1,0:T(4,128)(2,1)} %param.25) | copy-start | bytes 148
  15.3 27.3 %copy-start.15 = (bf16[24]{0:T(256)(128)(2,1)S(1)}, bf16[24]{0:T(256)(128)(2,1)}, u32[]{:S(2)}) copy-start(bf16[24]{0:T(256)(128)(2,1)} %param.29) | copy-start | bytes 148
  15.3 27.3 %copy-start.16 = (bf16[24]{0:T(256)(128)(2,1)S(1)}, bf16[24]{0:T(256)(128)(2,1)}, u32[]{:S(2)}) copy-start(bf16[24]{0:T(256)(128)(2,1)} %param.30) | copy-start | bytes 148
  15.3 27.3 %copy-start.17 = (bf16[24]{0:T(256)(128)(2,1)S(1)}, bf16[24]{0:T(256)(128)(2,1)}, u32[]{:S(2)}) copy-start(bf16[24]{0:T(256)(128)(2,1)} %param.31) | copy-start | bytes 148
  15.3 27.3 %copy-start.18 = (bf16[24]{0:T(256)(128)(2,1)S(1)}, bf16[24]{0:T(256)(128)(2,1)}, u32[]{:S(2)}) copy-start(bf16[24]{0:T(256)(128)(2,1)} %param.32) | copy-start | bytes 148
  15.3 27.3 %copy-start.19 = (bf16[24]{0:T(256)(128)(2,1)S(1)}, bf16[24]{0:T(256)(128)(2,1)}, u32[]{:S(2)}) copy-start(bf16[24]{0:T(256)(128)(2,1)} %param.33) | copy-start | bytes 148
  15.4 27.3 %copy-start.20 = (bf16[24]{0:T(256)(128)(2,1)S(1)}, bf16[24]{0:T(256)(128)(2,1)}, u32[]{:S(2)}) copy-start(bf16[24]{0:T(256)(128)(2,1)} %param.34) | copy-start | bytes 148
  15.4 28.9 %copy-start.8 = (bf16[2,512,768]{2,1,0:T(8,128)(2,1)S(1)}, bf16[2,512,768]{2,1,0:T(8,128)(2,1)}, u32[]{:S(2)}) copy-start(bf16[2,512,768]{2,1,0:T(8,128)(2,1)} %param.18) | copy-start | bytes 4718596
  15.4 13.4 %collective-permute-start.3 = (bf16[2,96,576]{2,1,0:T(8,128)(2,1)S(1)}, bf16[2,96,576]{2,1,0:T(8,128)(2,1)S(1)}, u32[]{:S(2)}, u32[]{:S(2)}) collective-permute-start(bf16[2,96,576]{2,1,0:T(8,128)(2,1)S(1)} %pad_maximum_fusion.7), channel_id=1, source_target_pairs={{0,16},{4,20},{8,24},{12,28},{16,0},{20,4},{24,8},{28,12},{1,17},{... | collective-permute-start | bytes 663560 | tf_op jit(solution)/shard_map/ppermute | solution.py:830
  28.8 12.2 %collective-permute-start.4 = (bf16[4,96,576]{2,1,0:T(8,128)(2,1)S(1)}, bf16[4,96,576]{2,1,0:T(8,128)(2,1)S(1)}, u32[]{:S(2)}, u32[]{:S(2)}) collective-permute-start(bf16[4,96,576]{2,1,0:T(8,128)(2,1)S(1)} %pad_maximum_fusion.6), channel_id=1, source_target_pairs={{0,8},{4,12},{8,0},{12,4},{16,24},{20,28},{24,16},{28,20},{1,9},{5... | collective-permute-start | bytes 1327112 | tf_op jit(solution)/shard_map/ppermute | solution.py:830
  42.2 448.4 %reduce-scatter.2.cloned.1.call-start = ((), (), s32[]{:S(2)}) async-start(), calls=%async_computation.1 | async-start | bytes 11354112 | tf_op jit(solution)/shard_map/reduce_scatter | solution.py:925
  42.8 9.0 %collective-permute-start.6 = (bf16[1,384]{1,0:T(2,128)(2,1)S(1)}, bf16[1,384]{1,0:T(2,128)(2,1)S(1)}, u32[]{:S(2)}, u32[]{:S(2)}) collective-permute-start(bf16[1,384]{1,0:T(2,128)(2,1)S(1)} %reshape.288), channel_id=1, source_target_pairs={{0,4},{4,0},{8,12},{12,8},{16,20},{20,16},{24,28},{28,24},{1,5},{5... | collective-permute-start | bytes 2312 | tf_op jit(solution)/shard_map/ppermute | solution.py:830
  44.4 56.5 %collective-permute-start = (bf16[512,768]{1,0:T(8,128)(2,1)S(1)}, bf16[512,768]{1,0:T(8,128)(2,1)}, u32[]{:S(2)}, u32[]{:S(2)}) collective-permute-start(bf16[512,768]{1,0:T(8,128)(2,1)S(1)} %dynamic-slice_bitcast_fusion.1), channel_id=1, source_target_pairs={{0,2},{2,0},{1,3},{3,1},{4,6},{6,4},{5,7},{7,5},{8,10},{10,8},{9,1... | collective-permute-start | bytes 2359304 | tf_op jit(solution)/shard_map/ppermute | solution.py:824
  48.3 179.5 %collective-permute-start.11 = (bf16[512,768]{1,0:T(8,128)(2,1)}, bf16[512,768]{1,0:T(8,128)(2,1)}, u32[]{:S(2)}, u32[]{:S(2)}) collective-permute-start(bf16[512,768]{1,0:T(8,128)(2,1)} %fusion.13), channel_id=1, source_target_pairs={{0,2},{2,0},{1,3},{3,1},{4,6},{6,4},{5,7},{7,5},{8,10},{10,8},{9,1... | collective-permute-start | bytes 2359304 | tf_op jit(solution)/shard_map/ppermute | solution.py:824
  51.8 38.3 %collective-permute-start.7 = (bf16[2,1,384]{2,0,1:T(2,128)(2,1)S(1)}, bf16[2,1,384]{2,0,1:T(2,128)(2,1)S(1)}, u32[]{:S(2)}, u32[]{:S(2)}) collective-permute-start(bf16[2,1,384]{2,0,1:T(2,128)(2,1)S(1)} %pad_maximum_fusion.13), channel_id=1, source_target_pairs={{0,2},{2,0},{1,3},{3,1},{4,6},{6,4},{5,7},{7,5},{8,10},{10,8},{9,1... | collective-permute-start | bytes 4616 | tf_op jit(solution)/shard_map/ppermute | solution.py:824
  90.1 6.9 %collective-permute-start.8 = (bf16[2,2,1,384]{3,1,0,2:T(2,128)(2,1)S(1)}, bf16[2,2,1,384]{3,1,0,2:T(2,128)(2,1)S(1)}, u32[]{:S(2)}, u32[]{:S(2)}) collective-permute-start(bf16[2,2,1,384]{3,1,0,2:T(2,128)(2,1)S(1)} %fusion.36), channel_id=1, source_target_pairs={{0,16},{4,20},{8,24},{12,28},{16,0},{20,4},{24,8},{28,12},{1,17},{... | collective-permute-start | bytes 9224 | tf_op jit(solution)/shard_map/ppermute | solution.py:830
  97.0 3.9 collective-permute-start.9
  102.3 48.6 %copy-start.2 = (bf16[2,512,768]{2,1,0:T(8,128)(2,1)}, bf16[2,512,768]{2,1,0:T(8,128)(2,1)S(1)}, u32[]{:S(2)}) copy-start(bf16[2,512,768]{2,1,0:T(8,128)(2,1)S(1)} %pad_maximum_fusion.4) | copy-start | bytes 4718596
  102.3 48.6 %collective-permute-start.1 = (bf16[2,512,768]{2,1,0:T(8,128)(2,1)S(1)}, bf16[2,512,768]{2,1,0:T(8,128)(2,1)}, u32[]{:S(2)}, u32[]{:S(2)}) collective-permute-start(bf16[2,512,768]{2,1,0:T(8,128)(2,1)S(1)} %pad_maximum_fusion.4), channel_id=1, source_target_pairs={{0,1},{1,0},{2,3},{3,2},{4,5},{5,4},{6,7},{7,6},{8,9},{9,8},{10,11... | collective-permute-start | bytes 4718600 | tf_op jit(solution)/shard_map/ppermute | solution.py:827
  102.5 6.1 %collective-permute-start.12 = (bf16[8,2,1,384]{3,1,0,2:T(2,128)(2,1)S(1)}, bf16[8,2,1,384]{3,1,0,2:T(2,128)(2,1)}, u32[]{:S(2)}, u32[]{:S(2)}) collective-permute-start(bf16[8,2,1,384]{3,1,0,2:T(2,128)(2,1)S(1)} %bitcast.253), channel_id=1, source_target_pairs={{0,1},{1,0},{2,3},{3,2},{4,5},{5,4},{6,7},{7,6},{8,9},{9,8},{10,11... | collective-permute-start | bytes 36872 | tf_op jit(solution)/shard_map/ppermute | solution.py:827
  107.3 41.4 %collective-permute-start.5 = (bf16[8,96,576]{2,1,0:T(8,128)(2,1)}, bf16[8,96,576]{2,1,0:T(8,128)(2,1)}, u32[]{:S(2)}, u32[]{:S(2)}) collective-permute-start(bf16[8,96,576]{2,1,0:T(8,128)(2,1)} %pad_maximum_fusion.5), channel_id=1, source_target_pairs={{0,4},{4,0},{8,12},{12,8},{16,20},{20,16},{24,28},{28,24},{1,5},{5... | collective-permute-start | bytes 2654216 | tf_op jit(solution)/shard_map/ppermute | solution.py:830
  225.4 6.2 %collective-permute-start.10 = (bf16[2,512,384]{2,1,0:T(8,128)(2,1)}, bf16[2,512,384]{2,1,0:T(8,128)(2,1)S(1)}, u32[]{:S(2)}, u32[]{:S(2)}) collective-permute-start(bf16[2,512,384]{2,1,0:T(8,128)(2,1)} %get-tuple-element.50.sent_ref), channel_id=1, source_target_pairs={{0,1},{1,0},{2,3},{3,2},{4,5},{5,4},{6,7},{7,6},{8,9},{9,8},{10,11... | collective-permute-start | bytes 2359304 | tf_op jit(solution)/shard_map/ppermute | solution.py:827
  309.2 3.4 collective-permute-start.14
  312.4 107.4 %collective-permute-start.13 = (bf16[512,768]{1,0:T(8,128)(2,1)}, bf16[512,768]{1,0:T(8,128)(2,1)}, u32[]{:S(2)}, u32[]{:S(2)}) collective-permute-start(bf16[512,768]{1,0:T(8,128)(2,1)} %get-tuple-element.53), channel_id=1, source_target_pairs={{0,2},{2,0},{1,3},{3,1},{4,6},{6,4},{5,7},{7,5},{8,10},{10,8},{9,1... | collective-permute-start | bytes 2359304 | tf_op jit(solution)/shard_map/ppermute | solution.py:824
  378.3 11.3 %slice-start = ((s8[4718592]{0:T(1024)(128)(4,1)}), s8[4194304]{0:T(1024)(128)(4,1)S(1)}, s32[]{:S(2)}) async-start(s8[4718592]{0:T(1024)(128)(4,1)} %bitcast.216), calls=%async_computation.3 | async-start | bytes 8388608
  378.3 11.3 %slice-start.1 = ((s8[4718592]{0:T(1024)(128)(4,1)}), s8[524288]{0:T(1024)(128)(4,1)S(1)}, s32[]{:S(2)}) async-start(s8[4718592]{0:T(1024)(128)(4,1)} %bitcast.216), calls=%async_computation.4 | async-start | bytes 1048576
  378.3 11.3 %copy-start.25 = (bf16[768,1152]{1,0:T(8,128)(2,1)S(1)}, bf16[768,1152]{1,0:T(8,128)(2,1)}, u32[]{:S(2)}) copy-start(bf16[768,1152]{1,0:T(8,128)(2,1)} %get-tuple-element.68) | copy-start | bytes 5308420
  378.3 17.5 %collective-permute-start.21 = (f32[8,2,384]{2,0,1:T(8,128)S(1)}, f32[8,2,384]{2,0,1:T(8,128)S(1)}, u32[]{:S(2)}, u32[]{:S(2)}) collective-permute-start(f32[8,2,384]{2,0,1:T(8,128)S(1)} %fusion.19), channel_id=1, source_target_pairs={{0,1},{1,0},{2,3},{3,2},{4,5},{5,4},{6,7},{7,6},{8,9},{9,8},{10,11... | collective-permute-start | bytes 73736 | tf_op jit(solution)/shard_map/ppermute | solution.py:827
  387.5 30.6 %collective-permute-start.17 = (bf16[4,96,1152]{2,1,0:T(8,128)(2,1)}, bf16[4,96,1152]{2,1,0:T(8,128)(2,1)}, u32[]{:S(2)}, u32[]{:S(2)}) collective-permute-start(bf16[4,96,1152]{2,1,0:T(8,128)(2,1)} %dynamic-slice_bitcast_fusion), channel_id=1, source_target_pairs={{0,4},{4,0},{8,12},{12,8},{16,20},{20,16},{24,28},{28,24},{1,5},{5... | collective-permute-start | bytes 2654216 | tf_op jit(solution)/shard_map/ppermute | solution.py:830
  395.8 22.3 %copy-start.7 = (bf16[768,1152]{1,0:T(8,128)(2,1)S(1)}, bf16[768,1152]{1,0:T(8,128)(2,1)}, u32[]{:S(2)}) copy-start(bf16[768,1152]{1,0:T(8,128)(2,1)} %copy-done.6) | copy-start | bytes 5308420
  395.9 4.4 collective-permute-start.22
  399.9 20.0 %copy-start.9 = (f32[512,768]{1,0:T(8,128)S(1)}, f32[512,768]{1,0:T(8,128)}, u32[]{:S(2)}) copy-start(f32[512,768]{1,0:T(8,128)} %get-tuple-element.52) | copy-start | bytes 4718596
  399.9 56.7 %collective-permute-start.15 = (bf16[2,512,768]{2,1,0:T(8,128)(2,1)S(1)}, bf16[2,512,768]{2,1,0:T(8,128)(2,1)}, u32[]{:S(2)}, u32[]{:S(2)}) collective-permute-start(bf16[2,512,768]{2,1,0:T(8,128)(2,1)S(1)} %fusion.8), channel_id=1, source_target_pairs={{0,1},{1,0},{2,3},{3,2},{4,5},{5,4},{6,7},{7,6},{8,9},{9,8},{10,11... | collective-permute-start | bytes 4718600 | tf_op jit(solution)/shard_map/ppermute | solution.py:827
  400.3 21.0 %collective-permute-start.23 = (f32[2,2,384]{2,0,1:T(2,128)S(1)}, f32[2,2,384]{2,0,1:T(2,128)S(1)}, u32[]{:S(2)}, u32[]{:S(2)}) collective-permute-start(f32[2,2,384]{2,0,1:T(2,128)S(1)} %fusion.24), channel_id=1, source_target_pairs={{0,16},{4,20},{8,24},{12,28},{16,0},{20,4},{24,8},{28,12},{1,17},{... | collective-permute-start | bytes 18440 | tf_op jit(solution)/shard_map/ppermute | solution.py:830
  419.6 23.1 %collective-permute-start.18 = (bf16[2,96,1152]{2,1,0:T(8,128)(2,1)S(1)}, bf16[2,96,1152]{2,1,0:T(8,128)(2,1)S(1)}, u32[]{:S(2)}, u32[]{:S(2)}) collective-permute-start(bf16[2,96,1152]{2,1,0:T(8,128)(2,1)S(1)} %dynamic-slice_bitcast_fusion.2), channel_id=1, source_target_pairs={{0,8},{4,12},{8,0},{12,4},{16,24},{20,28},{24,16},{28,20},{1,9},{5... | collective-permute-start | bytes 1327112 | tf_op jit(solution)/shard_map/ppermute | solution.py:830
  421.3 21.6 %collective-permute-start.24 = (f32[2,384]{1,0:T(2,128)S(1)}, f32[2,384]{1,0:T(2,128)S(1)}, u32[]{:S(2)}, u32[]{:S(2)}) collective-permute-start(f32[2,384]{1,0:T(2,128)S(1)} %bitcast.256), channel_id=1, source_target_pairs={{0,4},{4,0},{8,12},{12,8},{16,20},{20,16},{24,28},{28,24},{1,5},{5... | collective-permute-start | bytes 9224 | tf_op jit(solution)/shard_map/ppermute | solution.py:830
  442.8 13.3 %collective-permute-start.19 = (bf16[1,96,1152]{2,1,0:T(8,128)(2,1)S(1)}, bf16[1,96,1152]{2,1,0:T(8,128)(2,1)S(1)}, u32[]{:S(2)}, u32[]{:S(2)}) collective-permute-start(bf16[1,96,1152]{2,1,0:T(8,128)(2,1)S(1)} %constant_dynamic-slice_fusion.6), channel_id=1, source_target_pairs={{0,16},{4,20},{8,24},{12,28},{16,0},{20,4},{24,8},{28,12},{1,17},{... | collective-permute-start | bytes 663560 | tf_op jit(solution)/shard_map/ppermute | solution.py:830
  442.9 10.1 %collective-permute-start.25 = (f32[384]{0:T(512)S(1)}, f32[384]{0:T(512)S(1)}, u32[]{:S(2)}, u32[]{:S(2)}) collective-permute-start(f32[384]{0:T(512)S(1)} %get-tuple-element.183), channel_id=1, source_target_pairs={{0,2},{2,0},{1,3},{3,1},{4,6},{6,4},{5,7},{7,5},{8,10},{10,8},{9,1... | collective-permute-start | bytes 4616 | tf_op jit(solution)/shard_map/ppermute | solution.py:824
  456.6 8.3 %copy-start.10 = (bf16[2,96,3,192]{1,3,2,0:T(8,128)(2,1)}, bf16[2,96,3,192]{1,3,2,0:T(8,128)(2,1)S(1)}, u32[]{:S(2)}) copy-start(bf16[2,96,3,192]{1,3,2,0:T(8,128)(2,1)S(1)} %copy.248) | copy-start | bytes 663556
  461.5 25.8 %collective-permute-start.16 = (bf16[512,768]{1,0:T(8,128)(2,1)}, bf16[512,768]{1,0:T(8,128)(2,1)}, u32[]{:S(2)}, u32[]{:S(2)}) collective-permute-start(bf16[512,768]{1,0:T(8,128)(2,1)} %fusion.14), channel_id=1, source_target_pairs={{0,2},{2,0},{1,3},{3,1},{4,6},{6,4},{5,7},{7,5},{8,10},{10,8},{9,1... | collective-permute-start | bytes 2359304 | tf_op jit(solution)/shard_map/ppermute | solution.py:824
  464.9 19.2 %collective-permute-start.20 = (bf16[96,576]{0,1:T(8,128)(2,1)S(1)}, bf16[96,576]{0,1:T(8,128)(2,1)S(1)}, u32[]{:S(2)}, u32[]{:S(2)}) collective-permute-start(bf16[96,576]{0,1:T(8,128)(2,1)S(1)} %dynamic-slice_bitcast_fusion.3), channel_id=1, source_target_pairs={{0,2},{2,0},{1,3},{3,1},{4,6},{6,4},{5,7},{7,5},{8,10},{10,8},{9,1... | collective-permute-start | bytes 331784 | tf_op jit(solution)/shard_map/ppermute | solution.py:824
  (8 other events, 17.8 us)
Sparse Core Ops, SparseCore 0:
  42.3 116.3 all-gather.2
  308.2 163.7 reduce-scatter.1
